TPU v7x, 768 devices: a whole 4x8x12 slice. The times are simulated.
768 devices in a mesh: shot: 128 (over x, y, z_hi, core), slab: 6 (over z_lo).
Axes of the slice: x: 4, y: 8, z: 12 (z_hi: 2, z_lo: 6; z = z_hi * 6 + z_lo), core: 2. Of those that a mesh axis runs over, the one named last changes fastest.
Arguments:
- velocity: float32 [128, 32, 96, 128], P('shot', None, 'slab'), may hold values from 0.15 to 0.45
- fwd_field: float32 [128, 64, 96, 256], P('shot', None, 'slab'), may hold values from -4 to 4
- adj_field: float32 [128, 64, 96, 256], P('shot', None, 'slab'), may hold values from -4 to 4
- aperture_anchor: int32 [128, 2], P('shot'), may hold values from 0 to 30, as said below
- source_cell: int32 [128, 16], P('shot'), may hold values from 0 to 1572863
- wavelet: float32 [128, 2, 16], P('shot'), may hold values from -6 to 6
- shot_count: int32 [128], P('shot'), may hold values from 1 to 16
- receiver_cell: int32 [128, 1024], P('shot'), may hold values from 0 to 1572863
- residual: float32 [128, 2, 1024], P('shot'), may hold values from -6 to 6
Outputs:
- gradient: float32 [128, 32, 96, 128], P('shot', None, 'slab')
Inputs may be any that keep to these rules, and one draw needn't show every extreme that they name: `aperture_anchor`: entry g, 0 is g // 4 or one less and entry g, 1 is g % 4 or one less, each clipped so that the 2 x 2 tiles of the aperture lie in the model.
All inputs are finite; a program needn't handle non-finite values.
Results may differ from a plain program's by a relative error of at most 0.0003.
Values sent between devices are 32-bit elements; how exact they have to be, the bound alone decides.
No kernel may reach another device: no remote copies, remote signals or barrier semaphores. Data moves between devices by JAX's collectives and lax.ppermute only.
A program may use at most 64 MiB of HBM per device.

v0:
```python
import functools

import jax
import jax.numpy as jnp
import numpy as np
from jax import lax
from jax.experimental import pallas as pl
from jax.experimental.pallas import tpu as pltpu
from jax.sharding import PartitionSpec as P


TILES_Y = 4
CENTRE = -205.0 / 72.0
STENCIL = (1.6, -0.2, 8.0 / 315.0, -1.0 / 560.0)

BX = 8
Z = 16
Y = 256
Y_BITS = 8
AX = 64
ROWS = BX * Z
BLOCKS = AX // BX
FLAT = AX * Z
F32 = jnp.float32
BF16 = jnp.bfloat16
VMEM = pl.BlockSpec(memory_space=pltpu.VMEM)
SMEM = pl.BlockSpec(memory_space=pltpu.SMEM)


def weight(distance):
    distance = np.abs(distance)
    table = np.array((0.0,) + STENCIL + (0.0,))
    return table[np.minimum(distance, 5)]


def parts_of(matrix):
    high = matrix.astype(np.float32).astype(jnp.bfloat16)
    low = (matrix - high.astype(np.float64)).astype(np.float32).astype(jnp.bfloat16)
    return high, low


def along_xz():
    out_x, out_z = np.divmod(np.arange(ROWS), Z)
    in_x, in_z = np.divmod(np.arange(2 * ROWS), Z)
    kinds = []
    for lead in (0, 4, 8):
        dx = out_x[:, None] - (in_x[None, :] - lead)
        dz = out_z[:, None] - in_z[None, :]
        both = np.where(dz == 0, weight(dx), 0.0) + np.where(dx == 0, weight(dz), 0.0)
        kinds.append(both + np.where((dx == 0) & (dz == 0), 3.0 * CENTRE, 0.0))
    return np.stack(kinds)


def along_y():
    at = np.arange(Y)
    return weight(at[:, None] - at[None, :])


def along_halo():
    out_x, out_z = np.divmod(np.arange(ROWS), Z)
    in_x, in_s = np.divmod(np.arange(BX * 8), 8)
    fields = []
    for field in (0, 1):
        sides = []
        for side in (0, 1):
            layer = in_s - 4 * field
            depth = layer - 4 if side == 0 else Z + layer
            mine = (layer >= 0) & (layer < 4)
            dz = out_z[:, None] - depth[None, :]
            same = (out_x[:, None] == in_x[None, :]) & mine[None, :]
            sides.append(np.where(same, weight(dz), 0.0))
        fields.append(np.concatenate(sides, 1))
    return np.concatenate(fields, 0)


def dot(a, b):
    return jnp.dot(a, b, preferred_element_type=F32)


def split(value):
    high = value.astype(BF16)
    return high, (value - high.astype(F32)).astype(BF16)


def cost(flops, nbytes):
    return pl.CostEstimate(flops=flops, transcendentals=0, bytes_accessed=nbytes)


def rims(fwd, adj):
    front = lax.broadcasted_iota(jnp.int32, (BX, 8, Y), 1) < 4
    top = jnp.where(front, pltpu.roll(fwd[:, 8:, :], 4, 1), adj[:, 8:, :])
    bottom = jnp.where(front, fwd[:, :8, :], pltpu.roll(adj[:, :8, :], 4, 1))
    return top, bottom


def pack_kernel(anchor, vel, fwd, adj, up, down, tagged, flags):
    device = lax.axis_index("shot")
    home_row = device // TILES_Y
    home_col = device - home_row * TILES_Y
    part_row = home_row - anchor[0, 0]
    part_col = home_col - anchor[0, 1]
    side_row = 1 - 2 * part_row
    side_col = 1 - 2 * part_col
    toward_e = 1 - 2 * (home_row & 1)
    toward_a = 1 - 2 * (home_col & 1)
    flags[0] = part_row
    flags[1] = part_col
    flags[2] = jnp.where(side_row == toward_e, 1, 0)
    flags[3] = jnp.where(side_col == toward_a, 1, 0)
    flags[4] = toward_e
    flags[5] = toward_a
    rows = vel.shape[0]
    tagged[rows] = jnp.full(tagged.shape[1:], side_row.astype(F32))
    tagged[rows + 1] = jnp.full(tagged.shape[1:], side_col.astype(F32))

    def step(b, _):
        at = pl.ds(b * BX, BX)
        up[at], down[at] = rims(fwd[at], adj[at])
        return 0

    lax.fori_loop(0, BLOCKS, step, 0)

    def copy(i, _):
        at = pl.ds(i * 8, 8)
        tagged[at] = vel[at]
        return 0

    lax.fori_loop(0, rows // 8, copy, 0)


def inner_laplace(b, high, low, s_high, s_low, y_high, y_low):
    kind = jnp.where(b == 0, 0, jnp.where(b == BLOCKS - 1, 2, 1))
    first = jnp.clip(b * BX - 4, 0, AX - 2 * BX) * Z
    window = pl.ds(pl.multiple_of(first, 64), 2 * ROWS)
    own = pl.ds(pl.multiple_of(b * ROWS, ROWS), ROWS)
    wide = high[window]
    near = high[own]
    result = dot(s_high[kind], wide) + dot(near, y_high[...])
    result = result + dot(s_high[kind], low[window]) + dot(low[own], y_high[...])
    return result + dot(s_low[kind], wide) + dot(near, y_low[...])


def split_all(field, high, low):
    def step(b, _):
        at = pl.ds(pl.multiple_of(b * ROWS, ROWS), ROWS)
        high[at], low[at] = split(field[at])
        return 0

    lax.fori_loop(0, BLOCKS, step, 0)


def table_of(cells, amounts, first_layer, total_depth, table):
    count = cells.shape[1]
    column = cells >> Y_BITS
    cell_x = ((column.astype(F32) + 0.5) * (1.0 / total_depth)).astype(jnp.int32)
    cell_z = column - cell_x * total_depth - first_layer
    inside = (cell_z >= 0) & (cell_z < Z)
    table[...] = jnp.full(table.shape, -1.0, F32)
    table[0:1, 0:count] = jnp.where(inside, cell_x * Z + cell_z, -1).astype(F32)
    table[1:2, 0:count] = (cells & (Y - 1)).astype(F32)
    table[2:3, 0:count] = amounts[0]
    table[3:4, 0:count] = amounts[1]


def columns_of(points, columns):
    def step(i, _):
        at = pl.ds(pl.multiple_of(i * 128, 128), 128)
        part = points[:, at].T
        here = lax.broadcasted_iota(jnp.int32, (128, Y), 1) == part[:, 1:2].astype(jnp.int32)
        for n in range(2):
            high, low = split(part[:, 2 + n : 3 + n])
            columns[at, pl.ds(2 * n * Y, Y)] = jnp.where(here, high.astype(F32), 0.0).astype(BF16)
            columns[at, pl.ds((2 * n + 1) * Y, Y)] = jnp.where(here, low.astype(F32), 0.0).astype(BF16)
        return 0

    lax.fori_loop(0, points.shape[1] // 128, step, 0)


def injected(b, points, columns):
    rows = lax.broadcasted_iota(jnp.int32, (ROWS, points.shape[1]), 0) + b * ROWS
    hot = jnp.where(rows == points[0:1, :].astype(jnp.int32), 1.0, 0.0).astype(BF16)
    first = dot(hot, columns[:, : 2 * Y])
    second = dot(hot, columns[:, 2 * Y :])
    return first[:, :Y] + first[:, Y:], second[:, :Y] + second[:, Y:]


def inject_kernel(total_depth, shot_count, source_cell, wavelet, receiver_cell, residual, fwd_in1, fwd_in2, adj_in1, adj_in2,
                  shots, receivers, shot_columns, receiver_columns):
    first_layer = lax.axis_index("slab") * Z
    active = lax.broadcasted_iota(jnp.int32, source_cell.shape, 1) < shot_count[0]
    waves = [jnp.where(active, wavelet[n : n + 1, :], 0.0) for n in range(2)]
    table_of(source_cell[...], waves, first_layer, total_depth, shots)
    table_of(receiver_cell[...], [residual[1:2, :], residual[0:1, :]], first_layer, total_depth, receivers)
    columns_of(shots, shot_columns)
    columns_of(receivers, receiver_columns)

    def step(b, _):
        at = pl.ds(pl.multiple_of(b * ROWS, ROWS), ROWS)
        fwd_in1[at], fwd_in2[at] = injected(b, shots, shot_columns)
        adj_in1[at], adj_in2[at] = injected(b, receivers, receiver_columns)
        return 0

    lax.fori_loop(0, BLOCKS, step, 0)


def laplace_kernel(fwd, adj, s_high, s_low, y_high, y_low, lap_fwd, lap_adj, fh, fl, ah, al):
    split_all(fwd, fh, fl)
    split_all(adj, ah, al)

    def step(b, _):
        at = pl.ds(pl.multiple_of(b * ROWS, ROWS), ROWS)
        lap_fwd[at] = inner_laplace(b, fh, fl, s_high, s_low, y_high, y_low)
        lap_adj[at] = inner_laplace(b, ah, al, s_high, s_low, y_high, y_low)
        return 0

    lax.fori_loop(0, BLOCKS, step, 0)


def halo_part(b, below, above, h_high, h_low):
    at = pl.ds(pl.multiple_of(b * (ROWS // 2), ROWS // 2), ROWS // 2)
    high, low = split(jnp.concatenate([below[at], above[at]], 0))
    both = dot(h_high[...], high) + dot(h_high[...], low) + dot(h_low[...], high)
    return both[:ROWS], both[ROWS:]


def advance_kernel(flags, own, col_a, col_b, row_e, row_o, diag_e, diag_o, lap_fwd, lap_adj, fwd, adj, fwd_in, adj_in,
                   below, above, h_high, h_low, speed2, mid_fwd, mid_adj, up, down):
    half = own.shape[0]
    wide = own.shape[2]
    with_e = flags[2] == 1
    with_a = flags[3] == 1
    row_at = flags[0] * half
    row_to = (1 - flags[0]) * half
    col_at = pl.ds(pl.multiple_of(flags[1] * wide, wide), wide)
    col_to = pl.ds(pl.multiple_of((1 - flags[1]) * wide, wide), wide)

    def assemble(i, _):
        at = pl.ds(i * 8, 8)
        near = pl.ds(row_at + i * 8, 8)
        far = pl.ds(row_to + i * 8, 8)
        speed = own[at]
        speed2[near, :, col_at] = speed * speed
        speed = jnp.where(with_a, col_a[at], col_b[at])
        speed2[near, :, col_to] = speed * speed
        speed = jnp.where(with_e, row_e[at], row_o[at])
        speed2[far, :, col_at] = speed * speed
        speed = jnp.where(with_e, diag_e[at], diag_o[at])
        speed2[far, :, col_to] = speed * speed
        return 0

    lax.fori_loop(0, half // 8, assemble, 0)

    def step(b, _):
        at = pl.ds(pl.multiple_of(b * ROWS, ROWS), ROWS)
        blk = pl.ds(b * BX, BX)
        halo_fwd, halo_adj = halo_part(b, below, above, h_high, h_low)
        c = speed2[blk].reshape(ROWS, Y)
        new_fwd = fwd[at] + (c * (lap_fwd[at] + halo_fwd) + fwd_in[at])
        new_adj = adj[at] + (c * (lap_adj[at] + halo_adj) + adj_in[at])
        mid_fwd[at] = new_fwd
        mid_adj[at] = new_adj
        up[blk], down[blk] = rims(new_fwd.reshape(BX, Z, Y), new_adj.reshape(BX, Z, Y))
        return 0

    lax.fori_loop(0, BLOCKS, step, 0)


def image_kernel(flags, speed2, lap_fwd, lap_adj, fwd, adj, mid_fwd, mid_adj, fwd_in, adj_in, below, above, h_high, h_low,
                 own, col, row, diag, image):
    def step(b, _):
        at = pl.ds(pl.multiple_of(b * ROWS, ROWS), ROWS)
        halo_fwd, halo_adj = halo_part(b, below, above, h_high, h_low)
        c = speed2[at]
        second_fwd = c * (lap_fwd[at] + halo_fwd) + fwd_in[at]
        second_adj = c * (lap_adj[at] + halo_adj) + adj_in[at]
        later = mid_adj[at]
        earlier = 2.0 * later - adj[at] + second_adj
        imaged = earlier * (mid_fwd[at] - fwd[at]) + later * second_fwd
        image[pl.ds(b * BX, BX)] = imaged.reshape(BX, Z, Y)
        return 0

    lax.fori_loop(0, BLOCKS, step, 0)
    half = own.shape[0]
    wide = own.shape[2]
    row_at = flags[0] * half
    row_to = (1 - flags[0]) * half
    col_at = pl.ds(pl.multiple_of(flags[1] * wide, wide), wide)
    col_to = pl.ds(pl.multiple_of((1 - flags[1]) * wide, wide), wide)

    def hand_out(i, _):
        at = pl.ds(i * 8, 8)
        near = pl.ds(row_at + i * 8, 8)
        far = pl.ds(row_to + i * 8, 8)
        own[at] = image[near, :, col_at]
        col[at] = image[near, :, col_to]
        row[at] = image[far, :, col_at]
        diag[at] = image[far, :, col_to]
        return 0

    lax.fori_loop(0, half // 8, hand_out, 0)


def swaps(count):
    rows = count // TILES_Y
    a = [(s, s ^ 1) for s in range(count)]
    b = [(s, s + 1) if s % TILES_Y == 1 else (s, s - 1) for s in range(count) if s % TILES_Y in (1, 2)]
    e = [(s, s + TILES_Y if (s // TILES_Y) % 2 == 0 else s - TILES_Y) for s in range(count)]
    o = []
    for s in range(count):
        other = s // TILES_Y + (1 if (s // TILES_Y) % 2 else -1)
        if 0 <= other < rows:
            o.append((s, other * TILES_Y + s % TILES_Y))
    return a, b, e, o


def select_kernel(flags, col_a, col_b, row_e, row_o, diag_e, diag_o, tag_e, tag_o):
    half = col_a.shape[0]
    toward_a = flags[5].astype(F32)
    tag_e[...] = row_e[half:]
    tag_o[...] = row_o[half:]
    e_wants_a = row_e[half + 1] == toward_a
    o_wants_a = row_o[half + 1] == toward_a

    def step(i, _):
        at = pl.ds(i * 8, 8)
        a = col_a[at]
        b = col_b[at]
        diag_e[at] = jnp.where(e_wants_a[None], a, b)
        diag_o[at] = jnp.where(o_wants_a[None], a, b)
        return 0

    lax.fori_loop(0, half // 8, step, 0)


def bucket_kernel(flags, col, back_e, back_o, tag_e, tag_o, sum_a, sum_b):
    toward_e = flags[4].astype(F32)
    toward_a = flags[5].astype(F32)
    with_a = flags[3] == 1
    from_e = tag_e[0] == -toward_e
    from_o = tag_o[0] == toward_e
    e_a = from_e & (tag_e[1] == toward_a)
    e_b = from_e & (tag_e[1] == -toward_a)
    o_a = from_o & (tag_o[1] == toward_a)
    o_b = from_o & (tag_o[1] == -toward_a)

    def step(i, _):
        at = pl.ds(i * 8, 8)
        c = col[at]
        e = back_e[at]
        o = back_o[at]
        sum_a[at] = jnp.where(with_a, c, 0.0) + jnp.where(e_a[None], e, 0.0) + jnp.where(o_a[None], o, 0.0)
        sum_b[at] = jnp.where(with_a, 0.0, c) + jnp.where(e_b[None], e, 0.0) + jnp.where(o_b[None], o, 0.0)
        return 0

    lax.fori_loop(0, col.shape[0] // 8, step, 0)


def final_kernel(flags, tile, own, same_e, same_o, tag_e, tag_o, sum_a, sum_b, out):
    toward_e = flags[4].astype(F32)
    from_e = tag_e[0] == -toward_e
    from_o = tag_o[0] == toward_e

    def step(i, _):
        at = pl.ds(i * 8, 8)
        total = own[at] + jnp.where(from_e[None], same_e[at], 0.0) + jnp.where(from_o[None], same_o[at], 0.0)
        out[at] = 2.0 * tile[at] * (total + sum_a[at] + sum_b[at])
        return 0

    lax.fori_loop(0, tile.shape[0] // 8, step, 0)


def steps(velocity, fwd_field, adj_field, aperture_anchor, source_cell, wavelet, shot_count, receiver_cell, residual):
    tile = velocity[0]
    half, depth, wide = tile.shape
    slabs = lax.axis_size("slab")
    pair_a, pair_b, pair_e, pair_o = swaps(lax.axis_size("shot"))
    to_up = [(i, i + 1) for i in range(slabs - 1)]
    to_down = [(i + 1, i) for i in range(slabs - 1)]

    def shape(*dims, dtype=F32):
        return jax.ShapeDtypeStruct(dims, dtype)

    def send(pairs, value, axis="shot"):
        return lax.ppermute(value, axis, pairs)

    def kernel(function, ins, outs, args, flops, mib=8, scratch=()):
        places = [SMEM if i == "s" else VMEM for i in ins]
        sent = tuple(SMEM if o.dtype == jnp.int32 else VMEM for o in outs)
        nbytes = sum(int(np.prod(a.shape)) * 4 for a in tuple(args) + tuple(outs))
        return pl.pallas_call(
            function,
            out_shape=tuple(outs),
            in_specs=places,
            out_specs=sent,
            scratch_shapes=list(scratch),
            compiler_params=pltpu.CompilerParams(vmem_limit_bytes=mib * 1024 * 1024),
            cost_estimate=cost(flops, nbytes),
        )(*args)

    piece = shape(half, depth, wide)
    rim_shape = shape(AX, 8, Y)
    flat = shape(FLAT, Y)
    halves = [pltpu.VMEM((FLAT, Y), BF16)] * 4
    s_high, s_low = parts_of(along_xz())
    y_high, y_low = parts_of(along_y())
    h_high, h_low = parts_of(along_halo())
    inner = tuple(jnp.asarray(m) for m in (s_high, s_low, y_high, y_low))
    rim = tuple(jnp.asarray(m) for m in (h_high, h_low))

    col_b = send(pair_b, tile)
    col_a = send(pair_a, tile)
    fwd = fwd_field[0]
    adj = adj_field[0]
    flat_fwd = fwd.reshape(FLAT, Y)
    flat_adj = adj.reshape(FLAT, Y)
    up, down, tagged, flags = kernel(
        pack_kernel, "svvv", (rim_shape, rim_shape, shape(half + 2, depth, wide), shape(8, dtype=jnp.int32)),
        (aperture_anchor, tile, fwd, adj), 1 << 20)
    row_e = send(pair_e, tagged)
    row_o = send(pair_o, tagged)
    below = send(to_up, up, "slab")
    above = send(to_down, down, "slab")
    recv = receiver_cell.shape[1]
    fwd_in1, fwd_in2, adj_in1, adj_in2 = kernel(
        functools.partial(inject_kernel, depth * slabs), "svvvv", (flat,) * 4,
        (shot_count, source_cell, wavelet[0], receiver_cell, residual[0]), 3 << 30, 12,
        [pltpu.VMEM((8, 128), F32), pltpu.VMEM((8, recv), F32), pltpu.VMEM((128, 4 * Y), BF16), pltpu.VMEM((recv, 4 * Y), BF16)])
    diag_e, diag_o, tag_e, tag_o = kernel(
        select_kernel, "svvvv", (piece, piece, shape(2, depth, wide), shape(2, depth, wide)),
        (flags, col_a, col_b, row_e, row_o), 1 << 20)
    diag_e = send(pair_e, diag_e)
    diag_o = send(pair_o, diag_o)
    lap_fwd, lap_adj = kernel(
        laplace_kernel, "vvvvvv", (flat,) * 2, (flat_fwd, flat_adj) + inner, 2 << 30, 8, halves)
    speed2, mid_fwd, mid_adj, up, down = kernel(
        advance_kernel, "s" + "v" * 17, (shape(AX, depth, Y), flat, flat, rim_shape, rim_shape),
        (flags, tile, col_a, col_b, row_e, row_o, diag_e, diag_o, lap_fwd, lap_adj, flat_fwd, flat_adj, fwd_in1, adj_in1,
         below.reshape(AX * 8, Y), above.reshape(AX * 8, Y)) + rim, 1 << 30)
    below = send(to_up, up, "slab")
    above = send(to_down, down, "slab")
    lap_fwd, lap_adj = kernel(laplace_kernel, "vvvvvv", (flat,) * 2, (mid_fwd, mid_adj) + inner, 2 << 30, 8, halves)
    own, col, row, diag = kernel(
        image_kernel, "s" + "v" * 13, (piece,) * 4,
        (flags, speed2.reshape(FLAT, Y), lap_fwd, lap_adj, flat_fwd, flat_adj, mid_fwd, mid_adj, fwd_in2, adj_in2,
         below.reshape(AX * 8, Y), above.reshape(AX * 8, Y)) + rim, 1 << 30, 8, [pltpu.VMEM((AX, depth, Y), F32)])
    back_e = send(pair_e, diag)
    back_o = send(pair_o, diag)
    sum_a, sum_b = kernel(
        bucket_kernel, "svvvvv", (piece,) * 2, (flags, col, back_e, back_o, tag_e, tag_o), 1 << 20)
    sum_b = send(pair_b, sum_b)
    sum_a = send(pair_a, sum_a)
    same_e = send(pair_e, row)
    same_o = send(pair_o, row)
    (out,) = kernel(
        final_kernel, "s" + "v" * 8, (piece,), (flags, tile, own, same_e, same_o, tag_e, tag_o, sum_a, sum_b), 1 << 20)
    return out[None]


def solution(mesh):
    placed = (
        P("shot", None, "slab", None),
        P("shot", None, "slab", None),
        P("shot", None, "slab", None),
        P("shot", None),
        P("shot", None),
        P("shot", None, None),
        P("shot"),
        P("shot", None),
        P("shot", None, None),
    )
    return jax.shard_map(steps, mesh=mesh, in_specs=placed, out_specs=P("shot", None, "slab", None), check_vma=False)
```

profile of v0, /device:TPU:199, one launch (start us, length us, event | category | flops | bytes accessed | tf_op | source)
XLA Modules:
  0.0 117.8 jit_solution(9679707221442115053)
XLA Ops:
  0.0 12.7 %collective-permute-start.1 = (f32[32,16,128]{2,1,0:T(8,128)}, f32[32,16,128]{2,1,0:T(8,128)S(1)}, u32[]{:S(2)}, u32[]{:S(2)}) collective-permute-start(f32[32,16,128]{2,1,0:T(8,128)} %bitcast.vel.own.tile), channel_id=1, source_target_pairs={{6,12},{12,6},{30,36},{36,30},{54,60},{60,54},{78,84},{84,78},{102... | collective-permute-start | bytes 786440 | tf_op jit(solution)/shard_map/ppermute | solution.py:384
  12.7 0.0 copy-start.6
  12.7 0.6 copy-done.6
  13.4 1.2 %copy-done = f32[1,64,16,256]{3,2,1,0:T(8,128)S(1)} copy-done((f32[1,64,16,256]{3,2,1,0:T(8,128)S(1)}, f32[1,64,16,256]{3,2,1,0:T(8,128)}, u32[]{:S(2)}) %copy-start) | copy-done | bytes 1048600
  14.6 1.2 %copy-done.2 = f32[1,64,16,256]{3,2,1,0:T(8,128)S(1)} copy-done((f32[1,64,16,256]{3,2,1,0:T(8,128)S(1)}, f32[1,64,16,256]{3,2,1,0:T(8,128)}, u32[]{:S(2)}) %copy-start.2) | copy-done | bytes 1048600
  15.8 1.9 %shard_map.145 = (f32[64,8,256]{2,1,0:T(8,128)S(1)}, f32[64,8,256]{2,1,0:T(8,128)S(1)}, f32[34,16,128]{2,1,0:T(8,128)S(1)}, s32[8]{0:T(128)S(1)}) custom-call(s32[1,2]{1,0:T(1,128)S(1)} %copy-done.6, f32[32,16,128]{2,1,0:T(8,128)} %bitcast.vel.own.tile, f32[64,16,256]{2,1,0:T(8,128)S(1)} %bitcast.13, f32[64,16,256]{2,1,0:T(8,128)S(1)} %bitcast.17), custom_call_target="tpu_custom_call" | custom-call | flops 1048576 | bytes 3686440 | tf_op jit(solution)/shard_map/pallas_call | solution.py:390
  17.7 5.4 %collective-permute-start.3 = (f32[34,16,128]{2,1,0:T(8,128)S(1)}, f32[34,16,128]{2,1,0:T(8,128)S(1)}, u32[]{:S(2)}, u32[]{:S(2)}) collective-permute-start(f32[34,16,128]{2,1,0:T(8,128)S(1)} %get-tuple-element.33), channel_id=1, source_target_pairs={{24,48},{30,54},{36,60},{42,66},{48,24},{54,30},{60,36},{66,42},{7... | collective-permute-start | bytes 835592 | tf_op jit(solution)/shard_map/ppermute | solution.py:384
  23.1 1.9 %collective-permute-start.2 = (f32[34,16,128]{2,1,0:T(8,128)S(1)}, f32[34,16,128]{2,1,0:T(8,128)S(1)}, u32[]{:S(2)}, u32[]{:S(2)}) collective-permute-start(f32[34,16,128]{2,1,0:T(8,128)S(1)} %get-tuple-element.33), channel_id=1, source_target_pairs={{0,24},{6,30},{12,36},{18,42},{24,0},{30,6},{36,12},{42,18},{48,72... | collective-permute-start | bytes 835592 | tf_op jit(solution)/shard_map/ppermute | solution.py:384
  25.0 1.9 %collective-permute-start = (f32[32,16,128]{2,1,0:T(8,128)}, f32[32,16,128]{2,1,0:T(8,128)S(1)}, u32[]{:S(2)}, u32[]{:S(2)}) collective-permute-start(f32[32,16,128]{2,1,0:T(8,128)} %bitcast.vel.own.tile), channel_id=1, source_target_pairs={{0,6},{6,0},{12,18},{18,12},{24,30},{30,24},{36,42},{42,36},{48,54... | collective-permute-start | bytes 786440 | tf_op jit(solution)/shard_map/ppermute | solution.py:384
  27.0 3.7 %collective-permute-start.6 = (f32[64,8,256]{2,1,0:T(8,128)S(1)}, f32[64,8,256]{2,1,0:T(8,128)S(1)}, u32[]{:S(2)}, u32[]{:S(2)}) collective-permute-start(f32[64,8,256]{2,1,0:T(8,128)S(1)} %get-tuple-element.40), channel_id=1, source_target_pairs={{0,1},{1,2},{2,3},{3,4},{4,5},{6,7},{7,8},{8,9},{9,10},{10,11},{12... | collective-permute-start | bytes 1572872 | tf_op jit(solution)/shard_map/ppermute | solution.py:384
  30.7 0.0 collective-permute-done.1.col_b
  30.7 1.9 %collective-permute-start.7 = (f32[64,8,256]{2,1,0:T(8,128)S(1)}, f32[64,8,256]{2,1,0:T(8,128)S(1)}, u32[]{:S(2)}, u32[]{:S(2)}) collective-permute-start(f32[64,8,256]{2,1,0:T(8,128)S(1)} %get-tuple-element.41), channel_id=1, source_target_pairs={{1,0},{2,1},{3,2},{4,3},{5,4},{7,6},{8,7},{9,8},{10,9},{11,10},{13... | collective-permute-start | bytes 1572872 | tf_op jit(solution)/shard_map/ppermute | solution.py:384
  33.3 0.0 copy-done.1
  33.3 0.0 copy-done.3
  33.3 0.0 copy-done.11
  33.3 0.0 copy-start.12
  33.3 0.9 copy-done.12
  34.2 0.9 copy-done.14
  35.1 0.9 copy-done.16
  36.0 3.3 %shard_map.147 = (f32[1024,256]{1,0:T(8,128)S(1)}, f32[1024,256]{1,0:T(8,128)S(1)}) custom-call(f32[1024,256]{1,0:T(8,128)S(1)} %bitcast.14, f32[1024,256]{1,0:T(8,128)S(1)} %bitcast.18, bf16[3,128,256]{2,1,0:T(8,128)(2,1)S(1)} %copy-done.12, bf16[3,128,256]{2,1,0:T(8,128)(2,1)S(1)} %copy-done.11, bf16[256,256]{1,0:T(8,128)(2,1)S(1)} %copy-done.16, ...), custom_call_target="tpu_custom_call" | custom-call | flops 2147483648 | bytes 5505024 | tf_op jit(solution)/shard_map/pallas_call | solution.py:390
  39.4 0.0 collective-permute-done.col_a
  39.4 0.0 collective-permute-done.3.row_o
  39.4 0.0 collective-permute-done.2.row_e
  39.4 0.0 copy-start.7
  39.4 0.6 shard_map.146
  40.0 0.0 copy-start.8
  40.0 3.4 %collective-permute-start.4 = (f32[32,16,128]{2,1,0:T(8,128)S(1)}, f32[32,16,128]{2,1,0:T(8,128)S(1)}, u32[]{:S(2)}, u32[]{:S(2)}) collective-permute-start(f32[32,16,128]{2,1,0:T(8,128)S(1)} %get-tuple-element.34), channel_id=1, source_target_pairs={{0,24},{6,30},{12,36},{18,42},{24,0},{30,6},{36,12},{42,18},{48,72... | collective-permute-start | bytes 786440 | tf_op jit(solution)/shard_map/ppermute | solution.py:384
  43.5 2.6 %collective-permute-start.5 = (f32[32,16,128]{2,1,0:T(8,128)S(1)}, f32[32,16,128]{2,1,0:T(8,128)S(1)}, u32[]{:S(2)}, u32[]{:S(2)}) collective-permute-start(f32[32,16,128]{2,1,0:T(8,128)S(1)} %get-tuple-element.35), channel_id=1, source_target_pairs={{24,48},{30,54},{36,60},{42,66},{48,24},{54,30},{60,36},{66,42},{7... | collective-permute-start | bytes 786440 | tf_op jit(solution)/shard_map/ppermute | solution.py:384
  46.1 0.0 copy-start.9
  46.1 0.0 copy-start.10
  46.1 0.0 copy-done.7
  46.1 0.0 copy-done.8
  46.1 0.6 copy-done.9
  46.7 6.1 %shard_map.148 = (f32[1024,256]{1,0:T(8,128)S(1)}, f32[1024,256]{1,0:T(8,128)S(1)}, f32[1024,256]{1,0:T(8,128)S(1)}, f32[1024,256]{1,0:T(8,128)S(1)}) custom-call(s32[1]{0:T(128)S(6)} %copy.16.shot_count, s32[1,16]{1,0:T(1,128)S(1)} %copy-done.10, f32[2,16]{1,0:T(2,128)S(1)} %bitcast.27, s32[1,1024]{1,0:T(1,128)S(1)} %copy-done.8, f32[2,1024]{1,0:T(2,128)S(1)} %bitcast.26), custom_call_target="tpu_custom_call" | custom-call | flops 3221225472 | bytes 4206788 | tf_op jit(solution)/shard_map/pallas_call | solution.py:390
  52.9 0.0 collective-permute-done.6
  52.9 0.0 collective-permute-done.7
  52.9 0.0 collective-permute-done.4.diag_e
  52.9 1.4 %collective-permute-done.5.diag_o = f32[32,16,128]{2,1,0:T(8,128)S(1)} collective-permute-done((f32[32,16,128]{2,1,0:T(8,128)S(1)}, f32[32,16,128]{2,1,0:T(8,128)S(1)}, u32[]{:S(2)}, u32[]{:S(2)}) %collective-permute-start.5) | collective-permute-done | bytes 262176 | tf_op jit(solution)/shard_map/ppermute | solution.py:384
  54.3 0.0 copy-done.4
  54.3 0.0 copy-start.17
  54.3 3.3 %shard_map.149 = (f32[64,16,256]{2,1,0:T(8,128)S(1)}, f32[1024,256]{1,0:T(8,128)S(1)}, f32[1024,256]{1,0:T(8,128)S(1)}, f32[64,8,256]{2,1,0:T(8,128)S(1)}, f32[64,8,256]{2,1,0:T(8,128)S(1)}) custom-call(s32[8]{0:T(128)S(1)} %get-tuple-element.32.flags, f32[32,16,128]{2,1,0:T(8,128)} %bitcast.vel.own.tile, f32[32,16,128]{2,1,0:T(8,128)S(1)} %collective-permute-done.col_a, ...), custom_call_target="tpu_custom_call" | custom-call | flops 1073741824 | bytes 13664288 | tf_op jit(solution)/shard_map/pallas_call | solution.py:390
  57.6 4.2 %collective-permute-start.8 = (f32[64,8,256]{2,1,0:T(8,128)S(1)}, f32[64,8,256]{2,1,0:T(8,128)S(1)}, u32[]{:S(2)}, u32[]{:S(2)}) collective-permute-start(f32[64,8,256]{2,1,0:T(8,128)S(1)} %get-tuple-element.49), channel_id=1, source_target_pairs={{0,1},{1,2},{2,3},{3,4},{4,5},{6,7},{7,8},{8,9},{9,10},{10,11},{12... | collective-permute-start | bytes 1572872 | tf_op jit(solution)/shard_map/ppermute | solution.py:384
  61.8 1.9 %collective-permute-start.9 = (f32[64,8,256]{2,1,0:T(8,128)S(1)}, f32[64,8,256]{2,1,0:T(8,128)S(1)}, u32[]{:S(2)}, u32[]{:S(2)}) collective-permute-start(f32[64,8,256]{2,1,0:T(8,128)S(1)} %get-tuple-element.50), channel_id=1, source_target_pairs={{1,0},{2,1},{3,2},{4,3},{5,4},{7,6},{8,7},{9,8},{10,9},{11,10},{13... | collective-permute-start | bytes 1572872 | tf_op jit(solution)/shard_map/ppermute | solution.py:384
  63.8 0.0 copy-done.13
  63.8 0.0 copy-done.15
  63.8 0.0 copy-done.17
  63.8 3.4 %shard_map.150 = (f32[1024,256]{1,0:T(8,128)S(1)}, f32[1024,256]{1,0:T(8,128)S(1)}) custom-call(f32[1024,256]{1,0:T(8,128)S(1)} %get-tuple-element.43.fwd.mid_fwd, f32[1024,256]{1,0:T(8,128)S(1)} %get-tuple-element.44.adj.mid_adj, bf16[3,128,256]{2,1,0:T(8,128)(2,1)S(1)} %copy-done.13, bf16[3,128,256]{2,1,0:T(8,128)(2,1)S(1)} %copy-done.11, ...), custom_call_target="tpu_custom_call" | custom-call | flops 2147483648 | bytes 5505024 | tf_op jit(solution)/shard_map/pallas_call | solution.py:390
  67.2 3.9 %collective-permute-done.8 = f32[64,8,256]{2,1,0:T(8,128)S(1)} collective-permute-done((f32[64,8,256]{2,1,0:T(8,128)S(1)}, f32[64,8,256]{2,1,0:T(8,128)S(1)}, u32[]{:S(2)}, u32[]{:S(2)}) %collective-permute-start.8) | collective-permute-done | bytes 524320 | tf_op jit(solution)/shard_map/ppermute | solution.py:384
  71.1 4.8 %collective-permute-done.9 = f32[64,8,256]{2,1,0:T(8,128)S(1)} collective-permute-done((f32[64,8,256]{2,1,0:T(8,128)S(1)}, f32[64,8,256]{2,1,0:T(8,128)S(1)}, u32[]{:S(2)}, u32[]{:S(2)}) %collective-permute-start.9) | collective-permute-done | bytes 524320 | tf_op jit(solution)/shard_map/ppermute | solution.py:384
  75.9 3.1 %shard_map.151 = (f32[32,16,128]{2,1,0:T(8,128)S(1)}, f32[32,16,128]{2,1,0:T(8,128)S(1)}, f32[32,16,128]{2,1,0:T(8,128)S(1)}, f32[32,16,128]{2,1,0:T(8,128)S(1)}) custom-call(s32[8]{0:T(128)S(1)} %get-tuple-element.32.flags, f32[1024,256]{1,0:T(8,128)S(1)} %bitcast.21, f32[1024,256]{1,0:T(8,128)S(1)} %get-tuple-element.45.lap_fwd, ...), custom_call_target="tpu_custom_call" | custom-call | flops 1073741824 | bytes 11796512 | tf_op jit(solution)/shard_map/pallas_call | solution.py:390
  79.0 4.4 %collective-permute-start.13 = (f32[32,16,128]{2,1,0:T(8,128)S(1)}, f32[32,16,128]{2,1,0:T(8,128)S(1)}, u32[]{:S(2)}, u32[]{:S(2)}) collective-permute-start(f32[32,16,128]{2,1,0:T(8,128)S(1)} %get-tuple-element.56), channel_id=1, source_target_pairs={{24,48},{30,54},{36,60},{42,66},{48,24},{54,30},{60,36},{66,42},{7... | collective-permute-start | bytes 786440 | tf_op jit(solution)/shard_map/ppermute | solution.py:384
  83.3 1.9 %collective-permute-start.12 = (f32[32,16,128]{2,1,0:T(8,128)S(1)}, f32[32,16,128]{2,1,0:T(8,128)S(1)}, u32[]{:S(2)}, u32[]{:S(2)}) collective-permute-start(f32[32,16,128]{2,1,0:T(8,128)S(1)} %get-tuple-element.56), channel_id=1, source_target_pairs={{0,24},{6,30},{12,36},{18,42},{24,0},{30,6},{36,12},{42,18},{48,72... | collective-permute-start | bytes 786440 | tf_op jit(solution)/shard_map/ppermute | solution.py:384
  85.3 3.0 %collective-permute-start.11 = (f32[32,16,128]{2,1,0:T(8,128)S(1)}, f32[32,16,128]{2,1,0:T(8,128)S(1)}, u32[]{:S(2)}, u32[]{:S(2)}) collective-permute-start(f32[32,16,128]{2,1,0:T(8,128)S(1)} %get-tuple-element.52), channel_id=1, source_target_pairs={{24,48},{30,54},{36,60},{42,66},{48,24},{54,30},{60,36},{66,42},{7... | collective-permute-start | bytes 786440 | tf_op jit(solution)/shard_map/ppermute | solution.py:384
  88.3 2.9 %collective-permute-start.10 = (f32[32,16,128]{2,1,0:T(8,128)S(1)}, f32[32,16,128]{2,1,0:T(8,128)S(1)}, u32[]{:S(2)}, u32[]{:S(2)}) collective-permute-start(f32[32,16,128]{2,1,0:T(8,128)S(1)} %get-tuple-element.52), channel_id=1, source_target_pairs={{0,24},{6,30},{12,36},{18,42},{24,0},{30,6},{36,12},{42,18},{48,72... | collective-permute-start | bytes 786440 | tf_op jit(solution)/shard_map/ppermute | solution.py:384
  91.2 0.0 collective-permute-done.13.back_o
  91.2 0.0 collective-permute-done.12.back_e
  91.2 0.7 shard_map.152
  91.9 6.8 %collective-permute-start.14 = (f32[32,16,128]{2,1,0:T(8,128)S(1)}, f32[32,16,128]{2,1,0:T(8,128)S(1)}, u32[]{:S(2)}, u32[]{:S(2)}) collective-permute-start(f32[32,16,128]{2,1,0:T(8,128)S(1)} %get-tuple-element.57), channel_id=1, source_target_pairs={{0,6},{6,0},{12,18},{18,12},{24,30},{30,24},{36,42},{42,36},{48,54... | collective-permute-start | bytes 786440 | tf_op jit(solution)/shard_map/ppermute | solution.py:384
  98.7 1.9 %collective-permute-start.15 = (f32[32,16,128]{2,1,0:T(8,128)S(1)}, f32[32,16,128]{2,1,0:T(8,128)S(1)}, u32[]{:S(2)}, u32[]{:S(2)}) collective-permute-start(f32[32,16,128]{2,1,0:T(8,128)S(1)} %get-tuple-element.58), channel_id=1, source_target_pairs={{6,12},{12,6},{30,36},{36,30},{54,60},{60,54},{78,84},{84,78},{102... | collective-permute-start | bytes 786440 | tf_op jit(solution)/shard_map/ppermute | solution.py:384
  100.6 0.0 collective-permute-done.11.same_o
  100.6 0.0 collective-permute-done.10.same_e
  100.6 0.0 collective-permute-done.14.sum_a
  100.7 15.4 %collective-permute-done.15.sum_b = f32[32,16,128]{2,1,0:T(8,128)S(1)} collective-permute-done((f32[32,16,128]{2,1,0:T(8,128)S(1)}, f32[32,16,128]{2,1,0:T(8,128)S(1)}, u32[]{:S(2)}, u32[]{:S(2)}) %collective-permute-start.15) | collective-permute-done | bytes 262176 | tf_op jit(solution)/shard_map/ppermute | solution.py:384
  116.0 1.8 %shard_map.153 = f32[32,16,128]{2,1,0:T(8,128)} custom-call(s32[8]{0:T(128)S(1)} %get-tuple-element.32.flags, f32[32,16,128]{2,1,0:T(8,128)} %bitcast.vel.own.tile, f32[32,16,128]{2,1,0:T(8,128)S(1)} %get-tuple-element.51.own, f32[32,16,128]{2,1,0:T(8,128)S(1)} %collective-permute-done.10.same_e, f32[32,16,128]{2,1,0:T(8,128)S(1)} %collective-permute-done.11.same_o, ...), custom_call_target="tpu_custom_call" | custom-call | flops 1048576 | bytes 1867808 | tf_op jit(solution)/shard_map/pallas_call | solution.py:390
  (13 shorter events, 0.0 us)
Async XLA Ops:
  0.0 30.7 %collective-permute-start.1 = (f32[32,16,128]{2,1,0:T(8,128)}, f32[32,16,128]{2,1,0:T(8,128)S(1)}, u32[]{:S(2)}, u32[]{:S(2)}) collective-permute-start(f32[32,16,128]{2,1,0:T(8,128)} %bitcast.vel.own.tile), channel_id=1, source_target_pairs={{6,12},{12,6},{30,36},{36,30},{54,60},{60,54},{78,84},{84,78},{102... | collective-permute-start | bytes 786440 | tf_op jit(solution)/shard_map/ppermute | solution.py:384
  12.7 0.7 copy-start.6
  13.4 1.2 %copy-start = (f32[1,64,16,256]{3,2,1,0:T(8,128)S(1)}, f32[1,64,16,256]{3,2,1,0:T(8,128)}, u32[]{:S(2)}) copy-start(f32[1,64,16,256]{3,2,1,0:T(8,128)} %param.16) | copy-start | bytes 3145732
  14.6 1.2 %copy-start.2 = (f32[1,64,16,256]{3,2,1,0:T(8,128)S(1)}, f32[1,64,16,256]{3,2,1,0:T(8,128)}, u32[]{:S(2)}) copy-start(f32[1,64,16,256]{3,2,1,0:T(8,128)} %param.17) | copy-start | bytes 3145732
  15.8 17.4 %copy-start.1 = (f32[1,64,16,256]{3,2,1,0:T(8,128)S(1)}, f32[1,64,16,256]{3,2,1,0:T(8,128)}, u32[]{:S(2)}) copy-start(f32[1,64,16,256]{3,2,1,0:T(8,128)} %param.16) | copy-start | bytes 3145732
  15.8 17.4 %copy-start.3 = (f32[1,64,16,256]{3,2,1,0:T(8,128)S(1)}, f32[1,64,16,256]{3,2,1,0:T(8,128)}, u32[]{:S(2)}) copy-start(f32[1,64,16,256]{3,2,1,0:T(8,128)} %param.17) | copy-start | bytes 3145732
  15.8 17.5 %copy-start.11 = (bf16[3,128,256]{2,1,0:T(8,128)(2,1)S(1)}, bf16[3,128,256]{2,1,0:T(8,128)(2,1)}, u32[]{:S(2)}) copy-start(bf16[3,128,256]{2,1,0:T(8,128)(2,1)} %constant.13.clone.s_low) | copy-start | bytes 589828
  17.7 21.7 %collective-permute-start.3 = (f32[34,16,128]{2,1,0:T(8,128)S(1)}, f32[34,16,128]{2,1,0:T(8,128)S(1)}, u32[]{:S(2)}, u32[]{:S(2)}) collective-permute-start(f32[34,16,128]{2,1,0:T(8,128)S(1)} %get-tuple-element.33), channel_id=1, source_target_pairs={{24,48},{30,54},{36,60},{42,66},{48,24},{54,30},{60,36},{66,42},{7... | collective-permute-start | bytes 835592 | tf_op jit(solution)/shard_map/ppermute | solution.py:384
  23.1 16.3 %collective-permute-start.2 = (f32[34,16,128]{2,1,0:T(8,128)S(1)}, f32[34,16,128]{2,1,0:T(8,128)S(1)}, u32[]{:S(2)}, u32[]{:S(2)}) collective-permute-start(f32[34,16,128]{2,1,0:T(8,128)S(1)} %get-tuple-element.33), channel_id=1, source_target_pairs={{0,24},{6,30},{12,36},{18,42},{24,0},{30,6},{36,12},{42,18},{48,72... | collective-permute-start | bytes 835592 | tf_op jit(solution)/shard_map/ppermute | solution.py:384
  25.0 14.4 %collective-permute-start = (f32[32,16,128]{2,1,0:T(8,128)}, f32[32,16,128]{2,1,0:T(8,128)S(1)}, u32[]{:S(2)}, u32[]{:S(2)}) collective-permute-start(f32[32,16,128]{2,1,0:T(8,128)} %bitcast.vel.own.tile), channel_id=1, source_target_pairs={{0,6},{6,0},{12,18},{18,12},{24,30},{30,24},{36,42},{42,36},{48,54... | collective-permute-start | bytes 786440 | tf_op jit(solution)/shard_map/ppermute | solution.py:384
  27.0 25.9 %collective-permute-start.6 = (f32[64,8,256]{2,1,0:T(8,128)S(1)}, f32[64,8,256]{2,1,0:T(8,128)S(1)}, u32[]{:S(2)}, u32[]{:S(2)}) collective-permute-start(f32[64,8,256]{2,1,0:T(8,128)S(1)} %get-tuple-element.40), channel_id=1, source_target_pairs={{0,1},{1,2},{2,3},{3,4},{4,5},{6,7},{7,8},{8,9},{9,10},{10,11},{12... | collective-permute-start | bytes 1572872 | tf_op jit(solution)/shard_map/ppermute | solution.py:384
  30.7 22.2 %collective-permute-start.7 = (f32[64,8,256]{2,1,0:T(8,128)S(1)}, f32[64,8,256]{2,1,0:T(8,128)S(1)}, u32[]{:S(2)}, u32[]{:S(2)}) collective-permute-start(f32[64,8,256]{2,1,0:T(8,128)S(1)} %get-tuple-element.41), channel_id=1, source_target_pairs={{1,0},{2,1},{3,2},{4,3},{5,4},{7,6},{8,7},{9,8},{10,9},{11,10},{13... | collective-permute-start | bytes 1572872 | tf_op jit(solution)/shard_map/ppermute | solution.py:384
  33.3 0.9 copy-start.12
  34.2 0.9 copy-start.14
  35.1 0.9 copy-start.16
  39.4 6.7 %copy-start.7 = (f32[1,2,1024]{2,1,0:T(2,128)S(1)}, f32[1,2,1024]{2,1,0:T(2,128)}, u32[]{:S(2)}) copy-start(f32[1,2,1024]{2,1,0:T(2,128)} %param.23) | copy-start | bytes 24580
  40.0 6.1 %copy-start.8 = (s32[1,1024]{1,0:T(1,128)S(1)}, s32[1,1024]{1,0:T(1,128)}, u32[]{:S(2)}) copy-start(s32[1,1024]{1,0:T(1,128)} %receiver_cell.1) | copy-start | bytes 12292
  40.0 12.8 %collective-permute-start.4 = (f32[32,16,128]{2,1,0:T(8,128)S(1)}, f32[32,16,128]{2,1,0:T(8,128)S(1)}, u32[]{:S(2)}, u32[]{:S(2)}) collective-permute-start(f32[32,16,128]{2,1,0:T(8,128)S(1)} %get-tuple-element.34), channel_id=1, source_target_pairs={{0,24},{6,30},{12,36},{18,42},{24,0},{30,6},{36,12},{42,18},{48,72... | collective-permute-start | bytes 786440 | tf_op jit(solution)/shard_map/ppermute | solution.py:384
  43.5 10.8 %collective-permute-start.5 = (f32[32,16,128]{2,1,0:T(8,128)S(1)}, f32[32,16,128]{2,1,0:T(8,128)S(1)}, u32[]{:S(2)}, u32[]{:S(2)}) collective-permute-start(f32[32,16,128]{2,1,0:T(8,128)S(1)} %get-tuple-element.35), channel_id=1, source_target_pairs={{24,48},{30,54},{36,60},{42,66},{48,24},{54,30},{60,36},{66,42},{7... | collective-permute-start | bytes 786440 | tf_op jit(solution)/shard_map/ppermute | solution.py:384
  46.1 0.7 copy-start.9
  46.1 0.7 copy-start.10
  46.7 7.5 %copy-start.4 = (bf16[256,128]{1,0:T(8,128)(2,1)S(1)}, bf16[256,128]{1,0:T(8,128)(2,1)}, u32[]{:S(2)}) copy-start(bf16[256,128]{1,0:T(8,128)(2,1)} %constant.17.clone.h_low) | copy-start | bytes 196612
  46.7 7.5 %copy-start.5 = (bf16[256,128]{1,0:T(8,128)(2,1)S(1)}, bf16[256,128]{1,0:T(8,128)(2,1)}, u32[]{:S(2)}) copy-start(bf16[256,128]{1,0:T(8,128)(2,1)} %constant.16.clone.h_high) | copy-start | bytes 196612
  54.3 9.5 %copy-start.13 = (bf16[3,128,256]{2,1,0:T(8,128)(2,1)S(1)}, bf16[3,128,256]{2,1,0:T(8,128)(2,1)}, u32[]{:S(2)}) copy-start(bf16[3,128,256]{2,1,0:T(8,128)(2,1)} %constant.12.clone.s_high) | copy-start | bytes 589828
  54.3 9.5 %copy-start.15 = (bf16[256,256]{1,0:T(8,128)(2,1)S(1)}, bf16[256,256]{1,0:T(8,128)(2,1)}, u32[]{:S(2)}) copy-start(bf16[256,256]{1,0:T(8,128)(2,1)} %constant.15.clone.y_low) | copy-start | bytes 393220
  54.3 9.5 %copy-start.17 = (bf16[256,256]{1,0:T(8,128)(2,1)S(1)}, bf16[256,256]{1,0:T(8,128)(2,1)}, u32[]{:S(2)}) copy-start(bf16[256,256]{1,0:T(8,128)(2,1)} %constant.14.clone.y_high) | copy-start | bytes 393220
  57.6 13.5 %collective-permute-start.8 = (f32[64,8,256]{2,1,0:T(8,128)S(1)}, f32[64,8,256]{2,1,0:T(8,128)S(1)}, u32[]{:S(2)}, u32[]{:S(2)}) collective-permute-start(f32[64,8,256]{2,1,0:T(8,128)S(1)} %get-tuple-element.49), channel_id=1, source_target_pairs={{0,1},{1,2},{2,3},{3,4},{4,5},{6,7},{7,8},{8,9},{9,10},{10,11},{12... | collective-permute-start | bytes 1572872 | tf_op jit(solution)/shard_map/ppermute | solution.py:384
  61.8 14.1 %collective-permute-start.9 = (f32[64,8,256]{2,1,0:T(8,128)S(1)}, f32[64,8,256]{2,1,0:T(8,128)S(1)}, u32[]{:S(2)}, u32[]{:S(2)}) collective-permute-start(f32[64,8,256]{2,1,0:T(8,128)S(1)} %get-tuple-element.50), channel_id=1, source_target_pairs={{1,0},{2,1},{3,2},{4,3},{5,4},{7,6},{8,7},{9,8},{10,9},{11,10},{13... | collective-permute-start | bytes 1572872 | tf_op jit(solution)/shard_map/ppermute | solution.py:384
  79.0 12.2 %collective-permute-start.13 = (f32[32,16,128]{2,1,0:T(8,128)S(1)}, f32[32,16,128]{2,1,0:T(8,128)S(1)}, u32[]{:S(2)}, u32[]{:S(2)}) collective-permute-start(f32[32,16,128]{2,1,0:T(8,128)S(1)} %get-tuple-element.56), channel_id=1, source_target_pairs={{24,48},{30,54},{36,60},{42,66},{48,24},{54,30},{60,36},{66,42},{7... | collective-permute-start | bytes 786440 | tf_op jit(solution)/shard_map/ppermute | solution.py:384
  83.3 7.9 %collective-permute-start.12 = (f32[32,16,128]{2,1,0:T(8,128)S(1)}, f32[32,16,128]{2,1,0:T(8,128)S(1)}, u32[]{:S(2)}, u32[]{:S(2)}) collective-permute-start(f32[32,16,128]{2,1,0:T(8,128)S(1)} %get-tuple-element.56), channel_id=1, source_target_pairs={{0,24},{6,30},{12,36},{18,42},{24,0},{30,6},{36,12},{42,18},{48,72... | collective-permute-start | bytes 786440 | tf_op jit(solution)/shard_map/ppermute | solution.py:384
  85.3 15.3 %collective-permute-start.11 = (f32[32,16,128]{2,1,0:T(8,128)S(1)}, f32[32,16,128]{2,1,0:T(8,128)S(1)}, u32[]{:S(2)}, u32[]{:S(2)}) collective-permute-start(f32[32,16,128]{2,1,0:T(8,128)S(1)} %get-tuple-element.52), channel_id=1, source_target_pairs={{24,48},{30,54},{36,60},{42,66},{48,24},{54,30},{60,36},{66,42},{7... | collective-permute-start | bytes 786440 | tf_op jit(solution)/shard_map/ppermute | solution.py:384
  88.3 12.3 %collective-permute-start.10 = (f32[32,16,128]{2,1,0:T(8,128)S(1)}, f32[32,16,128]{2,1,0:T(8,128)S(1)}, u32[]{:S(2)}, u32[]{:S(2)}) collective-permute-start(f32[32,16,128]{2,1,0:T(8,128)S(1)} %get-tuple-element.52), channel_id=1, source_target_pairs={{0,24},{6,30},{12,36},{18,42},{24,0},{30,6},{36,12},{42,18},{48,72... | collective-permute-start | bytes 786440 | tf_op jit(solution)/shard_map/ppermute | solution.py:384
  91.9 8.8 %collective-permute-start.14 = (f32[32,16,128]{2,1,0:T(8,128)S(1)}, f32[32,16,128]{2,1,0:T(8,128)S(1)}, u32[]{:S(2)}, u32[]{:S(2)}) collective-permute-start(f32[32,16,128]{2,1,0:T(8,128)S(1)} %get-tuple-element.57), channel_id=1, source_target_pairs={{0,6},{6,0},{12,18},{18,12},{24,30},{30,24},{36,42},{42,36},{48,54... | collective-permute-start | bytes 786440 | tf_op jit(solution)/shard_map/ppermute | solution.py:384
  98.7 17.3 %collective-permute-start.15 = (f32[32,16,128]{2,1,0:T(8,128)S(1)}, f32[32,16,128]{2,1,0:T(8,128)S(1)}, u32[]{:S(2)}, u32[]{:S(2)}) collective-permute-start(f32[32,16,128]{2,1,0:T(8,128)S(1)} %get-tuple-element.58), channel_id=1, source_target_pairs={{6,12},{12,6},{30,36},{36,30},{54,60},{60,54},{78,84},{84,78},{102... | collective-permute-start | bytes 786440 | tf_op jit(solution)/shard_map/ppermute | solution.py:384
where the time goes:
time: 119 us; the launch traced here: 118 us
  starting transfers between devices  60.6 us (51%)
  waiting for transfers between devices  25.4 us (21%)
  Pallas kernels  24.2 us (20%)
  local copies, waits for them, and re-layouts  6.52 us (5%)
    ppermute x16, starting transfers between devices, send(): return lax.ppermute(value, axis, pairs)  60.6 us
    ppermute x16, waiting for transfers between devices, send(): return lax.ppermute(value, axis, pairs)  25.4 us
    pallas_call x9, Pallas kernels, kernel(): pl.pallas_call(function, out_shape=tuple(outs), in_specs=places, out_spec...  24.2 us
    unnamed x36, local copies, waits for them, and re-layouts  6.52 us
  transfers between devices with their start and end apart: 16, of which 4 were waited for; matrix products, arithmetic and copies ran while one was open for 0% of the time, Pallas kernels for 14%

commit v1 on v0

--- a/solution.py
+++ b/solution.py
@@ -10,8 +10,10 @@
 
 
 TILES_Y = 4
-CENTRE = -205.0 / 72.0
-STENCIL = (1.6, -0.2, 8.0 / 315.0, -1.0 / 560.0)
+SCALE = 5040.0
+STENCIL = (8064.0, -1008.0, 128.0, -9.0)
+CENTRE_XZ = -43008.0
+CENTRE_Y = -42.0
 
 BX = 8
 Z = 16
@@ -33,10 +35,10 @@
     return table[np.minimum(distance, 5)]
 
 
-def parts_of(matrix):
-    high = matrix.astype(np.float32).astype(jnp.bfloat16)
-    low = (matrix - high.astype(np.float64)).astype(np.float32).astype(jnp.bfloat16)
-    return high, low
+def exact(matrix):
+    narrow = matrix.astype(np.float32).astype(jnp.bfloat16)
+    assert np.array_equal(narrow.astype(np.float64), matrix)
+    return jnp.asarray(narrow)
 
 
 def along_xz():
@@ -47,30 +49,24 @@
         dx = out_x[:, None] - (in_x[None, :] - lead)
         dz = out_z[:, None] - in_z[None, :]
         both = np.where(dz == 0, weight(dx), 0.0) + np.where(dx == 0, weight(dz), 0.0)
-        kinds.append(both + np.where((dx == 0) & (dz == 0), 3.0 * CENTRE, 0.0))
+        kinds.append(both + np.where((dx == 0) & (dz == 0), CENTRE_XZ, 0.0))
     return np.stack(kinds)
 
 
 def along_y():
     at = np.arange(Y)
-    return weight(at[:, None] - at[None, :])
+    return weight(at[:, None] - at[None, :]) + CENTRE_Y * np.eye(Y)
 
 
 def along_halo():
-    out_x, out_z = np.divmod(np.arange(ROWS), Z)
-    in_x, in_s = np.divmod(np.arange(BX * 8), 8)
-    fields = []
-    for field in (0, 1):
-        sides = []
-        for side in (0, 1):
-            layer = in_s - 4 * field
-            depth = layer - 4 if side == 0 else Z + layer
-            mine = (layer >= 0) & (layer < 4)
-            dz = out_z[:, None] - depth[None, :]
-            same = (out_x[:, None] == in_x[None, :]) & mine[None, :]
-            sides.append(np.where(same, weight(dz), 0.0))
-        fields.append(np.concatenate(sides, 1))
-    return np.concatenate(fields, 0)
+    field, rest = np.divmod(np.arange(ROWS), BX * 8)
+    out_x, out_s = np.divmod(rest, 8)
+    out_z = np.where(out_s < 4, out_s, Z - 8 + out_s)
+    side, rest = np.divmod(np.arange(ROWS), BX * 8)
+    in_x, in_s = np.divmod(rest, 8)
+    in_z = np.where(side == 0, in_s % 4 - 4, Z + in_s % 4)
+    same = (out_x[:, None] == in_x[None, :]) & (field[:, None] == in_s[None, :] // 4)
+    return np.where(same, weight(out_z[:, None] - in_z[None, :]), 0.0)
 
 
 def dot(a, b):
@@ -80,6 +76,13 @@
 def split(value):
     high = value.astype(BF16)
     return high, (value - high.astype(F32)).astype(BF16)
+
+
+def split3(value):
+    high = value.astype(BF16)
+    rest = value - high.astype(F32)
+    middle = rest.astype(BF16)
+    return high, middle, (rest - middle.astype(F32)).astype(BF16)
 
 
 def cost(flops, nbytes):
@@ -93,7 +96,7 @@
     return top, bottom
 
 
-def pack_kernel(anchor, vel, fwd, adj, up, down, tagged, flags):
+def tag_kernel(anchor, vel, tagged, flags):
     device = lax.axis_index("shot")
     home_row = device // TILES_Y
     home_col = device - home_row * TILES_Y
@@ -113,6 +116,15 @@
     tagged[rows] = jnp.full(tagged.shape[1:], side_row.astype(F32))
     tagged[rows + 1] = jnp.full(tagged.shape[1:], side_col.astype(F32))
 
+    def copy(i, _):
+        at = pl.ds(i * 8, 8)
+        tagged[at] = vel[at]
+        return 0
+
+    lax.fori_loop(0, rows // 8, copy, 0)
+
+
+def rims_kernel(fwd, adj, up, down):
     def step(b, _):
         at = pl.ds(b * BX, BX)
         up[at], down[at] = rims(fwd[at], adj[at])
@@ -120,30 +132,22 @@
 
     lax.fori_loop(0, BLOCKS, step, 0)
 
-    def copy(i, _):
-        at = pl.ds(i * 8, 8)
-        tagged[at] = vel[at]
-        return 0
-
-    lax.fori_loop(0, rows // 8, copy, 0)
-
-
-def inner_laplace(b, high, low, s_high, s_low, y_high, y_low):
+
+def inner_laplace(b, parts, xz, y):
     kind = jnp.where(b == 0, 0, jnp.where(b == BLOCKS - 1, 2, 1))
     first = jnp.clip(b * BX - 4, 0, AX - 2 * BX) * Z
     window = pl.ds(pl.multiple_of(first, 64), 2 * ROWS)
     own = pl.ds(pl.multiple_of(b * ROWS, ROWS), ROWS)
-    wide = high[window]
-    near = high[own]
-    result = dot(s_high[kind], wide) + dot(near, y_high[...])
-    result = result + dot(s_high[kind], low[window]) + dot(low[own], y_high[...])
-    return result + dot(s_low[kind], wide) + dot(near, y_low[...])
-
-
-def split_all(field, high, low):
+    high, middle, low = parts
+    result = dot(xz[kind], low[window]) + dot(low[own], y[...])
+    result = result + (dot(xz[kind], middle[window]) + dot(middle[own], y[...]))
+    return result + (dot(xz[kind], high[window]) + dot(high[own], y[...]))
+
+
+def split_all(field, parts):
     def step(b, _):
         at = pl.ds(pl.multiple_of(b * ROWS, ROWS), ROWS)
-        high[at], low[at] = split(field[at])
+        parts[0][at], parts[1][at], parts[2][at] = split3(field[at])
         return 0
 
     lax.fori_loop(0, BLOCKS, step, 0)
@@ -162,15 +166,14 @@
     table[3:4, 0:count] = amounts[1]
 
 
-def columns_of(points, columns):
+def columns_of(points, n, columns):
     def step(i, _):
         at = pl.ds(pl.multiple_of(i * 128, 128), 128)
         part = points[:, at].T
         here = lax.broadcasted_iota(jnp.int32, (128, Y), 1) == part[:, 1:2].astype(jnp.int32)
-        for n in range(2):
-            high, low = split(part[:, 2 + n : 3 + n])
-            columns[at, pl.ds(2 * n * Y, Y)] = jnp.where(here, high.astype(F32), 0.0).astype(BF16)
-            columns[at, pl.ds((2 * n + 1) * Y, Y)] = jnp.where(here, low.astype(F32), 0.0).astype(BF16)
+        high, low = split(part[:, 2 + n : 3 + n])
+        columns[at, :Y] = jnp.where(here, high.astype(F32), 0.0).astype(BF16)
+        columns[at, Y:] = jnp.where(here, low.astype(F32), 0.0).astype(BF16)
         return 0
 
     lax.fori_loop(0, points.shape[1] // 128, step, 0)
@@ -179,52 +182,56 @@
 def injected(b, points, columns):
     rows = lax.broadcasted_iota(jnp.int32, (ROWS, points.shape[1]), 0) + b * ROWS
     hot = jnp.where(rows == points[0:1, :].astype(jnp.int32), 1.0, 0.0).astype(BF16)
-    first = dot(hot, columns[:, : 2 * Y])
-    second = dot(hot, columns[:, 2 * Y :])
-    return first[:, :Y] + first[:, Y:], second[:, :Y] + second[:, Y:]
-
-
-def inject_kernel(total_depth, shot_count, source_cell, wavelet, receiver_cell, residual, fwd_in1, fwd_in2, adj_in1, adj_in2,
+    both = dot(hot, columns[...])
+    return both[:, :Y] + both[:, Y:]
+
+
+def inject_kernel(total_depth, n, shot_count, source_cell, wavelet, receiver_cell, residual, after, fwd_in, adj_in,
                   shots, receivers, shot_columns, receiver_columns):
     first_layer = lax.axis_index("slab") * Z
     active = lax.broadcasted_iota(jnp.int32, source_cell.shape, 1) < shot_count[0]
-    waves = [jnp.where(active, wavelet[n : n + 1, :], 0.0) for n in range(2)]
+    waves = [jnp.where(active, wavelet[i : i + 1, :], 0.0) for i in range(2)]
     table_of(source_cell[...], waves, first_layer, total_depth, shots)
     table_of(receiver_cell[...], [residual[1:2, :], residual[0:1, :]], first_layer, total_depth, receivers)
-    columns_of(shots, shot_columns)
-    columns_of(receivers, receiver_columns)
+    columns_of(shots, n, shot_columns)
+    columns_of(receivers, n, receiver_columns)
 
     def step(b, _):
         at = pl.ds(pl.multiple_of(b * ROWS, ROWS), ROWS)
-        fwd_in1[at], fwd_in2[at] = injected(b, shots, shot_columns)
-        adj_in1[at], adj_in2[at] = injected(b, receivers, receiver_columns)
-        return 0
-
-    lax.fori_loop(0, BLOCKS, step, 0)
-
-
-def laplace_kernel(fwd, adj, s_high, s_low, y_high, y_low, lap_fwd, lap_adj, fh, fl, ah, al):
-    split_all(fwd, fh, fl)
-    split_all(adj, ah, al)
+        fwd_in[at] = injected(b, shots, shot_columns)
+        adj_in[at] = injected(b, receivers, receiver_columns)
+        return 0
+
+    lax.fori_loop(0, BLOCKS, step, 0)
+
+
+def laplace_kernel(fwd, adj, xz, y, lap_fwd, lap_adj, f0, f1, f2, a0, a1, a2):
+    split_all(fwd, (f0, f1, f2))
+    split_all(adj, (a0, a1, a2))
 
     def step(b, _):
         at = pl.ds(pl.multiple_of(b * ROWS, ROWS), ROWS)
-        lap_fwd[at] = inner_laplace(b, fh, fl, s_high, s_low, y_high, y_low)
-        lap_adj[at] = inner_laplace(b, ah, al, s_high, s_low, y_high, y_low)
-        return 0
-
-    lax.fori_loop(0, BLOCKS, step, 0)
-
-
-def halo_part(b, below, above, h_high, h_low):
+        lap_fwd[at] = inner_laplace(b, (f0, f1, f2), xz, y)
+        lap_adj[at] = inner_laplace(b, (a0, a1, a2), xz, y)
+        return 0
+
+    lax.fori_loop(0, BLOCKS, step, 0)
+
+
+def halo_part(b, below, above, halo):
     at = pl.ds(pl.multiple_of(b * (ROWS // 2), ROWS // 2), ROWS // 2)
-    high, low = split(jnp.concatenate([below[at], above[at]], 0))
-    both = dot(h_high[...], high) + dot(h_high[...], low) + dot(h_low[...], high)
-    return both[:ROWS], both[ROWS:]
+    high, middle, low = split3(jnp.concatenate([below[at], above[at]], 0))
+    both = dot(halo[...], low) + dot(halo[...], middle) + dot(halo[...], high)
+    front = lax.broadcasted_iota(jnp.int32, (BX, 8, Y), 1) < 4
+    fields = []
+    for part in (both[: ROWS // 2], both[ROWS // 2 :]):
+        part = part.reshape(BX, 8, Y)
+        fields.append(jnp.concatenate([jnp.where(front, part, 0.0), jnp.where(front, 0.0, part)], 1).reshape(ROWS, Y))
+    return fields
 
 
 def advance_kernel(flags, own, col_a, col_b, row_e, row_o, diag_e, diag_o, lap_fwd, lap_adj, fwd, adj, fwd_in, adj_in,
-                   below, above, h_high, h_low, speed2, mid_fwd, mid_adj, up, down):
+                   below, above, halo, speed2, mid_fwd, mid_adj, up, down):
     half = own.shape[0]
     wide = own.shape[2]
     with_e = flags[2] == 1
@@ -239,13 +246,13 @@
         near = pl.ds(row_at + i * 8, 8)
         far = pl.ds(row_to + i * 8, 8)
         speed = own[at]
-        speed2[near, :, col_at] = speed * speed
+        speed2[near, :, col_at] = speed * speed * (1.0 / SCALE)
         speed = jnp.where(with_a, col_a[at], col_b[at])
-        speed2[near, :, col_to] = speed * speed
+        speed2[near, :, col_to] = speed * speed * (1.0 / SCALE)
         speed = jnp.where(with_e, row_e[at], row_o[at])
-        speed2[far, :, col_at] = speed * speed
+        speed2[far, :, col_at] = speed * speed * (1.0 / SCALE)
         speed = jnp.where(with_e, diag_e[at], diag_o[at])
-        speed2[far, :, col_to] = speed * speed
+        speed2[far, :, col_to] = speed * speed * (1.0 / SCALE)
         return 0
 
     lax.fori_loop(0, half // 8, assemble, 0)
@@ -253,7 +260,7 @@
     def step(b, _):
         at = pl.ds(pl.multiple_of(b * ROWS, ROWS), ROWS)
         blk = pl.ds(b * BX, BX)
-        halo_fwd, halo_adj = halo_part(b, below, above, h_high, h_low)
+        halo_fwd, halo_adj = halo_part(b, below, above, halo)
         c = speed2[blk].reshape(ROWS, Y)
         new_fwd = fwd[at] + (c * (lap_fwd[at] + halo_fwd) + fwd_in[at])
         new_adj = adj[at] + (c * (lap_adj[at] + halo_adj) + adj_in[at])
@@ -265,11 +272,11 @@
     lax.fori_loop(0, BLOCKS, step, 0)
 
 
-def image_kernel(flags, speed2, lap_fwd, lap_adj, fwd, adj, mid_fwd, mid_adj, fwd_in, adj_in, below, above, h_high, h_low,
+def image_kernel(flags, speed2, lap_fwd, lap_adj, fwd, adj, mid_fwd, mid_adj, fwd_in, adj_in, below, above, halo,
                  own, col, row, diag, image):
     def step(b, _):
         at = pl.ds(pl.multiple_of(b * ROWS, ROWS), ROWS)
-        halo_fwd, halo_adj = halo_part(b, below, above, h_high, h_low)
+        halo_fwd, halo_adj = halo_part(b, below, above, halo)
         c = speed2[at]
         second_fwd = c * (lap_fwd[at] + halo_fwd) + fwd_in[at]
         second_adj = c * (lap_adj[at] + halo_adj) + adj_in[at]
@@ -400,12 +407,9 @@
     piece = shape(half, depth, wide)
     rim_shape = shape(AX, 8, Y)
     flat = shape(FLAT, Y)
-    halves = [pltpu.VMEM((FLAT, Y), BF16)] * 4
-    s_high, s_low = parts_of(along_xz())
-    y_high, y_low = parts_of(along_y())
-    h_high, h_low = parts_of(along_halo())
-    inner = tuple(jnp.asarray(m) for m in (s_high, s_low, y_high, y_low))
-    rim = tuple(jnp.asarray(m) for m in (h_high, h_low))
+    parts = [pltpu.VMEM((FLAT, Y), BF16)] * 6
+    inner = (exact(along_xz()), exact(along_y()))
+    rim = (exact(along_halo()),)
 
     col_b = send(pair_b, tile)
     col_a = send(pair_a, tile)
@@ -413,34 +417,39 @@
     adj = adj_field[0]
     flat_fwd = fwd.reshape(FLAT, Y)
     flat_adj = adj.reshape(FLAT, Y)
-    up, down, tagged, flags = kernel(
-        pack_kernel, "svvv", (rim_shape, rim_shape, shape(half + 2, depth, wide), shape(8, dtype=jnp.int32)),
-        (aperture_anchor, tile, fwd, adj), 1 << 20)
+    tagged, flags = kernel(
+        tag_kernel, "sv", (shape(half + 2, depth, wide), shape(8, dtype=jnp.int32)), (aperture_anchor, tile), 1 << 20)
     row_e = send(pair_e, tagged)
     row_o = send(pair_o, tagged)
+    up, down = kernel(rims_kernel, "vv", (rim_shape, rim_shape), (fwd, adj), 1 << 20)
     below = send(to_up, up, "slab")
     above = send(to_down, down, "slab")
     recv = receiver_cell.shape[1]
-    fwd_in1, fwd_in2, adj_in1, adj_in2 = kernel(
-        functools.partial(inject_kernel, depth * slabs), "svvvv", (flat,) * 4,
-        (shot_count, source_cell, wavelet[0], receiver_cell, residual[0]), 3 << 30, 12,
-        [pltpu.VMEM((8, 128), F32), pltpu.VMEM((8, recv), F32), pltpu.VMEM((128, 4 * Y), BF16), pltpu.VMEM((recv, 4 * Y), BF16)])
+
+    def inject(n, after):
+        return kernel(
+            functools.partial(inject_kernel, depth * slabs, n), "svvvvs", (flat,) * 2,
+            (shot_count, source_cell, wavelet[0], receiver_cell, residual[0], after), 2 << 30, 12,
+            [pltpu.VMEM((8, 128), F32), pltpu.VMEM((8, recv), F32), pltpu.VMEM((128, 2 * Y), BF16), pltpu.VMEM((recv, 2 * Y), BF16)])
+
+    fwd_in1, adj_in1 = inject(0, flags)
     diag_e, diag_o, tag_e, tag_o = kernel(
         select_kernel, "svvvv", (piece, piece, shape(2, depth, wide), shape(2, depth, wide)),
         (flags, col_a, col_b, row_e, row_o), 1 << 20)
     diag_e = send(pair_e, diag_e)
     diag_o = send(pair_o, diag_o)
     lap_fwd, lap_adj = kernel(
-        laplace_kernel, "vvvvvv", (flat,) * 2, (flat_fwd, flat_adj) + inner, 2 << 30, 8, halves)
+        laplace_kernel, "vvvv", (flat,) * 2, (flat_fwd, flat_adj) + inner, 2 << 30, 8, parts)
     speed2, mid_fwd, mid_adj, up, down = kernel(
-        advance_kernel, "s" + "v" * 17, (shape(AX, depth, Y), flat, flat, rim_shape, rim_shape),
+        advance_kernel, "s" + "v" * 16, (shape(AX, depth, Y), flat, flat, rim_shape, rim_shape),
         (flags, tile, col_a, col_b, row_e, row_o, diag_e, diag_o, lap_fwd, lap_adj, flat_fwd, flat_adj, fwd_in1, adj_in1,
          below.reshape(AX * 8, Y), above.reshape(AX * 8, Y)) + rim, 1 << 30)
     below = send(to_up, up, "slab")
     above = send(to_down, down, "slab")
-    lap_fwd, lap_adj = kernel(laplace_kernel, "vvvvvv", (flat,) * 2, (mid_fwd, mid_adj) + inner, 2 << 30, 8, halves)
+    lap_fwd, lap_adj = kernel(laplace_kernel, "vvvv", (flat,) * 2, (mid_fwd, mid_adj) + inner, 2 << 30, 8, parts)
+    fwd_in2, adj_in2 = inject(1, flags)
     own, col, row, diag = kernel(
-        image_kernel, "s" + "v" * 13, (piece,) * 4,
+        image_kernel, "s" + "v" * 12, (piece,) * 4,
         (flags, speed2.reshape(FLAT, Y), lap_fwd, lap_adj, flat_fwd, flat_adj, mid_fwd, mid_adj, fwd_in2, adj_in2,
          below.reshape(AX * 8, Y), above.reshape(AX * 8, Y)) + rim, 1 << 30, 8, [pltpu.VMEM((AX, depth, Y), F32)])
     back_e = send(pair_e, diag)

time: 119 us -> 113 us (0.950)
  the two profiles are of different devices: /device:TPU:199 before, /device:TPU:195 now
where the time goes in v1:
time: 113 us; the launch traced here: 112 us
  starting transfers between devices  68.5 us (61%)
  Pallas kernels  27.8 us (25%)
  waiting for transfers between devices  11.8 us (10%)
  local copies, waits for them, and re-layouts  3.13 us (3%)
    ppermute x16, starting transfers between devices, send(): return lax.ppermute(value, axis, pairs)  68.5 us
    pallas_call x11, Pallas kernels, kernel(): pl.pallas_call(function, out_shape=tuple(outs), in_specs=places, out_spec...  27.8 us
    ppermute x16, waiting for transfers between devices, send(): return lax.ppermute(value, axis, pairs)  11.8 us
    unnamed x24, local copies, waits for them, and re-layouts  3.13 us
  transfers between devices with their start and end apart: 16, of which 3 were waited for; matrix products, arithmetic and copies ran while one was open for 0% of the time, Pallas kernels for 18%

profile of v1, /device:TPU:195, one launch (start us, length us, event | category | flops | bytes accessed | tf_op | source)
XLA Modules:
  0.0 112.3 jit_solution(16429544414937623156)
XLA Ops:
  0.0 0.0 copy-start.5
  0.0 2.7 %collective-permute-start = (f32[32,16,128]{2,1,0:T(8,128)}, f32[32,16,128]{2,1,0:T(8,128)S(1)}, u32[]{:S(2)}, u32[]{:S(2)}) collective-permute-start(f32[32,16,128]{2,1,0:T(8,128)} %bitcast.vel.own.tile), channel_id=1, source_target_pairs={{0,6},{6,0},{12,18},{18,12},{24,30},{30,24},{36,42},{42,36},{48,54... | collective-permute-start | bytes 786440 | tf_op jit(solution)/shard_map/ppermute | solution.py:391
  2.7 0.0 copy-done.5
  2.7 1.6 %shard_map.118 = (f32[34,16,128]{2,1,0:T(8,128)S(1)}, s32[8]{0:T(128)S(1)}) custom-call(s32[1,2]{1,0:T(1,128)S(1)} %copy-done.5, f32[32,16,128]{2,1,0:T(8,128)} %bitcast.vel.own.tile), custom_call_target="tpu_custom_call" | custom-call | flops 1048576 | bytes 540712 | tf_op jit(solution)/shard_map/pallas_call | solution.py:397
  4.3 3.2 %collective-permute-start.2 = (f32[34,16,128]{2,1,0:T(8,128)S(1)}, f32[34,16,128]{2,1,0:T(8,128)S(1)}, u32[]{:S(2)}, u32[]{:S(2)}) collective-permute-start(f32[34,16,128]{2,1,0:T(8,128)S(1)} %get-tuple-element.33), channel_id=1, source_target_pairs={{0,24},{6,30},{12,36},{18,42},{24,0},{30,6},{36,12},{42,18},{48,72... | collective-permute-start | bytes 835592 | tf_op jit(solution)/shard_map/ppermute | solution.py:391
  7.5 4.8 %collective-permute-start.3 = (f32[34,16,128]{2,1,0:T(8,128)S(1)}, f32[34,16,128]{2,1,0:T(8,128)S(1)}, u32[]{:S(2)}, u32[]{:S(2)}) collective-permute-start(f32[34,16,128]{2,1,0:T(8,128)S(1)} %get-tuple-element.33), channel_id=1, source_target_pairs={{24,48},{30,54},{36,60},{42,66},{48,24},{54,30},{60,36},{66,42},{7... | collective-permute-start | bytes 835592 | tf_op jit(solution)/shard_map/ppermute | solution.py:391
  12.4 12.6 %collective-permute-start.1 = (f32[32,16,128]{2,1,0:T(8,128)}, f32[32,16,128]{2,1,0:T(8,128)S(1)}, u32[]{:S(2)}, u32[]{:S(2)}) collective-permute-start(f32[32,16,128]{2,1,0:T(8,128)} %bitcast.vel.own.tile), channel_id=1, source_target_pairs={{6,12},{12,6},{30,36},{36,30},{54,60},{60,54},{78,84},{84,78},{102... | collective-permute-start | bytes 786440 | tf_op jit(solution)/shard_map/ppermute | solution.py:391
  25.0 0.0 copy-start
  25.0 1.2 %copy-done = f32[1,64,16,256]{3,2,1,0:T(8,128)S(1)} copy-done((f32[1,64,16,256]{3,2,1,0:T(8,128)S(1)}, f32[1,64,16,256]{3,2,1,0:T(8,128)}, u32[]{:S(2)}) %copy-start) | copy-done | bytes 1048600
  26.3 0.0 copy-start.2
  26.3 1.2 %copy-done.2 = f32[1,64,16,256]{3,2,1,0:T(8,128)S(1)} copy-done((f32[1,64,16,256]{3,2,1,0:T(8,128)S(1)}, f32[1,64,16,256]{3,2,1,0:T(8,128)}, u32[]{:S(2)}) %copy-start.2) | copy-done | bytes 1048600
  27.5 0.0 copy-start.3
  27.5 0.1 shard_map.122
  27.6 0.0 copy-start.1
  27.6 3.8 %collective-permute-start.6 = (f32[64,8,256]{2,1,0:T(8,128)S(1)}, f32[64,8,256]{2,1,0:T(8,128)S(1)}, u32[]{:S(2)}, u32[]{:S(2)}) collective-permute-start(f32[64,8,256]{2,1,0:T(8,128)S(1)} %get-tuple-element.40), channel_id=1, source_target_pairs={{0,1},{1,2},{2,3},{3,4},{4,5},{6,7},{7,8},{8,9},{9,10},{10,11},{12... | collective-permute-start | bytes 1572872 | tf_op jit(solution)/shard_map/ppermute | solution.py:391
  31.5 0.0 collective-permute-done.col_a
  31.5 1.9 %collective-permute-start.7 = (f32[64,8,256]{2,1,0:T(8,128)S(1)}, f32[64,8,256]{2,1,0:T(8,128)S(1)}, u32[]{:S(2)}, u32[]{:S(2)}) collective-permute-start(f32[64,8,256]{2,1,0:T(8,128)S(1)} %get-tuple-element.41), channel_id=1, source_target_pairs={{1,0},{2,1},{3,2},{4,3},{5,4},{7,6},{8,7},{9,8},{10,9},{11,10},{13... | collective-permute-start | bytes 1572872 | tf_op jit(solution)/shard_map/ppermute | solution.py:391
  33.4 1.5 %collective-permute-done.1.col_b = f32[32,16,128]{2,1,0:T(8,128)S(1)} collective-permute-done((f32[32,16,128]{2,1,0:T(8,128)}, f32[32,16,128]{2,1,0:T(8,128)S(1)}, u32[]{:S(2)}, u32[]{:S(2)}) %collective-permute-start.1) | collective-permute-done | bytes 262176 | tf_op jit(solution)/shard_map/ppermute | solution.py:391
  35.0 0.0 collective-permute-done.2.row_e
  35.0 0.0 collective-permute-done.3.row_o
  35.0 0.6 shard_map.119
  35.6 1.9 %collective-permute-start.4 = (f32[32,16,128]{2,1,0:T(8,128)S(1)}, f32[32,16,128]{2,1,0:T(8,128)S(1)}, u32[]{:S(2)}, u32[]{:S(2)}) collective-permute-start(f32[32,16,128]{2,1,0:T(8,128)S(1)} %get-tuple-element.34), channel_id=1, source_target_pairs={{0,24},{6,30},{12,36},{18,42},{24,0},{30,6},{36,12},{42,18},{48,72... | collective-permute-start | bytes 786440 | tf_op jit(solution)/shard_map/ppermute | solution.py:391
  37.5 4.0 %collective-permute-start.5 = (f32[32,16,128]{2,1,0:T(8,128)S(1)}, f32[32,16,128]{2,1,0:T(8,128)S(1)}, u32[]{:S(2)}, u32[]{:S(2)}) collective-permute-start(f32[32,16,128]{2,1,0:T(8,128)S(1)} %get-tuple-element.35), channel_id=1, source_target_pairs={{24,48},{30,54},{36,60},{42,66},{48,24},{54,30},{60,36},{66,42},{7... | collective-permute-start | bytes 786440 | tf_op jit(solution)/shard_map/ppermute | solution.py:391
  41.5 0.0 copy-done.3
  41.6 0.0 copy-done.10
  41.6 0.0 copy-done.11
  41.6 0.0 copy-done.1
  41.6 0.0 copy-start.6
  41.6 3.5 %shard_map.120 = (f32[1024,256]{1,0:T(8,128)S(1)}, f32[1024,256]{1,0:T(8,128)S(1)}) custom-call(f32[1024,256]{1,0:T(8,128)S(1)} %bitcast.14, f32[1024,256]{1,0:T(8,128)S(1)} %bitcast.18, bf16[3,128,256]{2,1,0:T(8,128)(2,1)S(1)} %copy-done.10, bf16[256,256]{1,0:T(8,128)(2,1)S(1)} %copy-done.11), custom_call_target="tpu_custom_call" | custom-call | flops 2147483648 | bytes 4849664 | tf_op jit(solution)/shard_map/pallas_call | solution.py:397
  45.1 0.0 copy-start.7
  45.8 0.0 copy-start.8
  45.8 0.0 copy-start.9
  45.8 0.0 copy-done.6
  45.8 0.0 copy-done.7
  45.8 0.6 copy-done.8
  46.5 0.0 copy-done.9
  46.5 5.1 %shard_map.121 = (f32[1024,256]{1,0:T(8,128)S(1)}, f32[1024,256]{1,0:T(8,128)S(1)}) custom-call(s32[1]{0:T(128)S(6)} %copy.13.shot_count, s32[1,16]{1,0:T(1,128)S(1)} %copy-done.9, f32[2,16]{1,0:T(2,128)S(1)} %bitcast.28, s32[1,1024]{1,0:T(1,128)S(1)} %copy-done.7, f32[2,1024]{1,0:T(2,128)S(1)} %bitcast.26, s32[8]{0:T(128)S(1)} %get-tuple-element.32.flags.after), custom_call_target="tpu_custom_call" | custom-call | flops 2147483648 | bytes 2109668 | tf_op jit(solution)/shard_map/pallas_call | solution.py:397
  51.6 0.0 collective-permute-done.6
  51.6 0.0 collective-permute-done.7
  51.6 0.0 collective-permute-done.4.diag_e
  51.6 0.0 collective-permute-done.5.diag_o
  51.6 0.0 copy-done.4
  51.6 3.2 %shard_map.123 = (f32[64,16,256]{2,1,0:T(8,128)S(1)}, f32[1024,256]{1,0:T(8,128)S(1)}, f32[1024,256]{1,0:T(8,128)S(1)}, f32[64,8,256]{2,1,0:T(8,128)S(1)}, f32[64,8,256]{2,1,0:T(8,128)S(1)}) custom-call(s32[8]{0:T(128)S(1)} %get-tuple-element.32.flags.after, f32[32,16,128]{2,1,0:T(8,128)} %bitcast.vel.own.tile, ...), custom_call_target="tpu_custom_call" | custom-call | flops 1073741824 | bytes 13467680 | tf_op jit(solution)/shard_map/pallas_call | solution.py:397
  54.8 6.3 %collective-permute-start.8 = (f32[64,8,256]{2,1,0:T(8,128)S(1)}, f32[64,8,256]{2,1,0:T(8,128)S(1)}, u32[]{:S(2)}, u32[]{:S(2)}) collective-permute-start(f32[64,8,256]{2,1,0:T(8,128)S(1)} %get-tuple-element.49), channel_id=1, source_target_pairs={{0,1},{1,2},{2,3},{3,4},{4,5},{6,7},{7,8},{8,9},{9,10},{10,11},{12... | collective-permute-start | bytes 1572872 | tf_op jit(solution)/shard_map/ppermute | solution.py:391
  61.2 1.9 %collective-permute-start.9 = (f32[64,8,256]{2,1,0:T(8,128)S(1)}, f32[64,8,256]{2,1,0:T(8,128)S(1)}, u32[]{:S(2)}, u32[]{:S(2)}) collective-permute-start(f32[64,8,256]{2,1,0:T(8,128)S(1)} %get-tuple-element.50), channel_id=1, source_target_pairs={{1,0},{2,1},{3,2},{4,3},{5,4},{7,6},{8,7},{9,8},{10,9},{11,10},{13... | collective-permute-start | bytes 1572872 | tf_op jit(solution)/shard_map/ppermute | solution.py:391
  63.1 5.1 %shard_map.125 = (f32[1024,256]{1,0:T(8,128)S(1)}, f32[1024,256]{1,0:T(8,128)S(1)}) custom-call(s32[1]{0:T(128)S(6)} %copy.13.shot_count, s32[1,16]{1,0:T(1,128)S(1)} %copy-done.9, f32[2,16]{1,0:T(2,128)S(1)} %bitcast.29, s32[1,1024]{1,0:T(1,128)S(1)} %copy-done.7, f32[2,1024]{1,0:T(2,128)S(1)} %bitcast.27, s32[8]{0:T(128)S(1)} %get-tuple-element.32.flags.after), custom_call_target="tpu_custom_call" | custom-call | flops 2147483648 | bytes 2109668 | tf_op jit(solution)/shard_map/pallas_call | solution.py:397
  68.2 3.5 %shard_map.124 = (f32[1024,256]{1,0:T(8,128)S(1)}, f32[1024,256]{1,0:T(8,128)S(1)}) custom-call(f32[1024,256]{1,0:T(8,128)S(1)} %get-tuple-element.43.fwd.mid_fwd, f32[1024,256]{1,0:T(8,128)S(1)} %get-tuple-element.44.adj.mid_adj, bf16[3,128,256]{2,1,0:T(8,128)(2,1)S(1)} %copy-done.10, bf16[256,256]{1,0:T(8,128)(2,1)S(1)} %copy-done.11), custom_call_target="tpu_custom_call" | custom-call | flops 2147483648 | bytes 4849664 | tf_op jit(solution)/shard_map/pallas_call | solution.py:397
  71.7 0.0 collective-permute-done.8
  71.7 0.6 collective-permute-done.9
  72.3 2.7 %shard_map.126 = (f32[32,16,128]{2,1,0:T(8,128)S(1)}, f32[32,16,128]{2,1,0:T(8,128)S(1)}, f32[32,16,128]{2,1,0:T(8,128)S(1)}, f32[32,16,128]{2,1,0:T(8,128)S(1)}) custom-call(s32[8]{0:T(128)S(1)} %get-tuple-element.32.flags.after, f32[1024,256]{1,0:T(8,128)S(1)} %bitcast.21, f32[1024,256]{1,0:T(8,128)S(1)} %get-tuple-element.45.lap_fwd, ...), custom_call_target="tpu_custom_call" | custom-call | flops 1073741824 | bytes 11599904 | tf_op jit(solution)/shard_map/pallas_call | solution.py:397
  75.0 2.3 %collective-permute-start.12 = (f32[32,16,128]{2,1,0:T(8,128)S(1)}, f32[32,16,128]{2,1,0:T(8,128)S(1)}, u32[]{:S(2)}, u32[]{:S(2)}) collective-permute-start(f32[32,16,128]{2,1,0:T(8,128)S(1)} %get-tuple-element.56), channel_id=1, source_target_pairs={{0,24},{6,30},{12,36},{18,42},{24,0},{30,6},{36,12},{42,18},{48,72... | collective-permute-start | bytes 786440 | tf_op jit(solution)/shard_map/ppermute | solution.py:391
  77.3 2.9 %collective-permute-start.13 = (f32[32,16,128]{2,1,0:T(8,128)S(1)}, f32[32,16,128]{2,1,0:T(8,128)S(1)}, u32[]{:S(2)}, u32[]{:S(2)}) collective-permute-start(f32[32,16,128]{2,1,0:T(8,128)S(1)} %get-tuple-element.56), channel_id=1, source_target_pairs={{24,48},{30,54},{36,60},{42,66},{48,24},{54,30},{60,36},{66,42},{7... | collective-permute-start | bytes 786440 | tf_op jit(solution)/shard_map/ppermute | solution.py:391
  80.3 1.9 %collective-permute-start.10 = (f32[32,16,128]{2,1,0:T(8,128)S(1)}, f32[32,16,128]{2,1,0:T(8,128)S(1)}, u32[]{:S(2)}, u32[]{:S(2)}) collective-permute-start(f32[32,16,128]{2,1,0:T(8,128)S(1)} %get-tuple-element.52), channel_id=1, source_target_pairs={{0,24},{6,30},{12,36},{18,42},{24,0},{30,6},{36,12},{42,18},{48,72... | collective-permute-start | bytes 786440 | tf_op jit(solution)/shard_map/ppermute | solution.py:391
  82.2 4.4 %collective-permute-start.11 = (f32[32,16,128]{2,1,0:T(8,128)S(1)}, f32[32,16,128]{2,1,0:T(8,128)S(1)}, u32[]{:S(2)}, u32[]{:S(2)}) collective-permute-start(f32[32,16,128]{2,1,0:T(8,128)S(1)} %get-tuple-element.52), channel_id=1, source_target_pairs={{24,48},{30,54},{36,60},{42,66},{48,24},{54,30},{60,36},{66,42},{7... | collective-permute-start | bytes 786440 | tf_op jit(solution)/shard_map/ppermute | solution.py:391
  86.6 0.0 collective-permute-done.12.back_e
  86.7 0.0 collective-permute-done.13.back_o
  86.7 0.7 shard_map.127
  87.3 1.9 %collective-permute-start.14 = (f32[32,16,128]{2,1,0:T(8,128)S(1)}, f32[32,16,128]{2,1,0:T(8,128)S(1)}, u32[]{:S(2)}, u32[]{:S(2)}) collective-permute-start(f32[32,16,128]{2,1,0:T(8,128)S(1)} %get-tuple-element.57), channel_id=1, source_target_pairs={{0,6},{6,0},{12,18},{18,12},{24,30},{30,24},{36,42},{42,36},{48,54... | collective-permute-start | bytes 786440 | tf_op jit(solution)/shard_map/ppermute | solution.py:391
  89.3 11.6 %collective-permute-start.15 = (f32[32,16,128]{2,1,0:T(8,128)S(1)}, f32[32,16,128]{2,1,0:T(8,128)S(1)}, u32[]{:S(2)}, u32[]{:S(2)}) collective-permute-start(f32[32,16,128]{2,1,0:T(8,128)S(1)} %get-tuple-element.58), channel_id=1, source_target_pairs={{6,12},{12,6},{30,36},{36,30},{54,60},{60,54},{78,84},{84,78},{102... | collective-permute-start | bytes 786440 | tf_op jit(solution)/shard_map/ppermute | solution.py:391
  100.9 0.0 collective-permute-done.10.same_e
  100.9 0.0 collective-permute-done.11.same_o
  100.9 0.0 collective-permute-done.14.sum_a
  100.9 9.6 %collective-permute-done.15.sum_b = f32[32,16,128]{2,1,0:T(8,128)S(1)} collective-permute-done((f32[32,16,128]{2,1,0:T(8,128)S(1)}, f32[32,16,128]{2,1,0:T(8,128)S(1)}, u32[]{:S(2)}, u32[]{:S(2)}) %collective-permute-start.15) | collective-permute-done | bytes 262176 | tf_op jit(solution)/shard_map/ppermute | solution.py:391
  110.5 1.8 %shard_map.128 = f32[32,16,128]{2,1,0:T(8,128)} custom-call(s32[8]{0:T(128)S(1)} %get-tuple-element.32.flags.after, f32[32,16,128]{2,1,0:T(8,128)} %bitcast.vel.own.tile, f32[32,16,128]{2,1,0:T(8,128)S(1)} %get-tuple-element.51.own, f32[32,16,128]{2,1,0:T(8,128)S(1)} %collective-permute-done.10.same_e, f32[32,16,128]{2,1,0:T(8,128)S(1)} %collective-permute-done.11.same_o, ...), custom_call_target="tpu_custom_call" | custom-call | flops 1048576 | bytes 1867808 | tf_op jit(solution)/shard_map/pallas_call | solution.py:397
  (3 shorter events, 0.0 us)
Async XLA Ops:
  0.0 2.7 %copy-start.5 = (s32[1,2]{1,0:T(1,128)S(1)}, s32[1,2]{1,0:T(1,128)}, u32[]{:S(2)}) copy-start(s32[1,2]{1,0:T(1,128)} %anchor.1) | copy-start | bytes 28
  0.0 31.5 %collective-permute-start = (f32[32,16,128]{2,1,0:T(8,128)}, f32[32,16,128]{2,1,0:T(8,128)S(1)}, u32[]{:S(2)}, u32[]{:S(2)}) collective-permute-start(f32[32,16,128]{2,1,0:T(8,128)} %bitcast.vel.own.tile), channel_id=1, source_target_pairs={{0,6},{6,0},{12,18},{18,12},{24,30},{30,24},{36,42},{42,36},{48,54... | collective-permute-start | bytes 786440 | tf_op jit(solution)/shard_map/ppermute | solution.py:391
  4.3 30.6 %collective-permute-start.2 = (f32[34,16,128]{2,1,0:T(8,128)S(1)}, f32[34,16,128]{2,1,0:T(8,128)S(1)}, u32[]{:S(2)}, u32[]{:S(2)}) collective-permute-start(f32[34,16,128]{2,1,0:T(8,128)S(1)} %get-tuple-element.33), channel_id=1, source_target_pairs={{0,24},{6,30},{12,36},{18,42},{24,0},{30,6},{36,12},{42,18},{48,72... | collective-permute-start | bytes 835592 | tf_op jit(solution)/shard_map/ppermute | solution.py:391
  7.5 27.4 %collective-permute-start.3 = (f32[34,16,128]{2,1,0:T(8,128)S(1)}, f32[34,16,128]{2,1,0:T(8,128)S(1)}, u32[]{:S(2)}, u32[]{:S(2)}) collective-permute-start(f32[34,16,128]{2,1,0:T(8,128)S(1)} %get-tuple-element.33), channel_id=1, source_target_pairs={{24,48},{30,54},{36,60},{42,66},{48,24},{54,30},{60,36},{66,42},{7... | collective-permute-start | bytes 835592 | tf_op jit(solution)/shard_map/ppermute | solution.py:391
  12.4 22.6 %collective-permute-start.1 = (f32[32,16,128]{2,1,0:T(8,128)}, f32[32,16,128]{2,1,0:T(8,128)S(1)}, u32[]{:S(2)}, u32[]{:S(2)}) collective-permute-start(f32[32,16,128]{2,1,0:T(8,128)} %bitcast.vel.own.tile), channel_id=1, source_target_pairs={{6,12},{12,6},{30,36},{36,30},{54,60},{60,54},{78,84},{84,78},{102... | collective-permute-start | bytes 786440 | tf_op jit(solution)/shard_map/ppermute | solution.py:391
  25.0 1.2 %copy-start = (f32[1,64,16,256]{3,2,1,0:T(8,128)S(1)}, f32[1,64,16,256]{3,2,1,0:T(8,128)}, u32[]{:S(2)}) copy-start(f32[1,64,16,256]{3,2,1,0:T(8,128)} %param.13) | copy-start | bytes 3145732
  26.3 1.2 %copy-start.2 = (f32[1,64,16,256]{3,2,1,0:T(8,128)S(1)}, f32[1,64,16,256]{3,2,1,0:T(8,128)}, u32[]{:S(2)}) copy-start(f32[1,64,16,256]{3,2,1,0:T(8,128)} %param.14) | copy-start | bytes 3145732
  27.5 14.1 %copy-start.3 = (f32[1,64,16,256]{3,2,1,0:T(8,128)S(1)}, f32[1,64,16,256]{3,2,1,0:T(8,128)}, u32[]{:S(2)}) copy-start(f32[1,64,16,256]{3,2,1,0:T(8,128)} %param.14) | copy-start | bytes 3145732
  27.5 14.1 %copy-start.10 = (bf16[3,128,256]{2,1,0:T(8,128)(2,1)S(1)}, bf16[3,128,256]{2,1,0:T(8,128)(2,1)}, u32[]{:S(2)}) copy-start(bf16[3,128,256]{2,1,0:T(8,128)(2,1)} %constant.6.clone.xz) | copy-start | bytes 589828
  27.5 14.1 %copy-start.11 = (bf16[256,256]{1,0:T(8,128)(2,1)S(1)}, bf16[256,256]{1,0:T(8,128)(2,1)}, u32[]{:S(2)}) copy-start(bf16[256,256]{1,0:T(8,128)(2,1)} %constant.7.clone.y) | copy-start | bytes 393220
  27.6 13.9 %copy-start.1 = (f32[1,64,16,256]{3,2,1,0:T(8,128)S(1)}, f32[1,64,16,256]{3,2,1,0:T(8,128)}, u32[]{:S(2)}) copy-start(f32[1,64,16,256]{3,2,1,0:T(8,128)} %param.13) | copy-start | bytes 3145732
  27.6 23.9 %collective-permute-start.6 = (f32[64,8,256]{2,1,0:T(8,128)S(1)}, f32[64,8,256]{2,1,0:T(8,128)S(1)}, u32[]{:S(2)}, u32[]{:S(2)}) collective-permute-start(f32[64,8,256]{2,1,0:T(8,128)S(1)} %get-tuple-element.40), channel_id=1, source_target_pairs={{0,1},{1,2},{2,3},{3,4},{4,5},{6,7},{7,8},{8,9},{9,10},{10,11},{12... | collective-permute-start | bytes 1572872 | tf_op jit(solution)/shard_map/ppermute | solution.py:391
  31.5 20.1 %collective-permute-start.7 = (f32[64,8,256]{2,1,0:T(8,128)S(1)}, f32[64,8,256]{2,1,0:T(8,128)S(1)}, u32[]{:S(2)}, u32[]{:S(2)}) collective-permute-start(f32[64,8,256]{2,1,0:T(8,128)S(1)} %get-tuple-element.41), channel_id=1, source_target_pairs={{1,0},{2,1},{3,2},{4,3},{5,4},{7,6},{8,7},{9,8},{10,9},{11,10},{13... | collective-permute-start | bytes 1572872 | tf_op jit(solution)/shard_map/ppermute | solution.py:391
  35.6 16.0 %collective-permute-start.4 = (f32[32,16,128]{2,1,0:T(8,128)S(1)}, f32[32,16,128]{2,1,0:T(8,128)S(1)}, u32[]{:S(2)}, u32[]{:S(2)}) collective-permute-start(f32[32,16,128]{2,1,0:T(8,128)S(1)} %get-tuple-element.34), channel_id=1, source_target_pairs={{0,24},{6,30},{12,36},{18,42},{24,0},{30,6},{36,12},{42,18},{48,72... | collective-permute-start | bytes 786440 | tf_op jit(solution)/shard_map/ppermute | solution.py:391
  37.5 14.1 %collective-permute-start.5 = (f32[32,16,128]{2,1,0:T(8,128)S(1)}, f32[32,16,128]{2,1,0:T(8,128)S(1)}, u32[]{:S(2)}, u32[]{:S(2)}) collective-permute-start(f32[32,16,128]{2,1,0:T(8,128)S(1)} %get-tuple-element.35), channel_id=1, source_target_pairs={{24,48},{30,54},{36,60},{42,66},{48,24},{54,30},{60,36},{66,42},{7... | collective-permute-start | bytes 786440 | tf_op jit(solution)/shard_map/ppermute | solution.py:391
  41.6 4.2 %copy-start.6 = (f32[1,2,1024]{2,1,0:T(2,128)S(1)}, f32[1,2,1024]{2,1,0:T(2,128)}, u32[]{:S(2)}) copy-start(f32[1,2,1024]{2,1,0:T(2,128)} %param.20) | copy-start | bytes 24580
  45.1 0.7 copy-start.7
  45.8 0.7 copy-start.8
  45.8 0.7 copy-start.9
  46.5 5.1 %copy-start.4 = (bf16[128,128]{1,0:T(8,128)(2,1)S(1)}, bf16[128,128]{1,0:T(8,128)(2,1)}, u32[]{:S(2)}) copy-start(bf16[128,128]{1,0:T(8,128)(2,1)} %constant.8.clone.halo) | copy-start | bytes 98308
  54.8 16.9 %collective-permute-start.8 = (f32[64,8,256]{2,1,0:T(8,128)S(1)}, f32[64,8,256]{2,1,0:T(8,128)S(1)}, u32[]{:S(2)}, u32[]{:S(2)}) collective-permute-start(f32[64,8,256]{2,1,0:T(8,128)S(1)} %get-tuple-element.49), channel_id=1, source_target_pairs={{0,1},{1,2},{2,3},{3,4},{4,5},{6,7},{7,8},{8,9},{9,10},{10,11},{12... | collective-permute-start | bytes 1572872 | tf_op jit(solution)/shard_map/ppermute | solution.py:391
  61.2 11.1 %collective-permute-start.9 = (f32[64,8,256]{2,1,0:T(8,128)S(1)}, f32[64,8,256]{2,1,0:T(8,128)S(1)}, u32[]{:S(2)}, u32[]{:S(2)}) collective-permute-start(f32[64,8,256]{2,1,0:T(8,128)S(1)} %get-tuple-element.50), channel_id=1, source_target_pairs={{1,0},{2,1},{3,2},{4,3},{5,4},{7,6},{8,7},{9,8},{10,9},{11,10},{13... | collective-permute-start | bytes 1572872 | tf_op jit(solution)/shard_map/ppermute | solution.py:391
  75.0 11.7 %collective-permute-start.12 = (f32[32,16,128]{2,1,0:T(8,128)S(1)}, f32[32,16,128]{2,1,0:T(8,128)S(1)}, u32[]{:S(2)}, u32[]{:S(2)}) collective-permute-start(f32[32,16,128]{2,1,0:T(8,128)S(1)} %get-tuple-element.56), channel_id=1, source_target_pairs={{0,24},{6,30},{12,36},{18,42},{24,0},{30,6},{36,12},{42,18},{48,72... | collective-permute-start | bytes 786440 | tf_op jit(solution)/shard_map/ppermute | solution.py:391
  77.3 9.3 %collective-permute-start.13 = (f32[32,16,128]{2,1,0:T(8,128)S(1)}, f32[32,16,128]{2,1,0:T(8,128)S(1)}, u32[]{:S(2)}, u32[]{:S(2)}) collective-permute-start(f32[32,16,128]{2,1,0:T(8,128)S(1)} %get-tuple-element.56), channel_id=1, source_target_pairs={{24,48},{30,54},{36,60},{42,66},{48,24},{54,30},{60,36},{66,42},{7... | collective-permute-start | bytes 786440 | tf_op jit(solution)/shard_map/ppermute | solution.py:391
  80.3 20.6 %collective-permute-start.10 = (f32[32,16,128]{2,1,0:T(8,128)S(1)}, f32[32,16,128]{2,1,0:T(8,128)S(1)}, u32[]{:S(2)}, u32[]{:S(2)}) collective-permute-start(f32[32,16,128]{2,1,0:T(8,128)S(1)} %get-tuple-element.52), channel_id=1, source_target_pairs={{0,24},{6,30},{12,36},{18,42},{24,0},{30,6},{36,12},{42,18},{48,72... | collective-permute-start | bytes 786440 | tf_op jit(solution)/shard_map/ppermute | solution.py:391
  82.2 18.7 %collective-permute-start.11 = (f32[32,16,128]{2,1,0:T(8,128)S(1)}, f32[32,16,128]{2,1,0:T(8,128)S(1)}, u32[]{:S(2)}, u32[]{:S(2)}) collective-permute-start(f32[32,16,128]{2,1,0:T(8,128)S(1)} %get-tuple-element.52), channel_id=1, source_target_pairs={{24,48},{30,54},{36,60},{42,66},{48,24},{54,30},{60,36},{66,42},{7... | collective-permute-start | bytes 786440 | tf_op jit(solution)/shard_map/ppermute | solution.py:391
  87.3 13.6 %collective-permute-start.14 = (f32[32,16,128]{2,1,0:T(8,128)S(1)}, f32[32,16,128]{2,1,0:T(8,128)S(1)}, u32[]{:S(2)}, u32[]{:S(2)}) collective-permute-start(f32[32,16,128]{2,1,0:T(8,128)S(1)} %get-tuple-element.57), channel_id=1, source_target_pairs={{0,6},{6,0},{12,18},{18,12},{24,30},{30,24},{36,42},{42,36},{48,54... | collective-permute-start | bytes 786440 | tf_op jit(solution)/shard_map/ppermute | solution.py:391
  89.3 21.3 %collective-permute-start.15 = (f32[32,16,128]{2,1,0:T(8,128)S(1)}, f32[32,16,128]{2,1,0:T(8,128)S(1)}, u32[]{:S(2)}, u32[]{:S(2)}) collective-permute-start(f32[32,16,128]{2,1,0:T(8,128)S(1)} %get-tuple-element.58), channel_id=1, source_target_pairs={{6,12},{12,6},{30,36},{36,30},{54,60},{60,54},{78,84},{84,78},{102... | collective-permute-start | bytes 786440 | tf_op jit(solution)/shard_map/ppermute | solution.py:391

commit v2 on v1

--- a/solution.py
+++ b/solution.py
@@ -22,11 +22,14 @@
 AX = 64
 ROWS = BX * Z
 BLOCKS = AX // BX
+HOT = 512
 FLAT = AX * Z
 F32 = jnp.float32
 BF16 = jnp.bfloat16
 VMEM = pl.BlockSpec(memory_space=pltpu.VMEM)
 SMEM = pl.BlockSpec(memory_space=pltpu.SMEM)
+HBM = pl.BlockSpec(memory_space=pltpu.HBM)
+PIECES = 4
 
 
 def weight(distance):
@@ -73,11 +76,6 @@
     return jnp.dot(a, b, preferred_element_type=F32)
 
 
-def split(value):
-    high = value.astype(BF16)
-    return high, (value - high.astype(F32)).astype(BF16)
-
-
 def split3(value):
     high = value.astype(BF16)
     rest = value - high.astype(F32)
@@ -96,7 +94,18 @@
     return top, bottom
 
 
-def tag_kernel(anchor, vel, tagged, flags):
+def load_kernel(anchor, vel_hbm, fwd_hbm, adj_hbm, tagged, fwd, adj, up, down, flags, sems):
+    rows = vel_hbm.shape[0]
+    tile_copy = pltpu.make_async_copy(vel_hbm, tagged.at[pl.ds(0, rows)], sems.at[2 * PIECES])
+    size = AX // PIECES
+    copies = []
+    for n, (source, target) in enumerate(((fwd_hbm, fwd), (adj_hbm, adj))):
+        for i in range(PIECES):
+            at = pl.ds(i * size, size)
+            copies.append(pltpu.make_async_copy(source.at[at], target.at[at], sems.at[n * PIECES + i]))
+    for copy in copies:
+        copy.start()
+    tile_copy.start()
     device = lax.axis_index("shot")
     home_row = device // TILES_Y
     home_col = device - home_row * TILES_Y
@@ -112,25 +121,19 @@
     flags[3] = jnp.where(side_col == toward_a, 1, 0)
     flags[4] = toward_e
     flags[5] = toward_a
-    rows = vel.shape[0]
     tagged[rows] = jnp.full(tagged.shape[1:], side_row.astype(F32))
     tagged[rows + 1] = jnp.full(tagged.shape[1:], side_col.astype(F32))
 
-    def copy(i, _):
-        at = pl.ds(i * 8, 8)
-        tagged[at] = vel[at]
-        return 0
-
-    lax.fori_loop(0, rows // 8, copy, 0)
-
-
-def rims_kernel(fwd, adj, up, down):
+    for copy in copies:
+        copy.wait()
+
     def step(b, _):
         at = pl.ds(b * BX, BX)
         up[at], down[at] = rims(fwd[at], adj[at])
         return 0
 
     lax.fori_loop(0, BLOCKS, step, 0)
+    tile_copy.wait()
 
 
 def inner_laplace(b, parts, xz, y):
@@ -166,43 +169,55 @@
     table[3:4, 0:count] = amounts[1]
 
 
-def columns_of(points, n, columns):
+def ones_of(points, ones):
     def step(i, _):
         at = pl.ds(pl.multiple_of(i * 128, 128), 128)
-        part = points[:, at].T
-        here = lax.broadcasted_iota(jnp.int32, (128, Y), 1) == part[:, 1:2].astype(jnp.int32)
-        high, low = split(part[:, 2 + n : 3 + n])
-        columns[at, :Y] = jnp.where(here, high.astype(F32), 0.0).astype(BF16)
-        columns[at, Y:] = jnp.where(here, low.astype(F32), 0.0).astype(BF16)
+        place = jnp.broadcast_to(points[1:2, at], (8, 128)).T[:, 0:1].astype(jnp.int32)
+        here = lax.broadcasted_iota(jnp.int32, (128, Y), 1) == place
+        ones[at] = jnp.where(here, 1.0, 0.0).astype(BF16)
         return 0
 
     lax.fori_loop(0, points.shape[1] // 128, step, 0)
 
 
-def injected(b, points, columns):
-    rows = lax.broadcasted_iota(jnp.int32, (ROWS, points.shape[1]), 0) + b * ROWS
-    hot = jnp.where(rows == points[0:1, :].astype(jnp.int32), 1.0, 0.0).astype(BF16)
-    both = dot(hot, columns[...])
-    return both[:, :Y] + both[:, Y:]
-
-
-def inject_kernel(total_depth, n, shot_count, source_cell, wavelet, receiver_cell, residual, after, fwd_in, adj_in,
-                  shots, receivers, shot_columns, receiver_columns):
+def hot_rows(b, points, n, hot):
+    count = points.shape[1]
+    amount = points[2 + n : 3 + n, :]
+    part = amount.astype(BF16).astype(F32)
+    rest = (amount - part).astype(BF16).astype(F32)
+    rows = points[0:1, :].astype(jnp.int32)
+    for i in range(HOT // 128):
+        hit = lax.broadcasted_iota(jnp.int32, (128, count), 0) + (b * HOT + i * 128) == rows
+        hot[pl.ds(i * 128, 128)] = jnp.where(hit, part, 0.0).astype(BF16)
+        hot[pl.ds(HOT + i * 128, 128)] = jnp.where(hit, rest, 0.0).astype(BF16)
+
+
+def inject_all(n, shots, receivers, shot_ones, receiver_ones, fwd_in, adj_in, shot_hot, hot):
+    def step(b, _):
+        at = pl.ds(pl.multiple_of(b * HOT, HOT), HOT)
+        for points, ones, rows, field in ((shots, shot_ones, shot_hot, fwd_in), (receivers, receiver_ones, hot, adj_in)):
+            hot_rows(b, points, n, rows)
+            both = dot(rows[...], ones[...])
+            field[at] = both[:HOT] + both[HOT:]
+        return 0
+
+    lax.fori_loop(0, FLAT // HOT, step, 0)
+
+
+def inject_kernel(total_depth, shot_count, source_cell, wavelet, receiver_cell, residual,
+                  fwd_in, adj_in, shots, receivers, shot_ones, receiver_ones, *hot):
     first_layer = lax.axis_index("slab") * Z
     active = lax.broadcasted_iota(jnp.int32, source_cell.shape, 1) < shot_count[0]
     waves = [jnp.where(active, wavelet[i : i + 1, :], 0.0) for i in range(2)]
     table_of(source_cell[...], waves, first_layer, total_depth, shots)
     table_of(receiver_cell[...], [residual[1:2, :], residual[0:1, :]], first_layer, total_depth, receivers)
-    columns_of(shots, n, shot_columns)
-    columns_of(receivers, n, receiver_columns)
-
-    def step(b, _):
-        at = pl.ds(pl.multiple_of(b * ROWS, ROWS), ROWS)
-        fwd_in[at] = injected(b, shots, shot_columns)
-        adj_in[at] = injected(b, receivers, receiver_columns)
-        return 0
-
-    lax.fori_loop(0, BLOCKS, step, 0)
+    ones_of(shots, shot_ones)
+    ones_of(receivers, receiver_ones)
+    inject_all(0, shots, receivers, shot_ones, receiver_ones, fwd_in, adj_in, *hot)
+
+
+def inject_again_kernel(shots, receivers, shot_ones, receiver_ones, fwd_in, adj_in, *hot):
+    inject_all(1, shots, receivers, shot_ones, receiver_ones, fwd_in, adj_in, *hot)
 
 
 def laplace_kernel(fwd, adj, xz, y, lap_fwd, lap_adj, f0, f1, f2, a0, a1, a2):
@@ -218,21 +233,24 @@
     lax.fori_loop(0, BLOCKS, step, 0)
 
 
-def halo_part(b, below, above, halo):
+def halo_part(b, below, above, halo, both):
     at = pl.ds(pl.multiple_of(b * (ROWS // 2), ROWS // 2), ROWS // 2)
     high, middle, low = split3(jnp.concatenate([below[at], above[at]], 0))
-    both = dot(halo[...], low) + dot(halo[...], middle) + dot(halo[...], high)
-    front = lax.broadcasted_iota(jnp.int32, (BX, 8, Y), 1) < 4
+    both[...] = dot(halo[...], low) + dot(halo[...], middle) + dot(halo[...], high)
+
+
+def halo_of(i, both):
+    front = lax.broadcasted_iota(jnp.int32, (8, Y), 0) < 4
     fields = []
-    for part in (both[: ROWS // 2], both[ROWS // 2 :]):
-        part = part.reshape(BX, 8, Y)
-        fields.append(jnp.concatenate([jnp.where(front, part, 0.0), jnp.where(front, 0.0, part)], 1).reshape(ROWS, Y))
+    for field in (0, 1):
+        part = both[pl.ds(field * (ROWS // 2) + i * 8, 8)]
+        fields.append(jnp.concatenate([jnp.where(front, part, 0.0), jnp.where(front, 0.0, part)], 0))
     return fields
 
 
 def advance_kernel(flags, own, col_a, col_b, row_e, row_o, diag_e, diag_o, lap_fwd, lap_adj, fwd, adj, fwd_in, adj_in,
-                   below, above, halo, speed2, mid_fwd, mid_adj, up, down):
-    half = own.shape[0]
+                   below, above, halo, speed2, mid_fwd, mid_adj, up, down, both):
+    half = col_a.shape[0]
     wide = own.shape[2]
     with_e = flags[2] == 1
     with_a = flags[3] == 1
@@ -258,32 +276,38 @@
     lax.fori_loop(0, half // 8, assemble, 0)
 
     def step(b, _):
-        at = pl.ds(pl.multiple_of(b * ROWS, ROWS), ROWS)
-        blk = pl.ds(b * BX, BX)
-        halo_fwd, halo_adj = halo_part(b, below, above, halo)
-        c = speed2[blk].reshape(ROWS, Y)
-        new_fwd = fwd[at] + (c * (lap_fwd[at] + halo_fwd) + fwd_in[at])
-        new_adj = adj[at] + (c * (lap_adj[at] + halo_adj) + adj_in[at])
-        mid_fwd[at] = new_fwd
-        mid_adj[at] = new_adj
-        up[blk], down[blk] = rims(new_fwd.reshape(BX, Z, Y), new_adj.reshape(BX, Z, Y))
+        halo_part(b, below, above, halo, both)
+        front = lax.broadcasted_iota(jnp.int32, (8, Y), 0) < 4
+        for i in range(BX):
+            x = b * BX + i
+            at = pl.ds(pl.multiple_of(x * Z, Z), Z)
+            halo_fwd, halo_adj = halo_of(i, both)
+            c = speed2[x]
+            new_fwd = fwd[at] + (c * (lap_fwd[at] + halo_fwd) + fwd_in[at])
+            new_adj = adj[at] + (c * (lap_adj[at] + halo_adj) + adj_in[at])
+            mid_fwd[at] = new_fwd
+            mid_adj[at] = new_adj
+            up[x] = jnp.where(front, pltpu.roll(new_fwd[8:], 4, 0), new_adj[8:])
+            down[x] = jnp.where(front, new_fwd[:8], pltpu.roll(new_adj[:8], 4, 0))
         return 0
 
     lax.fori_loop(0, BLOCKS, step, 0)
 
 
 def image_kernel(flags, speed2, lap_fwd, lap_adj, fwd, adj, mid_fwd, mid_adj, fwd_in, adj_in, below, above, halo,
-                 own, col, row, diag, image):
+                 own, col, row, diag, image, both):
     def step(b, _):
-        at = pl.ds(pl.multiple_of(b * ROWS, ROWS), ROWS)
-        halo_fwd, halo_adj = halo_part(b, below, above, halo)
-        c = speed2[at]
-        second_fwd = c * (lap_fwd[at] + halo_fwd) + fwd_in[at]
-        second_adj = c * (lap_adj[at] + halo_adj) + adj_in[at]
-        later = mid_adj[at]
-        earlier = 2.0 * later - adj[at] + second_adj
-        imaged = earlier * (mid_fwd[at] - fwd[at]) + later * second_fwd
-        image[pl.ds(b * BX, BX)] = imaged.reshape(BX, Z, Y)
+        halo_part(b, below, above, halo, both)
+        for i in range(BX):
+            x = b * BX + i
+            at = pl.ds(pl.multiple_of(x * Z, Z), Z)
+            halo_fwd, halo_adj = halo_of(i, both)
+            c = speed2[at]
+            second_fwd = c * (lap_fwd[at] + halo_fwd) + fwd_in[at]
+            second_adj = c * (lap_adj[at] + halo_adj) + adj_in[at]
+            later = mid_adj[at]
+            earlier = 2.0 * later - adj[at] + second_adj
+            image[x] = earlier * (mid_fwd[at] - fwd[at]) + later * second_fwd
         return 0
 
     lax.fori_loop(0, BLOCKS, step, 0)
@@ -362,7 +386,7 @@
     lax.fori_loop(0, col.shape[0] // 8, step, 0)
 
 
-def final_kernel(flags, tile, own, same_e, same_o, tag_e, tag_o, sum_a, sum_b, out):
+def near_kernel(flags, tile, own, same_e, same_o, tag_e, tag_o, sum_a, near, twice):
     toward_e = flags[4].astype(F32)
     from_e = tag_e[0] == -toward_e
     from_o = tag_o[0] == toward_e
@@ -370,10 +394,12 @@
     def step(i, _):
         at = pl.ds(i * 8, 8)
         total = own[at] + jnp.where(from_e[None], same_e[at], 0.0) + jnp.where(from_o[None], same_o[at], 0.0)
-        out[at] = 2.0 * tile[at] * (total + sum_a[at] + sum_b[at])
-        return 0
-
-    lax.fori_loop(0, tile.shape[0] // 8, step, 0)
+        double = 2.0 * tile[at]
+        twice[at] = double
+        near[at] = double * (total + sum_a[at])
+        return 0
+
+    lax.fori_loop(0, own.shape[0] // 8, step, 0)
 
 
 def steps(velocity, fwd_field, adj_field, aperture_anchor, source_cell, wavelet, shot_count, receiver_cell, residual):
@@ -391,7 +417,7 @@
         return lax.ppermute(value, axis, pairs)
 
     def kernel(function, ins, outs, args, flops, mib=8, scratch=()):
-        places = [SMEM if i == "s" else VMEM for i in ins]
+        places = [{"s": SMEM, "h": HBM, "v": VMEM}[i] for i in ins]
         sent = tuple(SMEM if o.dtype == jnp.int32 else VMEM for o in outs)
         nbytes = sum(int(np.prod(a.shape)) * 4 for a in tuple(args) + tuple(outs))
         return pl.pallas_call(
@@ -408,31 +434,31 @@
     rim_shape = shape(AX, 8, Y)
     flat = shape(FLAT, Y)
     parts = [pltpu.VMEM((FLAT, Y), BF16)] * 6
+    both = [pltpu.VMEM((ROWS, Y), F32)]
     inner = (exact(along_xz()), exact(along_y()))
     rim = (exact(along_halo()),)
 
     col_b = send(pair_b, tile)
     col_a = send(pair_a, tile)
-    fwd = fwd_field[0]
-    adj = adj_field[0]
+    field = shape(AX, depth, Y)
+    tagged, fwd, adj, up, down, flags = kernel(
+        load_kernel, "shhh",
+        (shape(half + 2, depth, wide), field, field, rim_shape, rim_shape, shape(8, dtype=jnp.int32)),
+        (aperture_anchor, tile, fwd_field[0], adj_field[0]), 1 << 20, 50, [pltpu.SemaphoreType.DMA((2 * PIECES + 1,))])
     flat_fwd = fwd.reshape(FLAT, Y)
     flat_adj = adj.reshape(FLAT, Y)
-    tagged, flags = kernel(
-        tag_kernel, "sv", (shape(half + 2, depth, wide), shape(8, dtype=jnp.int32)), (aperture_anchor, tile), 1 << 20)
     row_e = send(pair_e, tagged)
     row_o = send(pair_o, tagged)
-    up, down = kernel(rims_kernel, "vv", (rim_shape, rim_shape), (fwd, adj), 1 << 20)
     below = send(to_up, up, "slab")
     above = send(to_down, down, "slab")
     recv = receiver_cell.shape[1]
 
-    def inject(n, after):
-        return kernel(
-            functools.partial(inject_kernel, depth * slabs, n), "svvvvs", (flat,) * 2,
-            (shot_count, source_cell, wavelet[0], receiver_cell, residual[0], after), 2 << 30, 12,
-            [pltpu.VMEM((8, 128), F32), pltpu.VMEM((8, recv), F32), pltpu.VMEM((128, 2 * Y), BF16), pltpu.VMEM((recv, 2 * Y), BF16)])
-
-    fwd_in1, adj_in1 = inject(0, flags)
+    hot = [pltpu.VMEM((2 * HOT, n), BF16) for n in (128, recv)]
+    ones = (shape(128, Y, dtype=BF16), shape(recv, Y, dtype=BF16))
+    fwd_in1, adj_in1, *points = kernel(
+        functools.partial(inject_kernel, depth * slabs), "svvvv",
+        (flat, flat, shape(8, 128), shape(8, recv)) + ones,
+        (shot_count, source_cell, wavelet[0], receiver_cell, residual[0]), 2 << 30, 12, hot)
     diag_e, diag_o, tag_e, tag_o = kernel(
         select_kernel, "svvvv", (piece, piece, shape(2, depth, wide), shape(2, depth, wide)),
         (flags, col_a, col_b, row_e, row_o), 1 << 20)
@@ -442,16 +468,16 @@
         laplace_kernel, "vvvv", (flat,) * 2, (flat_fwd, flat_adj) + inner, 2 << 30, 8, parts)
     speed2, mid_fwd, mid_adj, up, down = kernel(
         advance_kernel, "s" + "v" * 16, (shape(AX, depth, Y), flat, flat, rim_shape, rim_shape),
-        (flags, tile, col_a, col_b, row_e, row_o, diag_e, diag_o, lap_fwd, lap_adj, flat_fwd, flat_adj, fwd_in1, adj_in1,
-         below.reshape(AX * 8, Y), above.reshape(AX * 8, Y)) + rim, 1 << 30)
+        (flags, tagged, col_a, col_b, row_e, row_o, diag_e, diag_o, lap_fwd, lap_adj, flat_fwd, flat_adj, fwd_in1, adj_in1,
+         below.reshape(AX * 8, Y), above.reshape(AX * 8, Y)) + rim, 1 << 30, 8, both)
     below = send(to_up, up, "slab")
     above = send(to_down, down, "slab")
     lap_fwd, lap_adj = kernel(laplace_kernel, "vvvv", (flat,) * 2, (mid_fwd, mid_adj) + inner, 2 << 30, 8, parts)
-    fwd_in2, adj_in2 = inject(1, flags)
+    fwd_in2, adj_in2 = kernel(inject_again_kernel, "vvvv", (flat, flat), tuple(points), 2 << 30, 12, hot)
     own, col, row, diag = kernel(
         image_kernel, "s" + "v" * 12, (piece,) * 4,
         (flags, speed2.reshape(FLAT, Y), lap_fwd, lap_adj, flat_fwd, flat_adj, mid_fwd, mid_adj, fwd_in2, adj_in2,
-         below.reshape(AX * 8, Y), above.reshape(AX * 8, Y)) + rim, 1 << 30, 8, [pltpu.VMEM((AX, depth, Y), F32)])
+         below.reshape(AX * 8, Y), above.reshape(AX * 8, Y)) + rim, 1 << 30, 8, [pltpu.VMEM((AX, depth, Y), F32)] + both)
     back_e = send(pair_e, diag)
     back_o = send(pair_o, diag)
     sum_a, sum_b = kernel(
@@ -460,9 +486,9 @@
     sum_a = send(pair_a, sum_a)
     same_e = send(pair_e, row)
     same_o = send(pair_o, row)
-    (out,) = kernel(
-        final_kernel, "s" + "v" * 8, (piece,), (flags, tile, own, same_e, same_o, tag_e, tag_o, sum_a, sum_b), 1 << 20)
-    return out[None]
+    near, twice = kernel(
+        near_kernel, "s" + "v" * 7, (piece, piece), (flags, tagged, own, same_e, same_o, tag_e, tag_o, sum_a), 1 << 20)
+    return (near + twice * sum_b)[None]
 
 
 def solution(mesh):

time: 113 us -> 112 us (level)
  the two profiles are of different devices: /device:TPU:195 before, /device:TPU:67 now
where the time goes in v2:
time: 112 us; the launch traced here: 111 us
  starting transfers between devices  66.9 us (60%)
  Pallas kernels  22.2 us (20%)
  waiting for transfers between devices  17.9 us (16%)
  local copies, waits for them, and re-layouts  2.27 us (2%)
    ppermute x16, starting transfers between devices, send(): return lax.ppermute(value, axis, pairs)  66.9 us
    pallas_call x10, Pallas kernels, kernel(): pl.pallas_call(function, out_shape=tuple(outs), in_specs=places, out_spec...  22.2 us
    ppermute x16, waiting for transfers between devices, send(): return lax.ppermute(value, axis, pairs)  17.9 us
    unnamed x18, local copies, waits for them, and re-layouts  2.27 us
  transfers between devices with their start and end apart: 16, of which 4 were waited for; matrix products, arithmetic and copies ran while one was open for 0% of the time, Pallas kernels for 15%

profile of v2, /device:TPU:67, one launch (start us, length us, event | category | flops | bytes accessed | tf_op | source)
XLA Modules:
  0.0 111.0 jit_solution(2959731849685505363)
XLA Ops:
  0.0 2.6 %collective-permute-start = (f32[32,16,128]{2,1,0:T(8,128)}, f32[32,16,128]{2,1,0:T(8,128)S(1)}, u32[]{:S(2)}, u32[]{:S(2)}) collective-permute-start(f32[32,16,128]{2,1,0:T(8,128)} %bitcast.25), channel_id=1, source_target_pairs={{0,6},{6,0},{12,18},{18,12},{24,30},{30,24},{36,42},{42,36},{48,54... | collective-permute-start | bytes 786440 | tf_op jit(solution)/shard_map/ppermute | solution.py:417
  2.6 0.0 copy-start.2
  2.6 0.6 copy-done.2
  3.2 0.0 copy-start
  3.2 0.9 copy-done
  4.2 2.9 %shard_map.118 = (f32[34,16,128]{2,1,0:T(8,128)S(1)}, f32[64,16,256]{2,1,0:T(8,128)S(1)}, f32[64,16,256]{2,1,0:T(8,128)S(1)}, f32[64,8,256]{2,1,0:T(8,128)S(1)},...) custom-call(s32[1,2]{1,0:T(1,128)S(1)} %copy-done.2, f32[32,16,128]{2,1,0:T(8,128)S(1)} %bitcast.26, f32[64,16,256]{2,1,0:T(8,128)} %bitcast.30, ...), custom_call_target="tpu_custom_call" | custom-call | flops 1048576 | bytes 5783592 | tf_op jit(solution)/shard_map/pallas_call | solution.py:423
  7.1 3.2 %collective-permute-start.2 = (f32[34,16,128]{2,1,0:T(8,128)S(1)}, f32[34,16,128]{2,1,0:T(8,128)S(1)}, u32[]{:S(2)}, u32[]{:S(2)}) collective-permute-start(f32[34,16,128]{2,1,0:T(8,128)S(1)} %get-tuple-element.41.own.tile), channel_id=1, source_target_pairs={{0,24},{6,30},{12,36},{18,42},{24,0},{30,6},{36,12},{42,18},{48,72... | collective-permute-start | bytes 835592 | tf_op jit(solution)/shard_map/ppermute | solution.py:417
  10.3 4.8 %collective-permute-start.3 = (f32[34,16,128]{2,1,0:T(8,128)S(1)}, f32[34,16,128]{2,1,0:T(8,128)S(1)}, u32[]{:S(2)}, u32[]{:S(2)}) collective-permute-start(f32[34,16,128]{2,1,0:T(8,128)S(1)} %get-tuple-element.41.own.tile), channel_id=1, source_target_pairs={{24,48},{30,54},{36,60},{42,66},{48,24},{54,30},{60,36},{66,42},{7... | collective-permute-start | bytes 835592 | tf_op jit(solution)/shard_map/ppermute | solution.py:417
  15.1 14.4 %collective-permute-start.1 = (f32[32,16,128]{2,1,0:T(8,128)S(1)}, f32[32,16,128]{2,1,0:T(8,128)S(1)}, u32[]{:S(2)}, u32[]{:S(2)}) collective-permute-start(f32[32,16,128]{2,1,0:T(8,128)S(1)} %bitcast.27), channel_id=1, source_target_pairs={{6,12},{12,6},{30,36},{36,30},{54,60},{60,54},{78,84},{84,78},{102... | collective-permute-start | bytes 786440 | tf_op jit(solution)/shard_map/ppermute | solution.py:417
  29.5 2.5 %collective-permute-start.6 = (f32[64,8,256]{2,1,0:T(8,128)S(1)}, f32[64,8,256]{2,1,0:T(8,128)S(1)}, u32[]{:S(2)}, u32[]{:S(2)}) collective-permute-start(f32[64,8,256]{2,1,0:T(8,128)S(1)} %get-tuple-element.50), channel_id=1, source_target_pairs={{0,1},{1,2},{2,3},{3,4},{4,5},{6,7},{7,8},{8,9},{9,10},{10,11},{12... | collective-permute-start | bytes 1572872 | tf_op jit(solution)/shard_map/ppermute | solution.py:417
  32.0 0.0 collective-permute-done.col_a
  32.1 2.8 %collective-permute-start.7 = (f32[64,8,256]{2,1,0:T(8,128)S(1)}, f32[64,8,256]{2,1,0:T(8,128)S(1)}, u32[]{:S(2)}, u32[]{:S(2)}) collective-permute-start(f32[64,8,256]{2,1,0:T(8,128)S(1)} %get-tuple-element.51), channel_id=1, source_target_pairs={{1,0},{2,1},{3,2},{4,3},{5,4},{7,6},{8,7},{9,8},{10,9},{11,10},{13... | collective-permute-start | bytes 1572872 | tf_op jit(solution)/shard_map/ppermute | solution.py:417
  34.9 4.8 %collective-permute-done.1.col_b = f32[32,16,128]{2,1,0:T(8,128)S(1)} collective-permute-done((f32[32,16,128]{2,1,0:T(8,128)S(1)}, f32[32,16,128]{2,1,0:T(8,128)S(1)}, u32[]{:S(2)}, u32[]{:S(2)}) %collective-permute-start.1) | collective-permute-done | bytes 262176 | tf_op jit(solution)/shard_map/ppermute | solution.py:417
  39.7 0.0 collective-permute-done.2.row_e
  39.7 0.0 collective-permute-done.3.row_o
  39.7 0.0 copy-start.7
  39.7 0.0 copy-start.8
  39.7 0.6 shard_map.119
  40.3 1.9 %collective-permute-start.4 = (f32[32,16,128]{2,1,0:T(8,128)S(1)}, f32[32,16,128]{2,1,0:T(8,128)S(1)}, u32[]{:S(2)}, u32[]{:S(2)}) collective-permute-start(f32[32,16,128]{2,1,0:T(8,128)S(1)} %get-tuple-element.42), channel_id=1, source_target_pairs={{0,24},{6,30},{12,36},{18,42},{24,0},{30,6},{36,12},{42,18},{48,72... | collective-permute-start | bytes 786440 | tf_op jit(solution)/shard_map/ppermute | solution.py:417
  42.3 4.0 %collective-permute-start.5 = (f32[32,16,128]{2,1,0:T(8,128)S(1)}, f32[32,16,128]{2,1,0:T(8,128)S(1)}, u32[]{:S(2)}, u32[]{:S(2)}) collective-permute-start(f32[32,16,128]{2,1,0:T(8,128)S(1)} %get-tuple-element.43), channel_id=1, source_target_pairs={{24,48},{30,54},{36,60},{42,66},{48,24},{54,30},{60,36},{66,42},{7... | collective-permute-start | bytes 786440 | tf_op jit(solution)/shard_map/ppermute | solution.py:417
  46.3 0.0 copy-done.7
  46.3 0.0 copy-done.8
  46.3 0.0 copy-start.3
  46.3 3.5 %shard_map.120 = (f32[1024,256]{1,0:T(8,128)S(1)}, f32[1024,256]{1,0:T(8,128)S(1)}) custom-call(f32[1024,256]{1,0:T(8,128)S(1)} %bitcast.14, f32[1024,256]{1,0:T(8,128)S(1)} %bitcast.17, bf16[3,128,256]{2,1,0:T(8,128)(2,1)S(1)} %copy-done.7, bf16[256,256]{1,0:T(8,128)(2,1)S(1)} %copy-done.8), custom_call_target="tpu_custom_call" | custom-call | flops 2147483648 | bytes 4849664 | tf_op jit(solution)/shard_map/pallas_call | solution.py:423
  49.9 0.0 copy-start.4
  50.5 0.0 copy-start.5
  50.6 0.0 copy-start.6
  50.6 0.0 copy-done.3
  50.6 0.0 copy-done.4
  50.6 0.6 copy-done.5
  51.2 0.0 copy-done.6
  51.2 0.0 copy-start.1
  51.2 3.3 %shard_map.121 = (f32[1024,256]{1,0:T(8,128)S(1)}, f32[1024,256]{1,0:T(8,128)S(1)}, f32[8,128]{1,0:T(8,128)S(1)}, f32[8,1024]{1,0:T(8,128)S(1)}, bf16[128,256]{1...) custom-call(s32[1]{0:T(128)S(6)} %copy.13.shot_count, s32[1,16]{1,0:T(1,128)S(1)} %copy-done.6, f32[2,16]{1,0:T(2,128)S(1)} %bitcast.29, ...), custom_call_target="tpu_custom_call" | custom-call | flops 2147483648 | bytes 3326148 | tf_op jit(solution)/shard_map/pallas_call | solution.py:423
  54.5 0.0 collective-permute-done.6
  54.5 0.0 collective-permute-done.7
  54.5 0.0 collective-permute-done.4.diag_e
  54.5 0.0 collective-permute-done.5.diag_o
  54.6 0.0 copy-done.1
  54.6 2.7 %shard_map.122 = (f32[64,16,256]{2,1,0:T(8,128)S(1)}, f32[1024,256]{1,0:T(8,128)S(1)}, f32[1024,256]{1,0:T(8,128)S(1)}, f32[64,8,256]{2,1,0:T(8,128)S(1)}, f32[64,8,256]{2,1,0:T(8,128)S(1)}) custom-call(s32[8]{0:T(128)S(1)} %get-tuple-element.40.flags, f32[34,16,128]{2,1,0:T(8,128)S(1)} %get-tuple-element.41.own.tile, ...), custom_call_target="tpu_custom_call" | custom-call | flops 1073741824 | bytes 13484064 | tf_op jit(solution)/shard_map/pallas_call | solution.py:423
  57.3 1.9 %collective-permute-start.8 = (f32[64,8,256]{2,1,0:T(8,128)S(1)}, f32[64,8,256]{2,1,0:T(8,128)S(1)}, u32[]{:S(2)}, u32[]{:S(2)}) collective-permute-start(f32[64,8,256]{2,1,0:T(8,128)S(1)} %get-tuple-element.63), channel_id=1, source_target_pairs={{0,1},{1,2},{2,3},{3,4},{4,5},{6,7},{7,8},{8,9},{9,10},{10,11},{12... | collective-permute-start | bytes 1572872 | tf_op jit(solution)/shard_map/ppermute | solution.py:417
  59.2 3.4 %collective-permute-start.9 = (f32[64,8,256]{2,1,0:T(8,128)S(1)}, f32[64,8,256]{2,1,0:T(8,128)S(1)}, u32[]{:S(2)}, u32[]{:S(2)}) collective-permute-start(f32[64,8,256]{2,1,0:T(8,128)S(1)} %get-tuple-element.64), channel_id=1, source_target_pairs={{1,0},{2,1},{3,2},{4,3},{5,4},{7,6},{8,7},{9,8},{10,9},{11,10},{13... | collective-permute-start | bytes 1572872 | tf_op jit(solution)/shard_map/ppermute | solution.py:417
  62.6 1.7 %shard_map.124 = (f32[1024,256]{1,0:T(8,128)S(1)}, f32[1024,256]{1,0:T(8,128)S(1)}) custom-call(f32[8,128]{1,0:T(8,128)S(1)} %get-tuple-element.57.shots, f32[8,1024]{1,0:T(8,128)S(1)} %get-tuple-element.58.receivers, bf16[128,256]{1,0:T(8,128)(2,1)S(1)} %get-tuple-element.59.shot_ones, bf16[1024,256]{1,0:T(8,128)(2,1)S(1)} %get-tuple-element.60.receiver_ones), custom_call_target="tpu_custom_call" | custom-call | flops 2147483648 | bytes 3313664 | tf_op jit(solution)/shard_map/pallas_call | solution.py:423
  64.3 3.5 %shard_map.123 = (f32[1024,256]{1,0:T(8,128)S(1)}, f32[1024,256]{1,0:T(8,128)S(1)}) custom-call(f32[1024,256]{1,0:T(8,128)S(1)} %get-tuple-element.53.fwd.mid_fwd, f32[1024,256]{1,0:T(8,128)S(1)} %get-tuple-element.54.adj.mid_adj, bf16[3,128,256]{2,1,0:T(8,128)(2,1)S(1)} %copy-done.7, bf16[256,256]{1,0:T(8,128)(2,1)S(1)} %copy-done.8), custom_call_target="tpu_custom_call" | custom-call | flops 2147483648 | bytes 4849664 | tf_op jit(solution)/shard_map/pallas_call | solution.py:423
  67.8 0.0 collective-permute-done.8
  67.9 2.2 %collective-permute-done.9 = f32[64,8,256]{2,1,0:T(8,128)S(1)} collective-permute-done((f32[64,8,256]{2,1,0:T(8,128)S(1)}, f32[64,8,256]{2,1,0:T(8,128)S(1)}, u32[]{:S(2)}, u32[]{:S(2)}) %collective-permute-start.9) | collective-permute-done | bytes 524320 | tf_op jit(solution)/shard_map/ppermute | solution.py:417
  70.1 2.7 %shard_map.125 = (f32[32,16,128]{2,1,0:T(8,128)S(1)}, f32[32,16,128]{2,1,0:T(8,128)S(1)}, f32[32,16,128]{2,1,0:T(8,128)S(1)}, f32[32,16,128]{2,1,0:T(8,128)S(1)}) custom-call(s32[8]{0:T(128)S(1)} %get-tuple-element.40.flags, f32[1024,256]{1,0:T(8,128)S(1)} %bitcast.20, f32[1024,256]{1,0:T(8,128)S(1)} %get-tuple-element.55.lap_fwd, ...), custom_call_target="tpu_custom_call" | custom-call | flops 1073741824 | bytes 11599904 | tf_op jit(solution)/shard_map/pallas_call | solution.py:423
  72.8 2.3 %collective-permute-start.12 = (f32[32,16,128]{2,1,0:T(8,128)S(1)}, f32[32,16,128]{2,1,0:T(8,128)S(1)}, u32[]{:S(2)}, u32[]{:S(2)}) collective-permute-start(f32[32,16,128]{2,1,0:T(8,128)S(1)} %get-tuple-element.70), channel_id=1, source_target_pairs={{0,24},{6,30},{12,36},{18,42},{24,0},{30,6},{36,12},{42,18},{48,72... | collective-permute-start | bytes 786440 | tf_op jit(solution)/shard_map/ppermute | solution.py:417
  75.1 2.9 %collective-permute-start.13 = (f32[32,16,128]{2,1,0:T(8,128)S(1)}, f32[32,16,128]{2,1,0:T(8,128)S(1)}, u32[]{:S(2)}, u32[]{:S(2)}) collective-permute-start(f32[32,16,128]{2,1,0:T(8,128)S(1)} %get-tuple-element.70), channel_id=1, source_target_pairs={{24,48},{30,54},{36,60},{42,66},{48,24},{54,30},{60,36},{66,42},{7... | collective-permute-start | bytes 786440 | tf_op jit(solution)/shard_map/ppermute | solution.py:417
  78.1 1.9 %collective-permute-start.10 = (f32[32,16,128]{2,1,0:T(8,128)S(1)}, f32[32,16,128]{2,1,0:T(8,128)S(1)}, u32[]{:S(2)}, u32[]{:S(2)}) collective-permute-start(f32[32,16,128]{2,1,0:T(8,128)S(1)} %get-tuple-element.66), channel_id=1, source_target_pairs={{0,24},{6,30},{12,36},{18,42},{24,0},{30,6},{36,12},{42,18},{48,72... | collective-permute-start | bytes 786440 | tf_op jit(solution)/shard_map/ppermute | solution.py:417
  80.0 4.4 %collective-permute-start.11 = (f32[32,16,128]{2,1,0:T(8,128)S(1)}, f32[32,16,128]{2,1,0:T(8,128)S(1)}, u32[]{:S(2)}, u32[]{:S(2)}) collective-permute-start(f32[32,16,128]{2,1,0:T(8,128)S(1)} %get-tuple-element.66), channel_id=1, source_target_pairs={{24,48},{30,54},{36,60},{42,66},{48,24},{54,30},{60,36},{66,42},{7... | collective-permute-start | bytes 786440 | tf_op jit(solution)/shard_map/ppermute | solution.py:417
  84.5 0.0 collective-permute-done.12.back_e
  84.5 1.8 %collective-permute-done.13.back_o = f32[32,16,128]{2,1,0:T(8,128)S(1)} collective-permute-done((f32[32,16,128]{2,1,0:T(8,128)S(1)}, f32[32,16,128]{2,1,0:T(8,128)S(1)}, u32[]{:S(2)}, u32[]{:S(2)}) %collective-permute-start.13) | collective-permute-done | bytes 262176 | tf_op jit(solution)/shard_map/ppermute | solution.py:417
  86.3 0.7 shard_map.126
  86.9 1.9 %collective-permute-start.14 = (f32[32,16,128]{2,1,0:T(8,128)S(1)}, f32[32,16,128]{2,1,0:T(8,128)S(1)}, u32[]{:S(2)}, u32[]{:S(2)}) collective-permute-start(f32[32,16,128]{2,1,0:T(8,128)S(1)} %get-tuple-element.71), channel_id=1, source_target_pairs={{0,6},{6,0},{12,18},{18,12},{24,30},{30,24},{36,42},{42,36},{48,54... | collective-permute-start | bytes 786440 | tf_op jit(solution)/shard_map/ppermute | solution.py:417
  88.8 11.8 %collective-permute-start.15 = (f32[32,16,128]{2,1,0:T(8,128)S(1)}, f32[32,16,128]{2,1,0:T(8,128)S(1)}, u32[]{:S(2)}, u32[]{:S(2)}) collective-permute-start(f32[32,16,128]{2,1,0:T(8,128)S(1)} %get-tuple-element.74), channel_id=1, source_target_pairs={{6,12},{12,6},{30,36},{36,30},{54,60},{60,54},{78,84},{84,78},{102... | collective-permute-start | bytes 786440 | tf_op jit(solution)/shard_map/ppermute | solution.py:417
  100.6 0.0 collective-permute-done.10.same_e
  100.6 0.0 collective-permute-done.11.same_o
  100.6 0.0 collective-permute-done.14.sum_a
  100.6 0.6 shard_map.127
  101.3 9.0 %collective-permute-done.15 = f32[32,16,128]{2,1,0:T(8,128)S(1)} collective-permute-done((f32[32,16,128]{2,1,0:T(8,128)S(1)}, f32[32,16,128]{2,1,0:T(8,128)S(1)}, u32[]{:S(2)}, u32[]{:S(2)}) %collective-permute-start.15) | collective-permute-done | bytes 262176 | tf_op jit(solution)/shard_map/ppermute | solution.py:417
  110.3 0.8 add_bitcast_fusion
Async XLA Ops:
  0.0 32.0 %collective-permute-start = (f32[32,16,128]{2,1,0:T(8,128)}, f32[32,16,128]{2,1,0:T(8,128)S(1)}, u32[]{:S(2)}, u32[]{:S(2)}) collective-permute-start(f32[32,16,128]{2,1,0:T(8,128)} %bitcast.25), channel_id=1, source_target_pairs={{0,6},{6,0},{12,18},{18,12},{24,30},{30,24},{36,42},{42,36},{48,54... | collective-permute-start | bytes 786440 | tf_op jit(solution)/shard_map/ppermute | solution.py:417
  2.6 0.7 copy-start.2
  3.2 0.9 copy-start
  7.1 32.7 %collective-permute-start.2 = (f32[34,16,128]{2,1,0:T(8,128)S(1)}, f32[34,16,128]{2,1,0:T(8,128)S(1)}, u32[]{:S(2)}, u32[]{:S(2)}) collective-permute-start(f32[34,16,128]{2,1,0:T(8,128)S(1)} %get-tuple-element.41.own.tile), channel_id=1, source_target_pairs={{0,24},{6,30},{12,36},{18,42},{24,0},{30,6},{36,12},{42,18},{48,72... | collective-permute-start | bytes 835592 | tf_op jit(solution)/shard_map/ppermute | solution.py:417
  10.3 29.5 %collective-permute-start.3 = (f32[34,16,128]{2,1,0:T(8,128)S(1)}, f32[34,16,128]{2,1,0:T(8,128)S(1)}, u32[]{:S(2)}, u32[]{:S(2)}) collective-permute-start(f32[34,16,128]{2,1,0:T(8,128)S(1)} %get-tuple-element.41.own.tile), channel_id=1, source_target_pairs={{24,48},{30,54},{36,60},{42,66},{48,24},{54,30},{60,36},{66,42},{7... | collective-permute-start | bytes 835592 | tf_op jit(solution)/shard_map/ppermute | solution.py:417
  15.1 24.6 %collective-permute-start.1 = (f32[32,16,128]{2,1,0:T(8,128)S(1)}, f32[32,16,128]{2,1,0:T(8,128)S(1)}, u32[]{:S(2)}, u32[]{:S(2)}) collective-permute-start(f32[32,16,128]{2,1,0:T(8,128)S(1)} %bitcast.27), channel_id=1, source_target_pairs={{6,12},{12,6},{30,36},{36,30},{54,60},{60,54},{78,84},{84,78},{102... | collective-permute-start | bytes 786440 | tf_op jit(solution)/shard_map/ppermute | solution.py:417
  29.5 25.0 %collective-permute-start.6 = (f32[64,8,256]{2,1,0:T(8,128)S(1)}, f32[64,8,256]{2,1,0:T(8,128)S(1)}, u32[]{:S(2)}, u32[]{:S(2)}) collective-permute-start(f32[64,8,256]{2,1,0:T(8,128)S(1)} %get-tuple-element.50), channel_id=1, source_target_pairs={{0,1},{1,2},{2,3},{3,4},{4,5},{6,7},{7,8},{8,9},{9,10},{10,11},{12... | collective-permute-start | bytes 1572872 | tf_op jit(solution)/shard_map/ppermute | solution.py:417
  32.1 22.5 %collective-permute-start.7 = (f32[64,8,256]{2,1,0:T(8,128)S(1)}, f32[64,8,256]{2,1,0:T(8,128)S(1)}, u32[]{:S(2)}, u32[]{:S(2)}) collective-permute-start(f32[64,8,256]{2,1,0:T(8,128)S(1)} %get-tuple-element.51), channel_id=1, source_target_pairs={{1,0},{2,1},{3,2},{4,3},{5,4},{7,6},{8,7},{9,8},{10,9},{11,10},{13... | collective-permute-start | bytes 1572872 | tf_op jit(solution)/shard_map/ppermute | solution.py:417
  39.7 6.6 %copy-start.7 = (bf16[3,128,256]{2,1,0:T(8,128)(2,1)S(1)}, bf16[3,128,256]{2,1,0:T(8,128)(2,1)}, u32[]{:S(2)}) copy-start(bf16[3,128,256]{2,1,0:T(8,128)(2,1)} %constant.6.clone.xz) | copy-start | bytes 589828
  39.7 6.6 %copy-start.8 = (bf16[256,256]{1,0:T(8,128)(2,1)S(1)}, bf16[256,256]{1,0:T(8,128)(2,1)}, u32[]{:S(2)}) copy-start(bf16[256,256]{1,0:T(8,128)(2,1)} %constant.7.clone.y) | copy-start | bytes 393220
  40.3 14.2 %collective-permute-start.4 = (f32[32,16,128]{2,1,0:T(8,128)S(1)}, f32[32,16,128]{2,1,0:T(8,128)S(1)}, u32[]{:S(2)}, u32[]{:S(2)}) collective-permute-start(f32[32,16,128]{2,1,0:T(8,128)S(1)} %get-tuple-element.42), channel_id=1, source_target_pairs={{0,24},{6,30},{12,36},{18,42},{24,0},{30,6},{36,12},{42,18},{48,72... | collective-permute-start | bytes 786440 | tf_op jit(solution)/shard_map/ppermute | solution.py:417
  42.3 12.3 %collective-permute-start.5 = (f32[32,16,128]{2,1,0:T(8,128)S(1)}, f32[32,16,128]{2,1,0:T(8,128)S(1)}, u32[]{:S(2)}, u32[]{:S(2)}) collective-permute-start(f32[32,16,128]{2,1,0:T(8,128)S(1)} %get-tuple-element.43), channel_id=1, source_target_pairs={{24,48},{30,54},{36,60},{42,66},{48,24},{54,30},{60,36},{66,42},{7... | collective-permute-start | bytes 786440 | tf_op jit(solution)/shard_map/ppermute | solution.py:417
  46.3 4.2 %copy-start.3 = (f32[1,2,1024]{2,1,0:T(2,128)S(1)}, f32[1,2,1024]{2,1,0:T(2,128)}, u32[]{:S(2)}) copy-start(f32[1,2,1024]{2,1,0:T(2,128)} %param.20) | copy-start | bytes 24580
  49.9 0.7 copy-start.4
  50.5 0.7 copy-start.5
  50.6 0.7 copy-start.6
  51.2 3.3 %copy-start.1 = (bf16[128,128]{1,0:T(8,128)(2,1)S(1)}, bf16[128,128]{1,0:T(8,128)(2,1)}, u32[]{:S(2)}) copy-start(bf16[128,128]{1,0:T(8,128)(2,1)} %constant.8.clone.halo) | copy-start | bytes 98308
  57.3 10.6 %collective-permute-start.8 = (f32[64,8,256]{2,1,0:T(8,128)S(1)}, f32[64,8,256]{2,1,0:T(8,128)S(1)}, u32[]{:S(2)}, u32[]{:S(2)}) collective-permute-start(f32[64,8,256]{2,1,0:T(8,128)S(1)} %get-tuple-element.63), channel_id=1, source_target_pairs={{0,1},{1,2},{2,3},{3,4},{4,5},{6,7},{7,8},{8,9},{9,10},{10,11},{12... | collective-permute-start | bytes 1572872 | tf_op jit(solution)/shard_map/ppermute | solution.py:417
  59.2 10.9 %collective-permute-start.9 = (f32[64,8,256]{2,1,0:T(8,128)S(1)}, f32[64,8,256]{2,1,0:T(8,128)S(1)}, u32[]{:S(2)}, u32[]{:S(2)}) collective-permute-start(f32[64,8,256]{2,1,0:T(8,128)S(1)} %get-tuple-element.64), channel_id=1, source_target_pairs={{1,0},{2,1},{3,2},{4,3},{5,4},{7,6},{8,7},{9,8},{10,9},{11,10},{13... | collective-permute-start | bytes 1572872 | tf_op jit(solution)/shard_map/ppermute | solution.py:417
  72.8 11.7 %collective-permute-start.12 = (f32[32,16,128]{2,1,0:T(8,128)S(1)}, f32[32,16,128]{2,1,0:T(8,128)S(1)}, u32[]{:S(2)}, u32[]{:S(2)}) collective-permute-start(f32[32,16,128]{2,1,0:T(8,128)S(1)} %get-tuple-element.70), channel_id=1, source_target_pairs={{0,24},{6,30},{12,36},{18,42},{24,0},{30,6},{36,12},{42,18},{48,72... | collective-permute-start | bytes 786440 | tf_op jit(solution)/shard_map/ppermute | solution.py:417
  75.1 11.1 %collective-permute-start.13 = (f32[32,16,128]{2,1,0:T(8,128)S(1)}, f32[32,16,128]{2,1,0:T(8,128)S(1)}, u32[]{:S(2)}, u32[]{:S(2)}) collective-permute-start(f32[32,16,128]{2,1,0:T(8,128)S(1)} %get-tuple-element.70), channel_id=1, source_target_pairs={{24,48},{30,54},{36,60},{42,66},{48,24},{54,30},{60,36},{66,42},{7... | collective-permute-start | bytes 786440 | tf_op jit(solution)/shard_map/ppermute | solution.py:417
  78.1 22.5 %collective-permute-start.10 = (f32[32,16,128]{2,1,0:T(8,128)S(1)}, f32[32,16,128]{2,1,0:T(8,128)S(1)}, u32[]{:S(2)}, u32[]{:S(2)}) collective-permute-start(f32[32,16,128]{2,1,0:T(8,128)S(1)} %get-tuple-element.66), channel_id=1, source_target_pairs={{0,24},{6,30},{12,36},{18,42},{24,0},{30,6},{36,12},{42,18},{48,72... | collective-permute-start | bytes 786440 | tf_op jit(solution)/shard_map/ppermute | solution.py:417
  80.0 20.6 %collective-permute-start.11 = (f32[32,16,128]{2,1,0:T(8,128)S(1)}, f32[32,16,128]{2,1,0:T(8,128)S(1)}, u32[]{:S(2)}, u32[]{:S(2)}) collective-permute-start(f32[32,16,128]{2,1,0:T(8,128)S(1)} %get-tuple-element.66), channel_id=1, source_target_pairs={{24,48},{30,54},{36,60},{42,66},{48,24},{54,30},{60,36},{66,42},{7... | collective-permute-start | bytes 786440 | tf_op jit(solution)/shard_map/ppermute | solution.py:417
  86.9 13.7 %collective-permute-start.14 = (f32[32,16,128]{2,1,0:T(8,128)S(1)}, f32[32,16,128]{2,1,0:T(8,128)S(1)}, u32[]{:S(2)}, u32[]{:S(2)}) collective-permute-start(f32[32,16,128]{2,1,0:T(8,128)S(1)} %get-tuple-element.71), channel_id=1, source_target_pairs={{0,6},{6,0},{12,18},{18,12},{24,30},{30,24},{36,42},{42,36},{48,54... | collective-permute-start | bytes 786440 | tf_op jit(solution)/shard_map/ppermute | solution.py:417
  88.8 21.4 %collective-permute-start.15 = (f32[32,16,128]{2,1,0:T(8,128)S(1)}, f32[32,16,128]{2,1,0:T(8,128)S(1)}, u32[]{:S(2)}, u32[]{:S(2)}) collective-permute-start(f32[32,16,128]{2,1,0:T(8,128)S(1)} %get-tuple-element.74), channel_id=1, source_target_pairs={{6,12},{12,6},{30,36},{36,30},{54,60},{60,54},{78,84},{84,78},{102... | collective-permute-start | bytes 786440 | tf_op jit(solution)/shard_map/ppermute | solution.py:417

commit v3 on v2

--- a/solution.py
+++ b/solution.py
@@ -94,7 +94,9 @@
     return top, bottom
 
 
-def load_kernel(anchor, vel_hbm, fwd_hbm, adj_hbm, tagged, fwd, adj, up, down, flags, sems):
+def load_kernel(anchor_hbm, vel_hbm, fwd_hbm, adj_hbm, tagged, fwd, adj, up, down, flags, anchor, sems):
+    anchor_copy = pltpu.make_async_copy(anchor_hbm, anchor, sems.at[2 * PIECES + 1])
+    anchor_copy.start()
     rows = vel_hbm.shape[0]
     tile_copy = pltpu.make_async_copy(vel_hbm, tagged.at[pl.ds(0, rows)], sems.at[2 * PIECES])
     size = AX // PIECES
@@ -106,6 +108,7 @@
     for copy in copies:
         copy.start()
     tile_copy.start()
+    anchor_copy.wait()
     device = lax.axis_index("shot")
     home_row = device // TILES_Y
     home_col = device - home_row * TILES_Y
@@ -136,15 +139,17 @@
     tile_copy.wait()
 
 
-def inner_laplace(b, parts, xz, y):
-    kind = jnp.where(b == 0, 0, jnp.where(b == BLOCKS - 1, 2, 1))
-    first = jnp.clip(b * BX - 4, 0, AX - 2 * BX) * Z
-    window = pl.ds(pl.multiple_of(first, 64), 2 * ROWS)
-    own = pl.ds(pl.multiple_of(b * ROWS, ROWS), ROWS)
+def inner_laplace(b, parts, xz, y, result):
+    pair = pl.ds(pl.multiple_of(b * 2 * ROWS, 2 * ROWS), 2 * ROWS)
     high, middle, low = parts
-    result = dot(xz[kind], low[window]) + dot(low[own], y[...])
-    result = result + (dot(xz[kind], middle[window]) + dot(middle[own], y[...]))
-    return result + (dot(xz[kind], high[window]) + dot(high[own], y[...]))
+    total = dot(low[pair], y[...]) + dot(middle[pair], y[...]) + dot(high[pair], y[...])
+    for i in range(2):
+        block = 2 * b + i
+        kind = jnp.where(block == 0, 0, jnp.where(block == BLOCKS - 1, 2, 1))
+        first = jnp.clip(block * BX - 4, 0, AX - 2 * BX) * Z
+        window = pl.ds(pl.multiple_of(first, 64), 2 * ROWS)
+        part = dot(xz[kind], low[window]) + dot(xz[kind], middle[window]) + dot(xz[kind], high[window])
+        result[pl.ds(pl.multiple_of(block * ROWS, ROWS), ROWS)] = part + total[i * ROWS : (i + 1) * ROWS]
 
 
 def split_all(field, parts):
@@ -172,9 +177,10 @@
 def ones_of(points, ones):
     def step(i, _):
         at = pl.ds(pl.multiple_of(i * 128, 128), 128)
-        place = jnp.broadcast_to(points[1:2, at], (8, 128)).T[:, 0:1].astype(jnp.int32)
-        here = lax.broadcasted_iota(jnp.int32, (128, Y), 1) == place
-        ones[at] = jnp.where(here, 1.0, 0.0).astype(BF16)
+        place = jnp.broadcast_to(points[1:2, at], (128, 128)).T
+        y = lax.broadcasted_iota(jnp.int32, (128, 128), 1).astype(F32)
+        for n in range(Y // 128):
+            ones[at, pl.ds(n * 128, 128)] = jnp.where(place == y + float(n * 128), 1.0, 0.0).astype(BF16)
         return 0
 
     lax.fori_loop(0, points.shape[1] // 128, step, 0)
@@ -225,12 +231,11 @@
     split_all(adj, (a0, a1, a2))
 
     def step(b, _):
-        at = pl.ds(pl.multiple_of(b * ROWS, ROWS), ROWS)
-        lap_fwd[at] = inner_laplace(b, (f0, f1, f2), xz, y)
-        lap_adj[at] = inner_laplace(b, (a0, a1, a2), xz, y)
-        return 0
-
-    lax.fori_loop(0, BLOCKS, step, 0)
+        inner_laplace(b, (f0, f1, f2), xz, y, lap_fwd)
+        inner_laplace(b, (a0, a1, a2), xz, y, lap_adj)
+        return 0
+
+    lax.fori_loop(0, BLOCKS // 2, step, 0)
 
 
 def halo_part(b, below, above, halo, both):
@@ -250,7 +255,7 @@
 
 def advance_kernel(flags, own, col_a, col_b, row_e, row_o, diag_e, diag_o, lap_fwd, lap_adj, fwd, adj, fwd_in, adj_in,
                    below, above, halo, speed2, mid_fwd, mid_adj, up, down, both):
-    half = col_a.shape[0]
+    half = col_b.shape[0]
     wide = own.shape[2]
     with_e = flags[2] == 1
     with_a = flags[3] == 1
@@ -345,7 +350,7 @@
 
 
 def select_kernel(flags, col_a, col_b, row_e, row_o, diag_e, diag_o, tag_e, tag_o):
-    half = col_a.shape[0]
+    half = col_b.shape[0]
     toward_a = flags[5].astype(F32)
     tag_e[...] = row_e[half:]
     tag_o[...] = row_o[half:]
@@ -439,14 +444,14 @@
     rim = (exact(along_halo()),)
 
     col_b = send(pair_b, tile)
-    col_a = send(pair_a, tile)
     field = shape(AX, depth, Y)
     tagged, fwd, adj, up, down, flags = kernel(
-        load_kernel, "shhh",
+        load_kernel, "hhhh",
         (shape(half + 2, depth, wide), field, field, rim_shape, rim_shape, shape(8, dtype=jnp.int32)),
-        (aperture_anchor, tile, fwd_field[0], adj_field[0]), 1 << 20, 50, [pltpu.SemaphoreType.DMA((2 * PIECES + 1,))])
+        tuple(pltpu.with_memory_space_constraint(v, pltpu.HBM) for v in (aperture_anchor, tile, fwd_field[0], adj_field[0])), 1 << 20, 8, [pltpu.SMEM((1, 2), jnp.int32), pltpu.SemaphoreType.DMA((2 * PIECES + 2,))])
     flat_fwd = fwd.reshape(FLAT, Y)
     flat_adj = adj.reshape(FLAT, Y)
+    col_a = send(pair_a, tagged)
     row_e = send(pair_e, tagged)
     row_o = send(pair_o, tagged)
     below = send(to_up, up, "slab")

time: 112 us -> 109 us (0.973)
  the two profiles are of different devices: /device:TPU:67 before, /device:TPU:135 now
where the time goes in v3:
time: 109 us; the launch traced here: 108 us
  starting transfers between devices  61.2 us (56%)
  waiting for transfers between devices  25 us (23%)
  Pallas kernels  19.6 us (18%)
    ppermute x16, starting transfers between devices, send(): return lax.ppermute(value, axis, pairs)  61.2 us
    ppermute x16, waiting for transfers between devices, send(): return lax.ppermute(value, axis, pairs)  25 us
    pallas_call x10, Pallas kernels, kernel(): pl.pallas_call(function, out_shape=tuple(outs), in_specs=places, out_spec...  19.6 us
  transfers between devices with their start and end apart: 16, of which 4 were waited for; matrix products, arithmetic and copies ran while one was open for 0% of the time, Pallas kernels for 13%

profile of v3, /device:TPU:135, one launch (start us, length us, event | category | flops | bytes accessed | tf_op | source)
XLA Modules:
  0.0 108.2 jit_solution(14830004555768565192)
XLA Ops:
  0.0 13.0 %collective-permute-start.1 = (f32[32,16,128]{2,1,0:T(8,128)}, f32[32,16,128]{2,1,0:T(8,128)S(1)}, u32[]{:S(2)}, u32[]{:S(2)}) collective-permute-start(f32[32,16,128]{2,1,0:T(8,128)} %bitcast.29), channel_id=1, source_target_pairs={{6,12},{12,6},{30,36},{36,30},{54,60},{60,54},{78,84},{84,78},{102... | collective-permute-start | bytes 786440 | tf_op jit(solution)/shard_map/ppermute | solution.py:422
  13.0 2.3 %shard_map.118 = (f32[34,16,128]{2,1,0:T(8,128)S(1)}, f32[64,16,256]{2,1,0:T(8,128)S(1)}, f32[64,16,256]{2,1,0:T(8,128)S(1)}, f32[64,8,256]{2,1,0:T(8,128)S(1)},...) custom-call(s32[1,2]{1,0:T(1,128)} %anchor_hbm.1, f32[32,16,128]{2,1,0:T(8,128)} %bitcast.30, f32[64,16,256]{2,1,0:T(8,128)} %bitcast.27, ...), custom_call_target="tpu_custom_call" | custom-call | flops 1048576 | bytes 5783592 | tf_op jit(solution)/shard_map/pallas_call | solution.py:428
  15.3 1.9 %collective-permute-start = (f32[34,16,128]{2,1,0:T(8,128)S(1)}, f32[34,16,128]{2,1,0:T(8,128)S(1)}, u32[]{:S(2)}, u32[]{:S(2)}) collective-permute-start(f32[34,16,128]{2,1,0:T(8,128)S(1)} %get-tuple-element.41.own.tile), channel_id=1, source_target_pairs={{0,6},{6,0},{12,18},{18,12},{24,30},{30,24},{36,42},{42,36},{48,54... | collective-permute-start | bytes 835592 | tf_op jit(solution)/shard_map/ppermute | solution.py:422
  17.3 3.2 %collective-permute-start.2 = (f32[34,16,128]{2,1,0:T(8,128)S(1)}, f32[34,16,128]{2,1,0:T(8,128)S(1)}, u32[]{:S(2)}, u32[]{:S(2)}) collective-permute-start(f32[34,16,128]{2,1,0:T(8,128)S(1)} %get-tuple-element.41.own.tile), channel_id=1, source_target_pairs={{0,24},{6,30},{12,36},{18,42},{24,0},{30,6},{36,12},{42,18},{48,72... | collective-permute-start | bytes 835592 | tf_op jit(solution)/shard_map/ppermute | solution.py:422
  20.5 5.1 %collective-permute-start.3 = (f32[34,16,128]{2,1,0:T(8,128)S(1)}, f32[34,16,128]{2,1,0:T(8,128)S(1)}, u32[]{:S(2)}, u32[]{:S(2)}) collective-permute-start(f32[34,16,128]{2,1,0:T(8,128)S(1)} %get-tuple-element.41.own.tile), channel_id=1, source_target_pairs={{24,48},{30,54},{36,60},{42,66},{48,24},{54,30},{60,36},{66,42},{7... | collective-permute-start | bytes 835592 | tf_op jit(solution)/shard_map/ppermute | solution.py:422
  25.6 3.7 %collective-permute-start.6 = (f32[64,8,256]{2,1,0:T(8,128)S(1)}, f32[64,8,256]{2,1,0:T(8,128)S(1)}, u32[]{:S(2)}, u32[]{:S(2)}) collective-permute-start(f32[64,8,256]{2,1,0:T(8,128)S(1)} %get-tuple-element.50), channel_id=1, source_target_pairs={{0,1},{1,2},{2,3},{3,4},{4,5},{6,7},{7,8},{8,9},{9,10},{10,11},{12... | collective-permute-start | bytes 1572872 | tf_op jit(solution)/shard_map/ppermute | solution.py:422
  29.3 0.0 collective-permute-done.1.col_b
  29.4 1.9 %collective-permute-start.7 = (f32[64,8,256]{2,1,0:T(8,128)S(1)}, f32[64,8,256]{2,1,0:T(8,128)S(1)}, u32[]{:S(2)}, u32[]{:S(2)}) collective-permute-start(f32[64,8,256]{2,1,0:T(8,128)S(1)} %get-tuple-element.51), channel_id=1, source_target_pairs={{1,0},{2,1},{3,2},{4,3},{5,4},{7,6},{8,7},{9,8},{10,9},{11,10},{13... | collective-permute-start | bytes 1572872 | tf_op jit(solution)/shard_map/ppermute | solution.py:422
  31.3 0.0 collective-permute-done.col_a
  31.3 0.0 collective-permute-done.2.row_e
  31.3 0.6 collective-permute-done.3.row_o
  31.9 0.0 copy-start.5
  31.9 0.0 copy-start.6
  31.9 0.6 shard_map.119
  32.5 1.9 %collective-permute-start.4 = (f32[32,16,128]{2,1,0:T(8,128)S(1)}, f32[32,16,128]{2,1,0:T(8,128)S(1)}, u32[]{:S(2)}, u32[]{:S(2)}) collective-permute-start(f32[32,16,128]{2,1,0:T(8,128)S(1)} %get-tuple-element.42), channel_id=1, source_target_pairs={{0,24},{6,30},{12,36},{18,42},{24,0},{30,6},{36,12},{42,18},{48,72... | collective-permute-start | bytes 786440 | tf_op jit(solution)/shard_map/ppermute | solution.py:422
  34.5 5.1 %collective-permute-start.5 = (f32[32,16,128]{2,1,0:T(8,128)S(1)}, f32[32,16,128]{2,1,0:T(8,128)S(1)}, u32[]{:S(2)}, u32[]{:S(2)}) collective-permute-start(f32[32,16,128]{2,1,0:T(8,128)S(1)} %get-tuple-element.43), channel_id=1, source_target_pairs={{24,48},{30,54},{36,60},{42,66},{48,24},{54,30},{60,36},{66,42},{7... | collective-permute-start | bytes 786440 | tf_op jit(solution)/shard_map/ppermute | solution.py:422
  39.6 0.0 copy-done.5
  39.6 0.0 copy-done.6
  39.6 0.0 copy-start.1
  39.6 2.8 %shard_map.120 = (f32[1024,256]{1,0:T(8,128)S(1)}, f32[1024,256]{1,0:T(8,128)S(1)}) custom-call(f32[1024,256]{1,0:T(8,128)S(1)} %bitcast.14, f32[1024,256]{1,0:T(8,128)S(1)} %bitcast.17, bf16[3,128,256]{2,1,0:T(8,128)(2,1)S(1)} %copy-done.5, bf16[256,256]{1,0:T(8,128)(2,1)S(1)} %copy-done.6), custom_call_target="tpu_custom_call" | custom-call | flops 2147483648 | bytes 4849664 | tf_op jit(solution)/shard_map/pallas_call | solution.py:428
  42.5 0.0 copy-start.2
  43.1 0.0 copy-start.3
  43.2 0.0 copy-start.4
  43.2 0.0 copy-done.1
  43.2 0.0 copy-done.2
  43.2 0.6 copy-done.3
  43.8 0.0 copy-done.4
  43.8 0.0 copy-start
  43.8 2.6 %shard_map.121 = (f32[1024,256]{1,0:T(8,128)S(1)}, f32[1024,256]{1,0:T(8,128)S(1)}, f32[8,128]{1,0:T(8,128)S(1)}, f32[8,1024]{1,0:T(8,128)S(1)}, bf16[128,256]{1...) custom-call(s32[1]{0:T(128)S(6)} %copy.13.shot_count, s32[1,16]{1,0:T(1,128)S(1)} %copy-done.4, f32[2,16]{1,0:T(2,128)S(1)} %bitcast.26, ...), custom_call_target="tpu_custom_call" | custom-call | flops 2147483648 | bytes 3326148 | tf_op jit(solution)/shard_map/pallas_call | solution.py:428
  46.5 0.0 collective-permute-done.6
  46.5 0.0 collective-permute-done.7
  46.5 0.0 collective-permute-done.4.diag_e
  46.5 0.0 collective-permute-done.5.diag_o
  46.5 0.0 copy-done
  46.5 2.7 %shard_map.122 = (f32[64,16,256]{2,1,0:T(8,128)S(1)}, f32[1024,256]{1,0:T(8,128)S(1)}, f32[1024,256]{1,0:T(8,128)S(1)}, f32[64,8,256]{2,1,0:T(8,128)S(1)}, f32[64,8,256]{2,1,0:T(8,128)S(1)}) custom-call(s32[8]{0:T(128)S(1)} %get-tuple-element.40.flags, f32[34,16,128]{2,1,0:T(8,128)S(1)} %get-tuple-element.41.own.tile, ...), custom_call_target="tpu_custom_call" | custom-call | flops 1073741824 | bytes 13500448 | tf_op jit(solution)/shard_map/pallas_call | solution.py:428
  49.3 3.7 %collective-permute-start.8 = (f32[64,8,256]{2,1,0:T(8,128)S(1)}, f32[64,8,256]{2,1,0:T(8,128)S(1)}, u32[]{:S(2)}, u32[]{:S(2)}) collective-permute-start(f32[64,8,256]{2,1,0:T(8,128)S(1)} %get-tuple-element.63), channel_id=1, source_target_pairs={{0,1},{1,2},{2,3},{3,4},{4,5},{6,7},{7,8},{8,9},{9,10},{10,11},{12... | collective-permute-start | bytes 1572872 | tf_op jit(solution)/shard_map/ppermute | solution.py:422
  53.0 1.9 %collective-permute-start.9 = (f32[64,8,256]{2,1,0:T(8,128)S(1)}, f32[64,8,256]{2,1,0:T(8,128)S(1)}, u32[]{:S(2)}, u32[]{:S(2)}) collective-permute-start(f32[64,8,256]{2,1,0:T(8,128)S(1)} %get-tuple-element.64), channel_id=1, source_target_pairs={{1,0},{2,1},{3,2},{4,3},{5,4},{7,6},{8,7},{9,8},{10,9},{11,10},{13... | collective-permute-start | bytes 1572872 | tf_op jit(solution)/shard_map/ppermute | solution.py:422
  54.9 1.7 %shard_map.124 = (f32[1024,256]{1,0:T(8,128)S(1)}, f32[1024,256]{1,0:T(8,128)S(1)}) custom-call(f32[8,128]{1,0:T(8,128)S(1)} %get-tuple-element.57.shots, f32[8,1024]{1,0:T(8,128)S(1)} %get-tuple-element.58.receivers, bf16[128,256]{1,0:T(8,128)(2,1)S(1)} %get-tuple-element.59.shot_ones, bf16[1024,256]{1,0:T(8,128)(2,1)S(1)} %get-tuple-element.60.receiver_ones), custom_call_target="tpu_custom_call" | custom-call | flops 2147483648 | bytes 3313664 | tf_op jit(solution)/shard_map/pallas_call | solution.py:428
  56.6 2.8 %shard_map.123 = (f32[1024,256]{1,0:T(8,128)S(1)}, f32[1024,256]{1,0:T(8,128)S(1)}) custom-call(f32[1024,256]{1,0:T(8,128)S(1)} %get-tuple-element.53.fwd.mid_fwd, f32[1024,256]{1,0:T(8,128)S(1)} %get-tuple-element.54.adj.mid_adj, bf16[3,128,256]{2,1,0:T(8,128)(2,1)S(1)} %copy-done.5, bf16[256,256]{1,0:T(8,128)(2,1)S(1)} %copy-done.6), custom_call_target="tpu_custom_call" | custom-call | flops 2147483648 | bytes 4849664 | tf_op jit(solution)/shard_map/pallas_call | solution.py:428
  59.4 3.3 %collective-permute-done.8 = f32[64,8,256]{2,1,0:T(8,128)S(1)} collective-permute-done((f32[64,8,256]{2,1,0:T(8,128)S(1)}, f32[64,8,256]{2,1,0:T(8,128)S(1)}, u32[]{:S(2)}, u32[]{:S(2)}) %collective-permute-start.8) | collective-permute-done | bytes 524320 | tf_op jit(solution)/shard_map/ppermute | solution.py:422
  62.7 4.1 %collective-permute-done.9 = f32[64,8,256]{2,1,0:T(8,128)S(1)} collective-permute-done((f32[64,8,256]{2,1,0:T(8,128)S(1)}, f32[64,8,256]{2,1,0:T(8,128)S(1)}, u32[]{:S(2)}, u32[]{:S(2)}) %collective-permute-start.9) | collective-permute-done | bytes 524320 | tf_op jit(solution)/shard_map/ppermute | solution.py:422
  66.8 2.7 %shard_map.125 = (f32[32,16,128]{2,1,0:T(8,128)S(1)}, f32[32,16,128]{2,1,0:T(8,128)S(1)}, f32[32,16,128]{2,1,0:T(8,128)S(1)}, f32[32,16,128]{2,1,0:T(8,128)S(1)}) custom-call(s32[8]{0:T(128)S(1)} %get-tuple-element.40.flags, f32[1024,256]{1,0:T(8,128)S(1)} %bitcast.20, f32[1024,256]{1,0:T(8,128)S(1)} %get-tuple-element.55.lap_fwd, ...), custom_call_target="tpu_custom_call" | custom-call | flops 1073741824 | bytes 11599904 | tf_op jit(solution)/shard_map/pallas_call | solution.py:428
  69.4 1.9 %collective-permute-start.12 = (f32[32,16,128]{2,1,0:T(8,128)S(1)}, f32[32,16,128]{2,1,0:T(8,128)S(1)}, u32[]{:S(2)}, u32[]{:S(2)}) collective-permute-start(f32[32,16,128]{2,1,0:T(8,128)S(1)} %get-tuple-element.70), channel_id=1, source_target_pairs={{0,24},{6,30},{12,36},{18,42},{24,0},{30,6},{36,12},{42,18},{48,72... | collective-permute-start | bytes 786440 | tf_op jit(solution)/shard_map/ppermute | solution.py:422
  71.4 3.3 %collective-permute-start.13 = (f32[32,16,128]{2,1,0:T(8,128)S(1)}, f32[32,16,128]{2,1,0:T(8,128)S(1)}, u32[]{:S(2)}, u32[]{:S(2)}) collective-permute-start(f32[32,16,128]{2,1,0:T(8,128)S(1)} %get-tuple-element.70), channel_id=1, source_target_pairs={{24,48},{30,54},{36,60},{42,66},{48,24},{54,30},{60,36},{66,42},{7... | collective-permute-start | bytes 786440 | tf_op jit(solution)/shard_map/ppermute | solution.py:422
  74.6 2.0 %collective-permute-start.10 = (f32[32,16,128]{2,1,0:T(8,128)S(1)}, f32[32,16,128]{2,1,0:T(8,128)S(1)}, u32[]{:S(2)}, u32[]{:S(2)}) collective-permute-start(f32[32,16,128]{2,1,0:T(8,128)S(1)} %get-tuple-element.66), channel_id=1, source_target_pairs={{0,24},{6,30},{12,36},{18,42},{24,0},{30,6},{36,12},{42,18},{48,72... | collective-permute-start | bytes 786440 | tf_op jit(solution)/shard_map/ppermute | solution.py:422
  76.7 4.0 %collective-permute-start.11 = (f32[32,16,128]{2,1,0:T(8,128)S(1)}, f32[32,16,128]{2,1,0:T(8,128)S(1)}, u32[]{:S(2)}, u32[]{:S(2)}) collective-permute-start(f32[32,16,128]{2,1,0:T(8,128)S(1)} %get-tuple-element.66), channel_id=1, source_target_pairs={{24,48},{30,54},{36,60},{42,66},{48,24},{54,30},{60,36},{66,42},{7... | collective-permute-start | bytes 786440 | tf_op jit(solution)/shard_map/ppermute | solution.py:422
  80.7 0.0 collective-permute-done.12.back_e
  80.7 0.0 collective-permute-done.13.back_o
  80.7 0.7 shard_map.126
  81.4 6.5 %collective-permute-start.14 = (f32[32,16,128]{2,1,0:T(8,128)S(1)}, f32[32,16,128]{2,1,0:T(8,128)S(1)}, u32[]{:S(2)}, u32[]{:S(2)}) collective-permute-start(f32[32,16,128]{2,1,0:T(8,128)S(1)} %get-tuple-element.71), channel_id=1, source_target_pairs={{0,6},{6,0},{12,18},{18,12},{24,30},{30,24},{36,42},{42,36},{48,54... | collective-permute-start | bytes 786440 | tf_op jit(solution)/shard_map/ppermute | solution.py:422
  87.9 1.9 %collective-permute-start.15 = (f32[32,16,128]{2,1,0:T(8,128)S(1)}, f32[32,16,128]{2,1,0:T(8,128)S(1)}, u32[]{:S(2)}, u32[]{:S(2)}) collective-permute-start(f32[32,16,128]{2,1,0:T(8,128)S(1)} %get-tuple-element.74), channel_id=1, source_target_pairs={{6,12},{12,6},{30,36},{36,30},{54,60},{60,54},{78,84},{84,78},{102... | collective-permute-start | bytes 786440 | tf_op jit(solution)/shard_map/ppermute | solution.py:422
  89.8 0.0 collective-permute-done.10.same_e
  89.8 0.0 collective-permute-done.11.same_o
  89.8 0.0 collective-permute-done.14.sum_a
  89.8 0.6 shard_map.127
  90.5 17.0 %collective-permute-done.15 = f32[32,16,128]{2,1,0:T(8,128)S(1)} collective-permute-done((f32[32,16,128]{2,1,0:T(8,128)S(1)}, f32[32,16,128]{2,1,0:T(8,128)S(1)}, u32[]{:S(2)}, u32[]{:S(2)}) %collective-permute-start.15) | collective-permute-done | bytes 262176 | tf_op jit(solution)/shard_map/ppermute | solution.py:422
  107.5 0.8 add_bitcast_fusion
Async XLA Ops:
  0.0 29.3 %collective-permute-start.1 = (f32[32,16,128]{2,1,0:T(8,128)}, f32[32,16,128]{2,1,0:T(8,128)S(1)}, u32[]{:S(2)}, u32[]{:S(2)}) collective-permute-start(f32[32,16,128]{2,1,0:T(8,128)} %bitcast.29), channel_id=1, source_target_pairs={{6,12},{12,6},{30,36},{36,30},{54,60},{60,54},{78,84},{84,78},{102... | collective-permute-start | bytes 786440 | tf_op jit(solution)/shard_map/ppermute | solution.py:422
  15.3 15.9 %collective-permute-start = (f32[34,16,128]{2,1,0:T(8,128)S(1)}, f32[34,16,128]{2,1,0:T(8,128)S(1)}, u32[]{:S(2)}, u32[]{:S(2)}) collective-permute-start(f32[34,16,128]{2,1,0:T(8,128)S(1)} %get-tuple-element.41.own.tile), channel_id=1, source_target_pairs={{0,6},{6,0},{12,18},{18,12},{24,30},{30,24},{36,42},{42,36},{48,54... | collective-permute-start | bytes 835592 | tf_op jit(solution)/shard_map/ppermute | solution.py:422
  17.3 14.0 %collective-permute-start.2 = (f32[34,16,128]{2,1,0:T(8,128)S(1)}, f32[34,16,128]{2,1,0:T(8,128)S(1)}, u32[]{:S(2)}, u32[]{:S(2)}) collective-permute-start(f32[34,16,128]{2,1,0:T(8,128)S(1)} %get-tuple-element.41.own.tile), channel_id=1, source_target_pairs={{0,24},{6,30},{12,36},{18,42},{24,0},{30,6},{36,12},{42,18},{48,72... | collective-permute-start | bytes 835592 | tf_op jit(solution)/shard_map/ppermute | solution.py:422
  20.5 11.4 %collective-permute-start.3 = (f32[34,16,128]{2,1,0:T(8,128)S(1)}, f32[34,16,128]{2,1,0:T(8,128)S(1)}, u32[]{:S(2)}, u32[]{:S(2)}) collective-permute-start(f32[34,16,128]{2,1,0:T(8,128)S(1)} %get-tuple-element.41.own.tile), channel_id=1, source_target_pairs={{24,48},{30,54},{36,60},{42,66},{48,24},{54,30},{60,36},{66,42},{7... | collective-permute-start | bytes 835592 | tf_op jit(solution)/shard_map/ppermute | solution.py:422
  25.6 20.8 %collective-permute-start.6 = (f32[64,8,256]{2,1,0:T(8,128)S(1)}, f32[64,8,256]{2,1,0:T(8,128)S(1)}, u32[]{:S(2)}, u32[]{:S(2)}) collective-permute-start(f32[64,8,256]{2,1,0:T(8,128)S(1)} %get-tuple-element.50), channel_id=1, source_target_pairs={{0,1},{1,2},{2,3},{3,4},{4,5},{6,7},{7,8},{8,9},{9,10},{10,11},{12... | collective-permute-start | bytes 1572872 | tf_op jit(solution)/shard_map/ppermute | solution.py:422
  29.4 17.1 %collective-permute-start.7 = (f32[64,8,256]{2,1,0:T(8,128)S(1)}, f32[64,8,256]{2,1,0:T(8,128)S(1)}, u32[]{:S(2)}, u32[]{:S(2)}) collective-permute-start(f32[64,8,256]{2,1,0:T(8,128)S(1)} %get-tuple-element.51), channel_id=1, source_target_pairs={{1,0},{2,1},{3,2},{4,3},{5,4},{7,6},{8,7},{9,8},{10,9},{11,10},{13... | collective-permute-start | bytes 1572872 | tf_op jit(solution)/shard_map/ppermute | solution.py:422
  31.9 7.7 %copy-start.5 = (bf16[3,128,256]{2,1,0:T(8,128)(2,1)S(1)}, bf16[3,128,256]{2,1,0:T(8,128)(2,1)}, u32[]{:S(2)}) copy-start(bf16[3,128,256]{2,1,0:T(8,128)(2,1)} %constant.6.clone.xz) | copy-start | bytes 589828
  31.9 7.7 %copy-start.6 = (bf16[256,256]{1,0:T(8,128)(2,1)S(1)}, bf16[256,256]{1,0:T(8,128)(2,1)}, u32[]{:S(2)}) copy-start(bf16[256,256]{1,0:T(8,128)(2,1)} %constant.7.clone.y) | copy-start | bytes 393220
  32.5 13.9 %collective-permute-start.4 = (f32[32,16,128]{2,1,0:T(8,128)S(1)}, f32[32,16,128]{2,1,0:T(8,128)S(1)}, u32[]{:S(2)}, u32[]{:S(2)}) collective-permute-start(f32[32,16,128]{2,1,0:T(8,128)S(1)} %get-tuple-element.42), channel_id=1, source_target_pairs={{0,24},{6,30},{12,36},{18,42},{24,0},{30,6},{36,12},{42,18},{48,72... | collective-permute-start | bytes 786440 | tf_op jit(solution)/shard_map/ppermute | solution.py:422
  34.5 12.0 %collective-permute-start.5 = (f32[32,16,128]{2,1,0:T(8,128)S(1)}, f32[32,16,128]{2,1,0:T(8,128)S(1)}, u32[]{:S(2)}, u32[]{:S(2)}) collective-permute-start(f32[32,16,128]{2,1,0:T(8,128)S(1)} %get-tuple-element.43), channel_id=1, source_target_pairs={{24,48},{30,54},{36,60},{42,66},{48,24},{54,30},{60,36},{66,42},{7... | collective-permute-start | bytes 786440 | tf_op jit(solution)/shard_map/ppermute | solution.py:422
  39.6 3.5 %copy-start.1 = (f32[1,2,1024]{2,1,0:T(2,128)S(1)}, f32[1,2,1024]{2,1,0:T(2,128)}, u32[]{:S(2)}) copy-start(f32[1,2,1024]{2,1,0:T(2,128)} %param.20) | copy-start | bytes 24580
  42.5 0.7 copy-start.2
  43.1 0.7 copy-start.3
  43.2 0.7 copy-start.4
  43.8 2.7 %copy-start = (bf16[128,128]{1,0:T(8,128)(2,1)S(1)}, bf16[128,128]{1,0:T(8,128)(2,1)}, u32[]{:S(2)}) copy-start(bf16[128,128]{1,0:T(8,128)(2,1)} %constant.8.clone.halo) | copy-start | bytes 98308
  49.3 13.4 %collective-permute-start.8 = (f32[64,8,256]{2,1,0:T(8,128)S(1)}, f32[64,8,256]{2,1,0:T(8,128)S(1)}, u32[]{:S(2)}, u32[]{:S(2)}) collective-permute-start(f32[64,8,256]{2,1,0:T(8,128)S(1)} %get-tuple-element.63), channel_id=1, source_target_pairs={{0,1},{1,2},{2,3},{3,4},{4,5},{6,7},{7,8},{8,9},{9,10},{10,11},{12... | collective-permute-start | bytes 1572872 | tf_op jit(solution)/shard_map/ppermute | solution.py:422
  53.0 13.8 %collective-permute-start.9 = (f32[64,8,256]{2,1,0:T(8,128)S(1)}, f32[64,8,256]{2,1,0:T(8,128)S(1)}, u32[]{:S(2)}, u32[]{:S(2)}) collective-permute-start(f32[64,8,256]{2,1,0:T(8,128)S(1)} %get-tuple-element.64), channel_id=1, source_target_pairs={{1,0},{2,1},{3,2},{4,3},{5,4},{7,6},{8,7},{9,8},{10,9},{11,10},{13... | collective-permute-start | bytes 1572872 | tf_op jit(solution)/shard_map/ppermute | solution.py:422
  69.4 11.3 %collective-permute-start.12 = (f32[32,16,128]{2,1,0:T(8,128)S(1)}, f32[32,16,128]{2,1,0:T(8,128)S(1)}, u32[]{:S(2)}, u32[]{:S(2)}) collective-permute-start(f32[32,16,128]{2,1,0:T(8,128)S(1)} %get-tuple-element.70), channel_id=1, source_target_pairs={{0,24},{6,30},{12,36},{18,42},{24,0},{30,6},{36,12},{42,18},{48,72... | collective-permute-start | bytes 786440 | tf_op jit(solution)/shard_map/ppermute | solution.py:422
  71.4 9.3 %collective-permute-start.13 = (f32[32,16,128]{2,1,0:T(8,128)S(1)}, f32[32,16,128]{2,1,0:T(8,128)S(1)}, u32[]{:S(2)}, u32[]{:S(2)}) collective-permute-start(f32[32,16,128]{2,1,0:T(8,128)S(1)} %get-tuple-element.70), channel_id=1, source_target_pairs={{24,48},{30,54},{36,60},{42,66},{48,24},{54,30},{60,36},{66,42},{7... | collective-permute-start | bytes 786440 | tf_op jit(solution)/shard_map/ppermute | solution.py:422
  74.6 15.2 %collective-permute-start.10 = (f32[32,16,128]{2,1,0:T(8,128)S(1)}, f32[32,16,128]{2,1,0:T(8,128)S(1)}, u32[]{:S(2)}, u32[]{:S(2)}) collective-permute-start(f32[32,16,128]{2,1,0:T(8,128)S(1)} %get-tuple-element.66), channel_id=1, source_target_pairs={{0,24},{6,30},{12,36},{18,42},{24,0},{30,6},{36,12},{42,18},{48,72... | collective-permute-start | bytes 786440 | tf_op jit(solution)/shard_map/ppermute | solution.py:422
  76.7 13.1 %collective-permute-start.11 = (f32[32,16,128]{2,1,0:T(8,128)S(1)}, f32[32,16,128]{2,1,0:T(8,128)S(1)}, u32[]{:S(2)}, u32[]{:S(2)}) collective-permute-start(f32[32,16,128]{2,1,0:T(8,128)S(1)} %get-tuple-element.66), channel_id=1, source_target_pairs={{24,48},{30,54},{36,60},{42,66},{48,24},{54,30},{60,36},{66,42},{7... | collective-permute-start | bytes 786440 | tf_op jit(solution)/shard_map/ppermute | solution.py:422
  81.4 8.4 %collective-permute-start.14 = (f32[32,16,128]{2,1,0:T(8,128)S(1)}, f32[32,16,128]{2,1,0:T(8,128)S(1)}, u32[]{:S(2)}, u32[]{:S(2)}) collective-permute-start(f32[32,16,128]{2,1,0:T(8,128)S(1)} %get-tuple-element.71), channel_id=1, source_target_pairs={{0,6},{6,0},{12,18},{18,12},{24,30},{30,24},{36,42},{42,36},{48,54... | collective-permute-start | bytes 786440 | tf_op jit(solution)/shard_map/ppermute | solution.py:422
  87.9 19.6 %collective-permute-start.15 = (f32[32,16,128]{2,1,0:T(8,128)S(1)}, f32[32,16,128]{2,1,0:T(8,128)S(1)}, u32[]{:S(2)}, u32[]{:S(2)}) collective-permute-start(f32[32,16,128]{2,1,0:T(8,128)S(1)} %get-tuple-element.74), channel_id=1, source_target_pairs={{6,12},{12,6},{30,36},{36,30},{54,60},{60,54},{78,84},{84,78},{102... | collective-permute-start | bytes 786440 | tf_op jit(solution)/shard_map/ppermute | solution.py:422

commit v4 on v3

--- a/solution.py
+++ b/solution.py
@@ -299,20 +299,30 @@
     lax.fori_loop(0, BLOCKS, step, 0)
 
 
-def image_kernel(flags, speed2, lap_fwd, lap_adj, fwd, adj, mid_fwd, mid_adj, fwd_in, adj_in, below, above, halo,
-                 own, col, row, diag, image, both):
+def blend_kernel(speed2, lap_fwd, lap_adj, fwd, adj, mid_fwd, mid_adj, fwd_in, adj_in, inner, by_adj, by_fwd):
+    def step(b, _):
+        at = pl.ds(pl.multiple_of(b * Z * 2, Z * 2), Z * 2)
+        c = speed2[at]
+        later = mid_adj[at]
+        first = mid_fwd[at] - fwd[at]
+        second_fwd = c * lap_fwd[at] + fwd_in[at]
+        earlier = 2.0 * later - adj[at] + (c * lap_adj[at] + adj_in[at])
+        inner[at] = earlier * first + later * second_fwd
+        by_adj[at] = c * first
+        by_fwd[at] = c * later
+        return 0
+
+    lax.fori_loop(0, FLAT // (Z * 2), step, 0, unroll=2)
+
+
+def image_kernel(flags, inner, by_adj, by_fwd, below, above, halo, own, col, row, diag, image, both):
     def step(b, _):
         halo_part(b, below, above, halo, both)
         for i in range(BX):
             x = b * BX + i
             at = pl.ds(pl.multiple_of(x * Z, Z), Z)
             halo_fwd, halo_adj = halo_of(i, both)
-            c = speed2[at]
-            second_fwd = c * (lap_fwd[at] + halo_fwd) + fwd_in[at]
-            second_adj = c * (lap_adj[at] + halo_adj) + adj_in[at]
-            later = mid_adj[at]
-            earlier = 2.0 * later - adj[at] + second_adj
-            image[x] = earlier * (mid_fwd[at] - fwd[at]) + later * second_fwd
+            image[x] = inner[at] + by_adj[at] * halo_adj + by_fwd[at] * halo_fwd
         return 0
 
     lax.fori_loop(0, BLOCKS, step, 0)
@@ -479,10 +489,13 @@
     above = send(to_down, down, "slab")
     lap_fwd, lap_adj = kernel(laplace_kernel, "vvvv", (flat,) * 2, (mid_fwd, mid_adj) + inner, 2 << 30, 8, parts)
     fwd_in2, adj_in2 = kernel(inject_again_kernel, "vvvv", (flat, flat), tuple(points), 2 << 30, 12, hot)
+    inner_part, by_adj, by_fwd = kernel(
+        blend_kernel, "v" * 9, (flat,) * 3,
+        (speed2.reshape(FLAT, Y), lap_fwd, lap_adj, flat_fwd, flat_adj, mid_fwd, mid_adj, fwd_in2, adj_in2), 4 << 20)
     own, col, row, diag = kernel(
-        image_kernel, "s" + "v" * 12, (piece,) * 4,
-        (flags, speed2.reshape(FLAT, Y), lap_fwd, lap_adj, flat_fwd, flat_adj, mid_fwd, mid_adj, fwd_in2, adj_in2,
-         below.reshape(AX * 8, Y), above.reshape(AX * 8, Y)) + rim, 1 << 30, 8, [pltpu.VMEM((AX, depth, Y), F32)] + both)
+        image_kernel, "s" + "v" * 6, (piece,) * 4,
+        (flags, inner_part, by_adj, by_fwd, below.reshape(AX * 8, Y), above.reshape(AX * 8, Y)) + rim,
+        1 << 30, 8, [pltpu.VMEM((AX, depth, Y), F32)] + both)
     back_e = send(pair_e, diag)
     back_o = send(pair_o, diag)
     sum_a, sum_b = kernel(

time: 109 us -> 109 us (level)
    pallas_call x10 -> x11, Pallas kernels: 19.6 us -> 19.9 us  [kernel(): pl.pallas_call(function, out_shape=tuple(outs), in_specs=places, out_spec...]
  transfers between devices with their start and end apart: 16 -> 16, of which waited for: 4 -> 4; matrix products, arithmetic and copies ran while one was open for 0% -> 0% of each run, Pallas kernels for 13% -> 14%
where the time goes in v4:
time: 109 us; the launch traced here: 108 us
  starting transfers between devices  61.2 us (56%)
  waiting for transfers between devices  24.4 us (22%)
  Pallas kernels  19.9 us (18%)
    ppermute x16, starting transfers between devices, send(): return lax.ppermute(value, axis, pairs)  61.2 us
    ppermute x16, waiting for transfers between devices, send(): return lax.ppermute(value, axis, pairs)  24.4 us
    pallas_call x11, Pallas kernels, kernel(): pl.pallas_call(function, out_shape=tuple(outs), in_specs=places, out_spec...  19.9 us
  transfers between devices with their start and end apart: 16, of which 4 were waited for; matrix products, arithmetic and copies ran while one was open for 0% of the time, Pallas kernels for 14%

profile of v4, /device:TPU:135, one launch (start us, length us, event | category | flops | bytes accessed | tf_op | source)
XLA Modules:
  0.0 107.9 jit_solution(9624256473940083435)
XLA Ops:
  0.0 13.0 %collective-permute-start.1 = (f32[32,16,128]{2,1,0:T(8,128)}, f32[32,16,128]{2,1,0:T(8,128)S(1)}, u32[]{:S(2)}, u32[]{:S(2)}) collective-permute-start(f32[32,16,128]{2,1,0:T(8,128)} %bitcast.29), channel_id=1, source_target_pairs={{6,12},{12,6},{30,36},{36,30},{54,60},{60,54},{78,84},{84,78},{102... | collective-permute-start | bytes 786440 | tf_op jit(solution)/shard_map/ppermute | solution.py:432
  13.0 2.3 %shard_map.118 = (f32[34,16,128]{2,1,0:T(8,128)S(1)}, f32[64,16,256]{2,1,0:T(8,128)S(1)}, f32[64,16,256]{2,1,0:T(8,128)S(1)}, f32[64,8,256]{2,1,0:T(8,128)S(1)},...) custom-call(s32[1,2]{1,0:T(1,128)} %anchor_hbm.1, f32[32,16,128]{2,1,0:T(8,128)} %bitcast.30, f32[64,16,256]{2,1,0:T(8,128)} %bitcast.27, ...), custom_call_target="tpu_custom_call" | custom-call | flops 1048576 | bytes 5783592 | tf_op jit(solution)/shard_map/pallas_call | solution.py:438
  15.3 1.9 %collective-permute-start = (f32[34,16,128]{2,1,0:T(8,128)S(1)}, f32[34,16,128]{2,1,0:T(8,128)S(1)}, u32[]{:S(2)}, u32[]{:S(2)}) collective-permute-start(f32[34,16,128]{2,1,0:T(8,128)S(1)} %get-tuple-element.44.own.tile), channel_id=1, source_target_pairs={{0,6},{6,0},{12,18},{18,12},{24,30},{30,24},{36,42},{42,36},{48,54... | collective-permute-start | bytes 835592 | tf_op jit(solution)/shard_map/ppermute | solution.py:432
  17.3 3.2 %collective-permute-start.2 = (f32[34,16,128]{2,1,0:T(8,128)S(1)}, f32[34,16,128]{2,1,0:T(8,128)S(1)}, u32[]{:S(2)}, u32[]{:S(2)}) collective-permute-start(f32[34,16,128]{2,1,0:T(8,128)S(1)} %get-tuple-element.44.own.tile), channel_id=1, source_target_pairs={{0,24},{6,30},{12,36},{18,42},{24,0},{30,6},{36,12},{42,18},{48,72... | collective-permute-start | bytes 835592 | tf_op jit(solution)/shard_map/ppermute | solution.py:432
  20.5 5.1 %collective-permute-start.3 = (f32[34,16,128]{2,1,0:T(8,128)S(1)}, f32[34,16,128]{2,1,0:T(8,128)S(1)}, u32[]{:S(2)}, u32[]{:S(2)}) collective-permute-start(f32[34,16,128]{2,1,0:T(8,128)S(1)} %get-tuple-element.44.own.tile), channel_id=1, source_target_pairs={{24,48},{30,54},{36,60},{42,66},{48,24},{54,30},{60,36},{66,42},{7... | collective-permute-start | bytes 835592 | tf_op jit(solution)/shard_map/ppermute | solution.py:432
  25.6 3.7 %collective-permute-start.6 = (f32[64,8,256]{2,1,0:T(8,128)S(1)}, f32[64,8,256]{2,1,0:T(8,128)S(1)}, u32[]{:S(2)}, u32[]{:S(2)}) collective-permute-start(f32[64,8,256]{2,1,0:T(8,128)S(1)} %get-tuple-element.53), channel_id=1, source_target_pairs={{0,1},{1,2},{2,3},{3,4},{4,5},{6,7},{7,8},{8,9},{9,10},{10,11},{12... | collective-permute-start | bytes 1572872 | tf_op jit(solution)/shard_map/ppermute | solution.py:432
  29.3 0.0 collective-permute-done.1.col_b
  29.4 1.9 %collective-permute-start.7 = (f32[64,8,256]{2,1,0:T(8,128)S(1)}, f32[64,8,256]{2,1,0:T(8,128)S(1)}, u32[]{:S(2)}, u32[]{:S(2)}) collective-permute-start(f32[64,8,256]{2,1,0:T(8,128)S(1)} %get-tuple-element.54), channel_id=1, source_target_pairs={{1,0},{2,1},{3,2},{4,3},{5,4},{7,6},{8,7},{9,8},{10,9},{11,10},{13... | collective-permute-start | bytes 1572872 | tf_op jit(solution)/shard_map/ppermute | solution.py:432
  31.3 0.0 collective-permute-done.col_a
  31.3 0.0 collective-permute-done.2.row_e
  31.3 0.6 collective-permute-done.3.row_o
  31.9 0.0 copy-start.5
  31.9 0.0 copy-start.6
  31.9 0.6 shard_map.119
  32.5 1.9 %collective-permute-start.4 = (f32[32,16,128]{2,1,0:T(8,128)S(1)}, f32[32,16,128]{2,1,0:T(8,128)S(1)}, u32[]{:S(2)}, u32[]{:S(2)}) collective-permute-start(f32[32,16,128]{2,1,0:T(8,128)S(1)} %get-tuple-element.45), channel_id=1, source_target_pairs={{0,24},{6,30},{12,36},{18,42},{24,0},{30,6},{36,12},{42,18},{48,72... | collective-permute-start | bytes 786440 | tf_op jit(solution)/shard_map/ppermute | solution.py:432
  34.5 5.1 %collective-permute-start.5 = (f32[32,16,128]{2,1,0:T(8,128)S(1)}, f32[32,16,128]{2,1,0:T(8,128)S(1)}, u32[]{:S(2)}, u32[]{:S(2)}) collective-permute-start(f32[32,16,128]{2,1,0:T(8,128)S(1)} %get-tuple-element.46), channel_id=1, source_target_pairs={{24,48},{30,54},{36,60},{42,66},{48,24},{54,30},{60,36},{66,42},{7... | collective-permute-start | bytes 786440 | tf_op jit(solution)/shard_map/ppermute | solution.py:432
  39.6 0.0 copy-done.5
  39.6 0.0 copy-done.6
  39.6 0.0 copy-start.1
  39.6 2.8 %shard_map.120 = (f32[1024,256]{1,0:T(8,128)S(1)}, f32[1024,256]{1,0:T(8,128)S(1)}) custom-call(f32[1024,256]{1,0:T(8,128)S(1)} %bitcast.14, f32[1024,256]{1,0:T(8,128)S(1)} %bitcast.17, bf16[3,128,256]{2,1,0:T(8,128)(2,1)S(1)} %copy-done.5, bf16[256,256]{1,0:T(8,128)(2,1)S(1)} %copy-done.6), custom_call_target="tpu_custom_call" | custom-call | flops 2147483648 | bytes 4849664 | tf_op jit(solution)/shard_map/pallas_call | solution.py:438
  42.5 0.0 copy-start.2
  43.1 0.0 copy-start.3
  43.2 0.0 copy-start.4
  43.2 0.0 copy-done.1
  43.2 0.0 copy-done.2
  43.2 0.6 copy-done.3
  43.8 0.0 copy-done.4
  43.8 0.0 copy-start
  43.8 2.6 %shard_map.121 = (f32[1024,256]{1,0:T(8,128)S(1)}, f32[1024,256]{1,0:T(8,128)S(1)}, f32[8,128]{1,0:T(8,128)S(1)}, f32[8,1024]{1,0:T(8,128)S(1)}, bf16[128,256]{1...) custom-call(s32[1]{0:T(128)S(6)} %copy.13.shot_count, s32[1,16]{1,0:T(1,128)S(1)} %copy-done.4, f32[2,16]{1,0:T(2,128)S(1)} %bitcast.26, ...), custom_call_target="tpu_custom_call" | custom-call | flops 2147483648 | bytes 3326148 | tf_op jit(solution)/shard_map/pallas_call | solution.py:438
  46.5 0.0 collective-permute-done.6
  46.5 0.0 collective-permute-done.7
  46.5 0.0 collective-permute-done.4.diag_e
  46.5 0.0 collective-permute-done.5.diag_o
  46.5 0.0 copy-done
  46.5 2.7 %shard_map.122 = (f32[64,16,256]{2,1,0:T(8,128)S(1)}, f32[1024,256]{1,0:T(8,128)S(1)}, f32[1024,256]{1,0:T(8,128)S(1)}, f32[64,8,256]{2,1,0:T(8,128)S(1)}, f32[64,8,256]{2,1,0:T(8,128)S(1)}) custom-call(s32[8]{0:T(128)S(1)} %get-tuple-element.43.flags, f32[34,16,128]{2,1,0:T(8,128)S(1)} %get-tuple-element.44.own.tile, ...), custom_call_target="tpu_custom_call" | custom-call | flops 1073741824 | bytes 13500448 | tf_op jit(solution)/shard_map/pallas_call | solution.py:438
  49.3 3.7 %collective-permute-start.8 = (f32[64,8,256]{2,1,0:T(8,128)S(1)}, f32[64,8,256]{2,1,0:T(8,128)S(1)}, u32[]{:S(2)}, u32[]{:S(2)}) collective-permute-start(f32[64,8,256]{2,1,0:T(8,128)S(1)} %get-tuple-element.69), channel_id=1, source_target_pairs={{0,1},{1,2},{2,3},{3,4},{4,5},{6,7},{7,8},{8,9},{9,10},{10,11},{12... | collective-permute-start | bytes 1572872 | tf_op jit(solution)/shard_map/ppermute | solution.py:432
  53.0 1.9 %collective-permute-start.9 = (f32[64,8,256]{2,1,0:T(8,128)S(1)}, f32[64,8,256]{2,1,0:T(8,128)S(1)}, u32[]{:S(2)}, u32[]{:S(2)}) collective-permute-start(f32[64,8,256]{2,1,0:T(8,128)S(1)} %get-tuple-element.70), channel_id=1, source_target_pairs={{1,0},{2,1},{3,2},{4,3},{5,4},{7,6},{8,7},{9,8},{10,9},{11,10},{13... | collective-permute-start | bytes 1572872 | tf_op jit(solution)/shard_map/ppermute | solution.py:432
  54.9 1.7 %shard_map.124 = (f32[1024,256]{1,0:T(8,128)S(1)}, f32[1024,256]{1,0:T(8,128)S(1)}) custom-call(f32[8,128]{1,0:T(8,128)S(1)} %get-tuple-element.60.shots, f32[8,1024]{1,0:T(8,128)S(1)} %get-tuple-element.61.receivers, bf16[128,256]{1,0:T(8,128)(2,1)S(1)} %get-tuple-element.62.shot_ones, bf16[1024,256]{1,0:T(8,128)(2,1)S(1)} %get-tuple-element.63.receiver_ones), custom_call_target="tpu_custom_call" | custom-call | flops 2147483648 | bytes 3313664 | tf_op jit(solution)/shard_map/pallas_call | solution.py:438
  56.6 2.8 %shard_map.123 = (f32[1024,256]{1,0:T(8,128)S(1)}, f32[1024,256]{1,0:T(8,128)S(1)}) custom-call(f32[1024,256]{1,0:T(8,128)S(1)} %get-tuple-element.56.fwd.mid_fwd, f32[1024,256]{1,0:T(8,128)S(1)} %get-tuple-element.57.adj.mid_adj, bf16[3,128,256]{2,1,0:T(8,128)(2,1)S(1)} %copy-done.5, bf16[256,256]{1,0:T(8,128)(2,1)S(1)} %copy-done.6), custom_call_target="tpu_custom_call" | custom-call | flops 2147483648 | bytes 4849664 | tf_op jit(solution)/shard_map/pallas_call | solution.py:438
  59.4 0.6 shard_map.125
  60.0 2.7 %collective-permute-done.8 = f32[64,8,256]{2,1,0:T(8,128)S(1)} collective-permute-done((f32[64,8,256]{2,1,0:T(8,128)S(1)}, f32[64,8,256]{2,1,0:T(8,128)S(1)}, u32[]{:S(2)}, u32[]{:S(2)}) %collective-permute-start.8) | collective-permute-done | bytes 524320 | tf_op jit(solution)/shard_map/ppermute | solution.py:432
  62.7 4.1 %collective-permute-done.9 = f32[64,8,256]{2,1,0:T(8,128)S(1)} collective-permute-done((f32[64,8,256]{2,1,0:T(8,128)S(1)}, f32[64,8,256]{2,1,0:T(8,128)S(1)}, u32[]{:S(2)}, u32[]{:S(2)}) %collective-permute-start.9) | collective-permute-done | bytes 524320 | tf_op jit(solution)/shard_map/ppermute | solution.py:432
  66.8 2.4 %shard_map.126 = (f32[32,16,128]{2,1,0:T(8,128)S(1)}, f32[32,16,128]{2,1,0:T(8,128)S(1)}, f32[32,16,128]{2,1,0:T(8,128)S(1)}, f32[32,16,128]{2,1,0:T(8,128)S(1)}) custom-call(s32[8]{0:T(128)S(1)} %get-tuple-element.43.flags, f32[1024,256]{1,0:T(8,128)S(1)} %get-tuple-element.66.inner, f32[1024,256]{1,0:T(8,128)S(1)} %get-tuple-element.67.by_adj, ...), custom_call_target="tpu_custom_call" | custom-call | flops 1073741824 | bytes 5308448 | tf_op jit(solution)/shard_map/pallas_call | solution.py:438
  69.1 1.9 %collective-permute-start.12 = (f32[32,16,128]{2,1,0:T(8,128)S(1)}, f32[32,16,128]{2,1,0:T(8,128)S(1)}, u32[]{:S(2)}, u32[]{:S(2)}) collective-permute-start(f32[32,16,128]{2,1,0:T(8,128)S(1)} %get-tuple-element.76), channel_id=1, source_target_pairs={{0,24},{6,30},{12,36},{18,42},{24,0},{30,6},{36,12},{42,18},{48,72... | collective-permute-start | bytes 786440 | tf_op jit(solution)/shard_map/ppermute | solution.py:432
  71.1 3.3 %collective-permute-start.13 = (f32[32,16,128]{2,1,0:T(8,128)S(1)}, f32[32,16,128]{2,1,0:T(8,128)S(1)}, u32[]{:S(2)}, u32[]{:S(2)}) collective-permute-start(f32[32,16,128]{2,1,0:T(8,128)S(1)} %get-tuple-element.76), channel_id=1, source_target_pairs={{24,48},{30,54},{36,60},{42,66},{48,24},{54,30},{60,36},{66,42},{7... | collective-permute-start | bytes 786440 | tf_op jit(solution)/shard_map/ppermute | solution.py:432
  74.3 2.0 %collective-permute-start.10 = (f32[32,16,128]{2,1,0:T(8,128)S(1)}, f32[32,16,128]{2,1,0:T(8,128)S(1)}, u32[]{:S(2)}, u32[]{:S(2)}) collective-permute-start(f32[32,16,128]{2,1,0:T(8,128)S(1)} %get-tuple-element.72), channel_id=1, source_target_pairs={{0,24},{6,30},{12,36},{18,42},{24,0},{30,6},{36,12},{42,18},{48,72... | collective-permute-start | bytes 786440 | tf_op jit(solution)/shard_map/ppermute | solution.py:432
  76.4 4.0 %collective-permute-start.11 = (f32[32,16,128]{2,1,0:T(8,128)S(1)}, f32[32,16,128]{2,1,0:T(8,128)S(1)}, u32[]{:S(2)}, u32[]{:S(2)}) collective-permute-start(f32[32,16,128]{2,1,0:T(8,128)S(1)} %get-tuple-element.72), channel_id=1, source_target_pairs={{24,48},{30,54},{36,60},{42,66},{48,24},{54,30},{60,36},{66,42},{7... | collective-permute-start | bytes 786440 | tf_op jit(solution)/shard_map/ppermute | solution.py:432
  80.4 0.0 collective-permute-done.12.back_e
  80.4 0.0 collective-permute-done.13.back_o
  80.4 0.7 shard_map.127
  81.1 6.5 %collective-permute-start.14 = (f32[32,16,128]{2,1,0:T(8,128)S(1)}, f32[32,16,128]{2,1,0:T(8,128)S(1)}, u32[]{:S(2)}, u32[]{:S(2)}) collective-permute-start(f32[32,16,128]{2,1,0:T(8,128)S(1)} %get-tuple-element.77), channel_id=1, source_target_pairs={{0,6},{6,0},{12,18},{18,12},{24,30},{30,24},{36,42},{42,36},{48,54... | collective-permute-start | bytes 786440 | tf_op jit(solution)/shard_map/ppermute | solution.py:432
  87.6 1.9 %collective-permute-start.15 = (f32[32,16,128]{2,1,0:T(8,128)S(1)}, f32[32,16,128]{2,1,0:T(8,128)S(1)}, u32[]{:S(2)}, u32[]{:S(2)}) collective-permute-start(f32[32,16,128]{2,1,0:T(8,128)S(1)} %get-tuple-element.80), channel_id=1, source_target_pairs={{6,12},{12,6},{30,36},{36,30},{54,60},{60,54},{78,84},{84,78},{102... | collective-permute-start | bytes 786440 | tf_op jit(solution)/shard_map/ppermute | solution.py:432
  89.5 0.0 collective-permute-done.10.same_e
  89.5 0.0 collective-permute-done.11.same_o
  89.5 0.0 collective-permute-done.14.sum_a
  89.5 0.6 shard_map.128
  90.2 17.0 %collective-permute-done.15 = f32[32,16,128]{2,1,0:T(8,128)S(1)} collective-permute-done((f32[32,16,128]{2,1,0:T(8,128)S(1)}, f32[32,16,128]{2,1,0:T(8,128)S(1)}, u32[]{:S(2)}, u32[]{:S(2)}) %collective-permute-start.15) | collective-permute-done | bytes 262176 | tf_op jit(solution)/shard_map/ppermute | solution.py:432
  107.2 0.8 add_bitcast_fusion
Async XLA Ops:
  0.0 29.3 %collective-permute-start.1 = (f32[32,16,128]{2,1,0:T(8,128)}, f32[32,16,128]{2,1,0:T(8,128)S(1)}, u32[]{:S(2)}, u32[]{:S(2)}) collective-permute-start(f32[32,16,128]{2,1,0:T(8,128)} %bitcast.29), channel_id=1, source_target_pairs={{6,12},{12,6},{30,36},{36,30},{54,60},{60,54},{78,84},{84,78},{102... | collective-permute-start | bytes 786440 | tf_op jit(solution)/shard_map/ppermute | solution.py:432
  15.3 15.9 %collective-permute-start = (f32[34,16,128]{2,1,0:T(8,128)S(1)}, f32[34,16,128]{2,1,0:T(8,128)S(1)}, u32[]{:S(2)}, u32[]{:S(2)}) collective-permute-start(f32[34,16,128]{2,1,0:T(8,128)S(1)} %get-tuple-element.44.own.tile), channel_id=1, source_target_pairs={{0,6},{6,0},{12,18},{18,12},{24,30},{30,24},{36,42},{42,36},{48,54... | collective-permute-start | bytes 835592 | tf_op jit(solution)/shard_map/ppermute | solution.py:432
  17.3 14.0 %collective-permute-start.2 = (f32[34,16,128]{2,1,0:T(8,128)S(1)}, f32[34,16,128]{2,1,0:T(8,128)S(1)}, u32[]{:S(2)}, u32[]{:S(2)}) collective-permute-start(f32[34,16,128]{2,1,0:T(8,128)S(1)} %get-tuple-element.44.own.tile), channel_id=1, source_target_pairs={{0,24},{6,30},{12,36},{18,42},{24,0},{30,6},{36,12},{42,18},{48,72... | collective-permute-start | bytes 835592 | tf_op jit(solution)/shard_map/ppermute | solution.py:432
  20.5 11.4 %collective-permute-start.3 = (f32[34,16,128]{2,1,0:T(8,128)S(1)}, f32[34,16,128]{2,1,0:T(8,128)S(1)}, u32[]{:S(2)}, u32[]{:S(2)}) collective-permute-start(f32[34,16,128]{2,1,0:T(8,128)S(1)} %get-tuple-element.44.own.tile), channel_id=1, source_target_pairs={{24,48},{30,54},{36,60},{42,66},{48,24},{54,30},{60,36},{66,42},{7... | collective-permute-start | bytes 835592 | tf_op jit(solution)/shard_map/ppermute | solution.py:432
  25.6 20.8 %collective-permute-start.6 = (f32[64,8,256]{2,1,0:T(8,128)S(1)}, f32[64,8,256]{2,1,0:T(8,128)S(1)}, u32[]{:S(2)}, u32[]{:S(2)}) collective-permute-start(f32[64,8,256]{2,1,0:T(8,128)S(1)} %get-tuple-element.53), channel_id=1, source_target_pairs={{0,1},{1,2},{2,3},{3,4},{4,5},{6,7},{7,8},{8,9},{9,10},{10,11},{12... | collective-permute-start | bytes 1572872 | tf_op jit(solution)/shard_map/ppermute | solution.py:432
  29.4 17.1 %collective-permute-start.7 = (f32[64,8,256]{2,1,0:T(8,128)S(1)}, f32[64,8,256]{2,1,0:T(8,128)S(1)}, u32[]{:S(2)}, u32[]{:S(2)}) collective-permute-start(f32[64,8,256]{2,1,0:T(8,128)S(1)} %get-tuple-element.54), channel_id=1, source_target_pairs={{1,0},{2,1},{3,2},{4,3},{5,4},{7,6},{8,7},{9,8},{10,9},{11,10},{13... | collective-permute-start | bytes 1572872 | tf_op jit(solution)/shard_map/ppermute | solution.py:432
  31.9 7.7 %copy-start.5 = (bf16[3,128,256]{2,1,0:T(8,128)(2,1)S(1)}, bf16[3,128,256]{2,1,0:T(8,128)(2,1)}, u32[]{:S(2)}) copy-start(bf16[3,128,256]{2,1,0:T(8,128)(2,1)} %constant.6.clone.xz) | copy-start | bytes 589828
  31.9 7.7 %copy-start.6 = (bf16[256,256]{1,0:T(8,128)(2,1)S(1)}, bf16[256,256]{1,0:T(8,128)(2,1)}, u32[]{:S(2)}) copy-start(bf16[256,256]{1,0:T(8,128)(2,1)} %constant.7.clone.y) | copy-start | bytes 393220
  32.5 13.9 %collective-permute-start.4 = (f32[32,16,128]{2,1,0:T(8,128)S(1)}, f32[32,16,128]{2,1,0:T(8,128)S(1)}, u32[]{:S(2)}, u32[]{:S(2)}) collective-permute-start(f32[32,16,128]{2,1,0:T(8,128)S(1)} %get-tuple-element.45), channel_id=1, source_target_pairs={{0,24},{6,30},{12,36},{18,42},{24,0},{30,6},{36,12},{42,18},{48,72... | collective-permute-start | bytes 786440 | tf_op jit(solution)/shard_map/ppermute | solution.py:432
  34.5 12.0 %collective-permute-start.5 = (f32[32,16,128]{2,1,0:T(8,128)S(1)}, f32[32,16,128]{2,1,0:T(8,128)S(1)}, u32[]{:S(2)}, u32[]{:S(2)}) collective-permute-start(f32[32,16,128]{2,1,0:T(8,128)S(1)} %get-tuple-element.46), channel_id=1, source_target_pairs={{24,48},{30,54},{36,60},{42,66},{48,24},{54,30},{60,36},{66,42},{7... | collective-permute-start | bytes 786440 | tf_op jit(solution)/shard_map/ppermute | solution.py:432
  39.6 3.5 %copy-start.1 = (f32[1,2,1024]{2,1,0:T(2,128)S(1)}, f32[1,2,1024]{2,1,0:T(2,128)}, u32[]{:S(2)}) copy-start(f32[1,2,1024]{2,1,0:T(2,128)} %param.20) | copy-start | bytes 24580
  42.5 0.7 copy-start.2
  43.1 0.7 copy-start.3
  43.2 0.7 copy-start.4
  43.8 2.7 %copy-start = (bf16[128,128]{1,0:T(8,128)(2,1)S(1)}, bf16[128,128]{1,0:T(8,128)(2,1)}, u32[]{:S(2)}) copy-start(bf16[128,128]{1,0:T(8,128)(2,1)} %constant.8.clone.halo) | copy-start | bytes 98308
  49.3 13.4 %collective-permute-start.8 = (f32[64,8,256]{2,1,0:T(8,128)S(1)}, f32[64,8,256]{2,1,0:T(8,128)S(1)}, u32[]{:S(2)}, u32[]{:S(2)}) collective-permute-start(f32[64,8,256]{2,1,0:T(8,128)S(1)} %get-tuple-element.69), channel_id=1, source_target_pairs={{0,1},{1,2},{2,3},{3,4},{4,5},{6,7},{7,8},{8,9},{9,10},{10,11},{12... | collective-permute-start | bytes 1572872 | tf_op jit(solution)/shard_map/ppermute | solution.py:432
  53.0 13.8 %collective-permute-start.9 = (f32[64,8,256]{2,1,0:T(8,128)S(1)}, f32[64,8,256]{2,1,0:T(8,128)S(1)}, u32[]{:S(2)}, u32[]{:S(2)}) collective-permute-start(f32[64,8,256]{2,1,0:T(8,128)S(1)} %get-tuple-element.70), channel_id=1, source_target_pairs={{1,0},{2,1},{3,2},{4,3},{5,4},{7,6},{8,7},{9,8},{10,9},{11,10},{13... | collective-permute-start | bytes 1572872 | tf_op jit(solution)/shard_map/ppermute | solution.py:432
  69.1 11.3 %collective-permute-start.12 = (f32[32,16,128]{2,1,0:T(8,128)S(1)}, f32[32,16,128]{2,1,0:T(8,128)S(1)}, u32[]{:S(2)}, u32[]{:S(2)}) collective-permute-start(f32[32,16,128]{2,1,0:T(8,128)S(1)} %get-tuple-element.76), channel_id=1, source_target_pairs={{0,24},{6,30},{12,36},{18,42},{24,0},{30,6},{36,12},{42,18},{48,72... | collective-permute-start | bytes 786440 | tf_op jit(solution)/shard_map/ppermute | solution.py:432
  71.1 9.3 %collective-permute-start.13 = (f32[32,16,128]{2,1,0:T(8,128)S(1)}, f32[32,16,128]{2,1,0:T(8,128)S(1)}, u32[]{:S(2)}, u32[]{:S(2)}) collective-permute-start(f32[32,16,128]{2,1,0:T(8,128)S(1)} %get-tuple-element.76), channel_id=1, source_target_pairs={{24,48},{30,54},{36,60},{42,66},{48,24},{54,30},{60,36},{66,42},{7... | collective-permute-start | bytes 786440 | tf_op jit(solution)/shard_map/ppermute | solution.py:432
  74.3 15.2 %collective-permute-start.10 = (f32[32,16,128]{2,1,0:T(8,128)S(1)}, f32[32,16,128]{2,1,0:T(8,128)S(1)}, u32[]{:S(2)}, u32[]{:S(2)}) collective-permute-start(f32[32,16,128]{2,1,0:T(8,128)S(1)} %get-tuple-element.72), channel_id=1, source_target_pairs={{0,24},{6,30},{12,36},{18,42},{24,0},{30,6},{36,12},{42,18},{48,72... | collective-permute-start | bytes 786440 | tf_op jit(solution)/shard_map/ppermute | solution.py:432
  76.4 13.1 %collective-permute-start.11 = (f32[32,16,128]{2,1,0:T(8,128)S(1)}, f32[32,16,128]{2,1,0:T(8,128)S(1)}, u32[]{:S(2)}, u32[]{:S(2)}) collective-permute-start(f32[32,16,128]{2,1,0:T(8,128)S(1)} %get-tuple-element.72), channel_id=1, source_target_pairs={{24,48},{30,54},{36,60},{42,66},{48,24},{54,30},{60,36},{66,42},{7... | collective-permute-start | bytes 786440 | tf_op jit(solution)/shard_map/ppermute | solution.py:432
  81.1 8.4 %collective-permute-start.14 = (f32[32,16,128]{2,1,0:T(8,128)S(1)}, f32[32,16,128]{2,1,0:T(8,128)S(1)}, u32[]{:S(2)}, u32[]{:S(2)}) collective-permute-start(f32[32,16,128]{2,1,0:T(8,128)S(1)} %get-tuple-element.77), channel_id=1, source_target_pairs={{0,6},{6,0},{12,18},{18,12},{24,30},{30,24},{36,42},{42,36},{48,54... | collective-permute-start | bytes 786440 | tf_op jit(solution)/shard_map/ppermute | solution.py:432
  87.6 19.6 %collective-permute-start.15 = (f32[32,16,128]{2,1,0:T(8,128)S(1)}, f32[32,16,128]{2,1,0:T(8,128)S(1)}, u32[]{:S(2)}, u32[]{:S(2)}) collective-permute-start(f32[32,16,128]{2,1,0:T(8,128)S(1)} %get-tuple-element.80), channel_id=1, source_target_pairs={{6,12},{12,6},{30,36},{36,30},{54,60},{60,54},{78,84},{84,78},{102... | collective-permute-start | bytes 786440 | tf_op jit(solution)/shard_map/ppermute | solution.py:432

commit v5 on v4

--- a/solution.py
+++ b/solution.py
@@ -22,6 +22,7 @@
 AX = 64
 ROWS = BX * Z
 BLOCKS = AX // BX
+HALF = 128
 HOT = 512
 FLAT = AX * Z
 F32 = jnp.float32
@@ -59,17 +60,6 @@
 def along_y():
     at = np.arange(Y)
     return weight(at[:, None] - at[None, :]) + CENTRE_Y * np.eye(Y)
-
-
-def along_halo():
-    field, rest = np.divmod(np.arange(ROWS), BX * 8)
-    out_x, out_s = np.divmod(rest, 8)
-    out_z = np.where(out_s < 4, out_s, Z - 8 + out_s)
-    side, rest = np.divmod(np.arange(ROWS), BX * 8)
-    in_x, in_s = np.divmod(rest, 8)
-    in_z = np.where(side == 0, in_s % 4 - 4, Z + in_s % 4)
-    same = (out_x[:, None] == in_x[None, :]) & (field[:, None] == in_s[None, :] // 4)
-    return np.where(same, weight(out_z[:, None] - in_z[None, :]), 0.0)
 
 
 def dot(a, b):
@@ -238,23 +228,33 @@
     lax.fori_loop(0, BLOCKS // 2, step, 0)
 
 
-def halo_part(b, below, above, halo, both):
-    at = pl.ds(pl.multiple_of(b * (ROWS // 2), ROWS // 2), ROWS // 2)
-    high, middle, low = split3(jnp.concatenate([below[at], above[at]], 0))
-    both[...] = dot(halo[...], low) + dot(halo[...], middle) + dot(halo[...], high)
-
-
-def halo_of(i, both):
-    front = lax.broadcasted_iota(jnp.int32, (8, Y), 0) < 4
+def halo_weights():
+    row = lax.broadcasted_iota(jnp.int32, (8, HALF), 0)
+    low = [jnp.where(row + k <= 3, STENCIL[3 - k], 0.0) for k in range(4)]
+    high = [jnp.where(row - 4 - k >= 0, STENCIL[3 - k], 0.0) for k in range(4)]
+    return low, high
+
+
+def halo_of(x, lanes, below, above, weights):
+    at = pl.ds(pl.multiple_of(x * 8, 8), 8)
+    low, high = weights
+    under = below[at, lanes]
+    over = above[at, lanes]
     fields = []
     for field in (0, 1):
-        part = both[pl.ds(field * (ROWS // 2) + i * 8, 8)]
-        fields.append(jnp.concatenate([jnp.where(front, part, 0.0), jnp.where(front, 0.0, part)], 0))
+        parts = []
+        for rows, weight_of, shifts in (
+            (under, low, [(8 - 4 * field - k) % 8 for k in range(4)]),
+            (over, high, [(4 - 4 * field + k) % 8 for k in range(4)]),
+        ):
+            terms = [w * (pltpu.roll(rows, n, 0) if n else rows) for w, n in zip(weight_of, shifts)]
+            parts.append((terms[0] + terms[1]) + (terms[2] + terms[3]))
+        fields.append(jnp.concatenate(parts, 0))
     return fields
 
 
 def advance_kernel(flags, own, col_a, col_b, row_e, row_o, diag_e, diag_o, lap_fwd, lap_adj, fwd, adj, fwd_in, adj_in,
-                   below, above, halo, speed2, mid_fwd, mid_adj, up, down, both):
+                   below, above, speed2, mid_fwd, mid_adj, up, down):
     half = col_b.shape[0]
     wide = own.shape[2]
     with_e = flags[2] == 1
@@ -280,23 +280,24 @@
 
     lax.fori_loop(0, half // 8, assemble, 0)
 
-    def step(b, _):
-        halo_part(b, below, above, halo, both)
-        front = lax.broadcasted_iota(jnp.int32, (8, Y), 0) < 4
-        for i in range(BX):
-            x = b * BX + i
-            at = pl.ds(pl.multiple_of(x * Z, Z), Z)
-            halo_fwd, halo_adj = halo_of(i, both)
-            c = speed2[x]
-            new_fwd = fwd[at] + (c * (lap_fwd[at] + halo_fwd) + fwd_in[at])
-            new_adj = adj[at] + (c * (lap_adj[at] + halo_adj) + adj_in[at])
-            mid_fwd[at] = new_fwd
-            mid_adj[at] = new_adj
-            up[x] = jnp.where(front, pltpu.roll(new_fwd[8:], 4, 0), new_adj[8:])
-            down[x] = jnp.where(front, new_fwd[:8], pltpu.roll(new_adj[:8], 4, 0))
-        return 0
-
-    lax.fori_loop(0, BLOCKS, step, 0)
+    weights = halo_weights()
+    front = lax.broadcasted_iota(jnp.int32, (8, HALF), 0) < 4
+
+    def step(x, _):
+        at = pl.ds(pl.multiple_of(x * Z, Z), Z)
+        for h in range(Y // HALF):
+            lanes = pl.ds(h * HALF, HALF)
+            halo_fwd, halo_adj = halo_of(x, lanes, below, above, weights)
+            c = speed2[x, :, lanes]
+            new_fwd = fwd[at, lanes] + (c * (lap_fwd[at, lanes] + halo_fwd) + fwd_in[at, lanes])
+            new_adj = adj[at, lanes] + (c * (lap_adj[at, lanes] + halo_adj) + adj_in[at, lanes])
+            mid_fwd[at, lanes] = new_fwd
+            mid_adj[at, lanes] = new_adj
+            up[x, :, lanes] = jnp.where(front, pltpu.roll(new_fwd[8:], 4, 0), new_adj[8:])
+            down[x, :, lanes] = jnp.where(front, new_fwd[:8], pltpu.roll(new_adj[:8], 4, 0))
+        return 0
+
+    lax.fori_loop(0, AX, step, 0, unroll=2)
 
 
 def blend_kernel(speed2, lap_fwd, lap_adj, fwd, adj, mid_fwd, mid_adj, fwd_in, adj_in, inner, by_adj, by_fwd):
@@ -315,17 +316,18 @@
     lax.fori_loop(0, FLAT // (Z * 2), step, 0, unroll=2)
 
 
-def image_kernel(flags, inner, by_adj, by_fwd, below, above, halo, own, col, row, diag, image, both):
-    def step(b, _):
-        halo_part(b, below, above, halo, both)
-        for i in range(BX):
-            x = b * BX + i
-            at = pl.ds(pl.multiple_of(x * Z, Z), Z)
-            halo_fwd, halo_adj = halo_of(i, both)
-            image[x] = inner[at] + by_adj[at] * halo_adj + by_fwd[at] * halo_fwd
-        return 0
-
-    lax.fori_loop(0, BLOCKS, step, 0)
+def image_kernel(flags, inner, by_adj, by_fwd, below, above, own, col, row, diag, image):
+    weights = halo_weights()
+
+    def step(x, _):
+        at = pl.ds(pl.multiple_of(x * Z, Z), Z)
+        for h in range(Y // HALF):
+            lanes = pl.ds(h * HALF, HALF)
+            halo_fwd, halo_adj = halo_of(x, lanes, below, above, weights)
+            image[x, :, lanes] = inner[at, lanes] + by_adj[at, lanes] * halo_adj + by_fwd[at, lanes] * halo_fwd
+        return 0
+
+    lax.fori_loop(0, AX, step, 0, unroll=2)
     half = own.shape[0]
     wide = own.shape[2]
     row_at = flags[0] * half
@@ -449,9 +451,7 @@
     rim_shape = shape(AX, 8, Y)
     flat = shape(FLAT, Y)
     parts = [pltpu.VMEM((FLAT, Y), BF16)] * 6
-    both = [pltpu.VMEM((ROWS, Y), F32)]
     inner = (exact(along_xz()), exact(along_y()))
-    rim = (exact(along_halo()),)
 
     col_b = send(pair_b, tile)
     field = shape(AX, depth, Y)
@@ -482,9 +482,9 @@
     lap_fwd, lap_adj = kernel(
         laplace_kernel, "vvvv", (flat,) * 2, (flat_fwd, flat_adj) + inner, 2 << 30, 8, parts)
     speed2, mid_fwd, mid_adj, up, down = kernel(
-        advance_kernel, "s" + "v" * 16, (shape(AX, depth, Y), flat, flat, rim_shape, rim_shape),
+        advance_kernel, "s" + "v" * 15, (shape(AX, depth, Y), flat, flat, rim_shape, rim_shape),
         (flags, tagged, col_a, col_b, row_e, row_o, diag_e, diag_o, lap_fwd, lap_adj, flat_fwd, flat_adj, fwd_in1, adj_in1,
-         below.reshape(AX * 8, Y), above.reshape(AX * 8, Y)) + rim, 1 << 30, 8, both)
+         below.reshape(AX * 8, Y), above.reshape(AX * 8, Y)), 4 << 20)
     below = send(to_up, up, "slab")
     above = send(to_down, down, "slab")
     lap_fwd, lap_adj = kernel(laplace_kernel, "vvvv", (flat,) * 2, (mid_fwd, mid_adj) + inner, 2 << 30, 8, parts)
@@ -493,9 +493,9 @@
         blend_kernel, "v" * 9, (flat,) * 3,
         (speed2.reshape(FLAT, Y), lap_fwd, lap_adj, flat_fwd, flat_adj, mid_fwd, mid_adj, fwd_in2, adj_in2), 4 << 20)
     own, col, row, diag = kernel(
-        image_kernel, "s" + "v" * 6, (piece,) * 4,
-        (flags, inner_part, by_adj, by_fwd, below.reshape(AX * 8, Y), above.reshape(AX * 8, Y)) + rim,
-        1 << 30, 8, [pltpu.VMEM((AX, depth, Y), F32)] + both)
+        image_kernel, "s" + "v" * 5, (piece,) * 4,
+        (flags, inner_part, by_adj, by_fwd, below.reshape(AX * 8, Y), above.reshape(AX * 8, Y)),
+        4 << 20, 8, [pltpu.VMEM((AX, depth, Y), F32)])
     back_e = send(pair_e, diag)
     back_o = send(pair_o, diag)
     sum_a, sum_b = kernel(

time: 109 us -> 107 us (0.982)
  Pallas kernels: 19.9 us -> 18.5 us
    pallas_call x11, Pallas kernels: 19.9 us -> 18.5 us  [kernel(): pl.pallas_call(function, out_shape=tuple(outs), in_specs=places, out_spec...]
where the time goes in v5:
time: 107 us
  starting transfers between devices  61.2 us (57%)
  waiting for transfers between devices  24.4 us (23%)
  Pallas kernels  18.5 us (17%)
    ppermute x16, starting transfers between devices, send(): return lax.ppermute(value, axis, pairs)  61.2 us
    ppermute x16, waiting for transfers between devices, send(): return lax.ppermute(value, axis, pairs)  24.4 us
    pallas_call x11, Pallas kernels, kernel(): pl.pallas_call(function, out_shape=tuple(outs), in_specs=places, out_spec...  18.5 us
  transfers between devices with their start and end apart: 16, of which 4 were waited for; matrix products, arithmetic and copies ran while one was open for 0% of the time, Pallas kernels for 14%

profile of v5, /device:TPU:135, one launch (start us, length us, event | category | flops | bytes accessed | tf_op | source)
XLA Modules:
  0.0 106.6 jit_solution(1280064533337673951)
XLA Ops:
  0.0 13.0 %collective-permute-start.1 = (f32[32,16,128]{2,1,0:T(8,128)}, f32[32,16,128]{2,1,0:T(8,128)S(1)}, u32[]{:S(2)}, u32[]{:S(2)}) collective-permute-start(f32[32,16,128]{2,1,0:T(8,128)} %bitcast.29), channel_id=1, source_target_pairs={{6,12},{12,6},{30,36},{36,30},{54,60},{60,54},{78,84},{84,78},{102... | collective-permute-start | bytes 786440 | tf_op jit(solution)/shard_map/ppermute | solution.py:434
  13.0 2.3 %shard_map.109 = (f32[34,16,128]{2,1,0:T(8,128)S(1)}, f32[64,16,256]{2,1,0:T(8,128)S(1)}, f32[64,16,256]{2,1,0:T(8,128)S(1)}, f32[64,8,256]{2,1,0:T(8,128)S(1)},...) custom-call(s32[1,2]{1,0:T(1,128)} %anchor_hbm.1, f32[32,16,128]{2,1,0:T(8,128)} %bitcast.30, f32[64,16,256]{2,1,0:T(8,128)} %bitcast.27, ...), custom_call_target="tpu_custom_call" | custom-call | flops 1048576 | bytes 5783592 | tf_op jit(solution)/shard_map/pallas_call | solution.py:440
  15.3 1.9 %collective-permute-start = (f32[34,16,128]{2,1,0:T(8,128)S(1)}, f32[34,16,128]{2,1,0:T(8,128)S(1)}, u32[]{:S(2)}, u32[]{:S(2)}) collective-permute-start(f32[34,16,128]{2,1,0:T(8,128)S(1)} %get-tuple-element.44.own.tile), channel_id=1, source_target_pairs={{0,6},{6,0},{12,18},{18,12},{24,30},{30,24},{36,42},{42,36},{48,54... | collective-permute-start | bytes 835592 | tf_op jit(solution)/shard_map/ppermute | solution.py:434
  17.3 3.2 %collective-permute-start.2 = (f32[34,16,128]{2,1,0:T(8,128)S(1)}, f32[34,16,128]{2,1,0:T(8,128)S(1)}, u32[]{:S(2)}, u32[]{:S(2)}) collective-permute-start(f32[34,16,128]{2,1,0:T(8,128)S(1)} %get-tuple-element.44.own.tile), channel_id=1, source_target_pairs={{0,24},{6,30},{12,36},{18,42},{24,0},{30,6},{36,12},{42,18},{48,72... | collective-permute-start | bytes 835592 | tf_op jit(solution)/shard_map/ppermute | solution.py:434
  20.5 5.1 %collective-permute-start.3 = (f32[34,16,128]{2,1,0:T(8,128)S(1)}, f32[34,16,128]{2,1,0:T(8,128)S(1)}, u32[]{:S(2)}, u32[]{:S(2)}) collective-permute-start(f32[34,16,128]{2,1,0:T(8,128)S(1)} %get-tuple-element.44.own.tile), channel_id=1, source_target_pairs={{24,48},{30,54},{36,60},{42,66},{48,24},{54,30},{60,36},{66,42},{7... | collective-permute-start | bytes 835592 | tf_op jit(solution)/shard_map/ppermute | solution.py:434
  25.6 3.7 %collective-permute-start.6 = (f32[64,8,256]{2,1,0:T(8,128)S(1)}, f32[64,8,256]{2,1,0:T(8,128)S(1)}, u32[]{:S(2)}, u32[]{:S(2)}) collective-permute-start(f32[64,8,256]{2,1,0:T(8,128)S(1)} %get-tuple-element.53), channel_id=1, source_target_pairs={{0,1},{1,2},{2,3},{3,4},{4,5},{6,7},{7,8},{8,9},{9,10},{10,11},{12... | collective-permute-start | bytes 1572872 | tf_op jit(solution)/shard_map/ppermute | solution.py:434
  29.3 0.0 collective-permute-done.1.col_b
  29.4 1.9 %collective-permute-start.7 = (f32[64,8,256]{2,1,0:T(8,128)S(1)}, f32[64,8,256]{2,1,0:T(8,128)S(1)}, u32[]{:S(2)}, u32[]{:S(2)}) collective-permute-start(f32[64,8,256]{2,1,0:T(8,128)S(1)} %get-tuple-element.54), channel_id=1, source_target_pairs={{1,0},{2,1},{3,2},{4,3},{5,4},{7,6},{8,7},{9,8},{10,9},{11,10},{13... | collective-permute-start | bytes 1572872 | tf_op jit(solution)/shard_map/ppermute | solution.py:434
  31.3 0.0 collective-permute-done.col_a
  31.3 0.0 collective-permute-done.2.row_e
  31.3 0.6 collective-permute-done.3.row_o
  31.9 0.0 copy-start.4
  31.9 0.0 copy-start.5
  31.9 0.6 shard_map.110
  32.5 1.9 %collective-permute-start.4 = (f32[32,16,128]{2,1,0:T(8,128)S(1)}, f32[32,16,128]{2,1,0:T(8,128)S(1)}, u32[]{:S(2)}, u32[]{:S(2)}) collective-permute-start(f32[32,16,128]{2,1,0:T(8,128)S(1)} %get-tuple-element.45), channel_id=1, source_target_pairs={{0,24},{6,30},{12,36},{18,42},{24,0},{30,6},{36,12},{42,18},{48,72... | collective-permute-start | bytes 786440 | tf_op jit(solution)/shard_map/ppermute | solution.py:434
  34.5 5.1 %collective-permute-start.5 = (f32[32,16,128]{2,1,0:T(8,128)S(1)}, f32[32,16,128]{2,1,0:T(8,128)S(1)}, u32[]{:S(2)}, u32[]{:S(2)}) collective-permute-start(f32[32,16,128]{2,1,0:T(8,128)S(1)} %get-tuple-element.46), channel_id=1, source_target_pairs={{24,48},{30,54},{36,60},{42,66},{48,24},{54,30},{60,36},{66,42},{7... | collective-permute-start | bytes 786440 | tf_op jit(solution)/shard_map/ppermute | solution.py:434
  39.6 0.0 copy-done.4
  39.6 0.0 copy-done.5
  39.6 0.0 copy-start
  39.6 2.8 %shard_map.111 = (f32[1024,256]{1,0:T(8,128)S(1)}, f32[1024,256]{1,0:T(8,128)S(1)}) custom-call(f32[1024,256]{1,0:T(8,128)S(1)} %bitcast.14, f32[1024,256]{1,0:T(8,128)S(1)} %bitcast.17, bf16[3,128,256]{2,1,0:T(8,128)(2,1)S(1)} %copy-done.4, bf16[256,256]{1,0:T(8,128)(2,1)S(1)} %copy-done.5), custom_call_target="tpu_custom_call" | custom-call | flops 2147483648 | bytes 4849664 | tf_op jit(solution)/shard_map/pallas_call | solution.py:440
  42.5 0.0 copy-start.1
  43.1 0.0 copy-start.2
  43.2 0.0 copy-start.3
  43.2 0.0 copy-done
  43.2 0.0 copy-done.1
  43.2 0.6 copy-done.2
  43.8 0.0 copy-done.3
  43.8 2.6 %shard_map.112 = (f32[1024,256]{1,0:T(8,128)S(1)}, f32[1024,256]{1,0:T(8,128)S(1)}, f32[8,128]{1,0:T(8,128)S(1)}, f32[8,1024]{1,0:T(8,128)S(1)}, bf16[128,256]{1...) custom-call(s32[1]{0:T(128)S(6)} %copy.12.shot_count, s32[1,16]{1,0:T(1,128)S(1)} %copy-done.3, f32[2,16]{1,0:T(2,128)S(1)} %bitcast.26, ...), custom_call_target="tpu_custom_call" | custom-call | flops 2147483648 | bytes 3326148 | tf_op jit(solution)/shard_map/pallas_call | solution.py:440
  46.5 0.0 collective-permute-done.6
  46.5 0.0 collective-permute-done.7
  46.5 0.0 collective-permute-done.4.diag_e
  46.5 0.0 collective-permute-done.5.diag_o
  46.5 2.0 %shard_map.113 = (f32[64,16,256]{2,1,0:T(8,128)S(1)}, f32[1024,256]{1,0:T(8,128)S(1)}, f32[1024,256]{1,0:T(8,128)S(1)}, f32[64,8,256]{2,1,0:T(8,128)S(1)}, f32[64,8,256]{2,1,0:T(8,128)S(1)}) custom-call(s32[8]{0:T(128)S(1)} %get-tuple-element.43.flags, f32[34,16,128]{2,1,0:T(8,128)S(1)} %get-tuple-element.44.own.tile, ...), custom_call_target="tpu_custom_call" | custom-call | flops 4194304 | bytes 13434912 | tf_op jit(solution)/shard_map/pallas_call | solution.py:440
  48.5 3.7 %collective-permute-start.8 = (f32[64,8,256]{2,1,0:T(8,128)S(1)}, f32[64,8,256]{2,1,0:T(8,128)S(1)}, u32[]{:S(2)}, u32[]{:S(2)}) collective-permute-start(f32[64,8,256]{2,1,0:T(8,128)S(1)} %get-tuple-element.69), channel_id=1, source_target_pairs={{0,1},{1,2},{2,3},{3,4},{4,5},{6,7},{7,8},{8,9},{9,10},{10,11},{12... | collective-permute-start | bytes 1572872 | tf_op jit(solution)/shard_map/ppermute | solution.py:434
  52.2 1.9 %collective-permute-start.9 = (f32[64,8,256]{2,1,0:T(8,128)S(1)}, f32[64,8,256]{2,1,0:T(8,128)S(1)}, u32[]{:S(2)}, u32[]{:S(2)}) collective-permute-start(f32[64,8,256]{2,1,0:T(8,128)S(1)} %get-tuple-element.70), channel_id=1, source_target_pairs={{1,0},{2,1},{3,2},{4,3},{5,4},{7,6},{8,7},{9,8},{10,9},{11,10},{13... | collective-permute-start | bytes 1572872 | tf_op jit(solution)/shard_map/ppermute | solution.py:434
  54.2 1.7 %shard_map.115 = (f32[1024,256]{1,0:T(8,128)S(1)}, f32[1024,256]{1,0:T(8,128)S(1)}) custom-call(f32[8,128]{1,0:T(8,128)S(1)} %get-tuple-element.60.shots, f32[8,1024]{1,0:T(8,128)S(1)} %get-tuple-element.61.receivers, bf16[128,256]{1,0:T(8,128)(2,1)S(1)} %get-tuple-element.62.shot_ones, bf16[1024,256]{1,0:T(8,128)(2,1)S(1)} %get-tuple-element.63.receiver_ones), custom_call_target="tpu_custom_call" | custom-call | flops 2147483648 | bytes 3313664 | tf_op jit(solution)/shard_map/pallas_call | solution.py:440
  55.9 2.8 %shard_map.114 = (f32[1024,256]{1,0:T(8,128)S(1)}, f32[1024,256]{1,0:T(8,128)S(1)}) custom-call(f32[1024,256]{1,0:T(8,128)S(1)} %get-tuple-element.56.fwd.mid_fwd, f32[1024,256]{1,0:T(8,128)S(1)} %get-tuple-element.57.adj.mid_adj, bf16[3,128,256]{2,1,0:T(8,128)(2,1)S(1)} %copy-done.4, bf16[256,256]{1,0:T(8,128)(2,1)S(1)} %copy-done.5), custom_call_target="tpu_custom_call" | custom-call | flops 2147483648 | bytes 4849664 | tf_op jit(solution)/shard_map/pallas_call | solution.py:440
  58.7 0.6 shard_map.116
  59.3 2.7 %collective-permute-done.8 = f32[64,8,256]{2,1,0:T(8,128)S(1)} collective-permute-done((f32[64,8,256]{2,1,0:T(8,128)S(1)}, f32[64,8,256]{2,1,0:T(8,128)S(1)}, u32[]{:S(2)}, u32[]{:S(2)}) %collective-permute-start.8) | collective-permute-done | bytes 524320 | tf_op jit(solution)/shard_map/ppermute | solution.py:434
  62.0 4.1 %collective-permute-done.9 = f32[64,8,256]{2,1,0:T(8,128)S(1)} collective-permute-done((f32[64,8,256]{2,1,0:T(8,128)S(1)}, f32[64,8,256]{2,1,0:T(8,128)S(1)}, u32[]{:S(2)}, u32[]{:S(2)}) %collective-permute-start.9) | collective-permute-done | bytes 524320 | tf_op jit(solution)/shard_map/ppermute | solution.py:434
  66.0 1.7 %shard_map.117 = (f32[32,16,128]{2,1,0:T(8,128)S(1)}, f32[32,16,128]{2,1,0:T(8,128)S(1)}, f32[32,16,128]{2,1,0:T(8,128)S(1)}, f32[32,16,128]{2,1,0:T(8,128)S(1)}) custom-call(s32[8]{0:T(128)S(1)} %get-tuple-element.43.flags, f32[1024,256]{1,0:T(8,128)S(1)} %get-tuple-element.66.inner, f32[1024,256]{1,0:T(8,128)S(1)} %get-tuple-element.67.by_adj, ...), custom_call_target="tpu_custom_call" | custom-call | flops 4194304 | bytes 5242912 | tf_op jit(solution)/shard_map/pallas_call | solution.py:440
  67.8 1.9 %collective-permute-start.12 = (f32[32,16,128]{2,1,0:T(8,128)S(1)}, f32[32,16,128]{2,1,0:T(8,128)S(1)}, u32[]{:S(2)}, u32[]{:S(2)}) collective-permute-start(f32[32,16,128]{2,1,0:T(8,128)S(1)} %get-tuple-element.76), channel_id=1, source_target_pairs={{0,24},{6,30},{12,36},{18,42},{24,0},{30,6},{36,12},{42,18},{48,72... | collective-permute-start | bytes 786440 | tf_op jit(solution)/shard_map/ppermute | solution.py:434
  69.7 3.2 %collective-permute-start.13 = (f32[32,16,128]{2,1,0:T(8,128)S(1)}, f32[32,16,128]{2,1,0:T(8,128)S(1)}, u32[]{:S(2)}, u32[]{:S(2)}) collective-permute-start(f32[32,16,128]{2,1,0:T(8,128)S(1)} %get-tuple-element.76), channel_id=1, source_target_pairs={{24,48},{30,54},{36,60},{42,66},{48,24},{54,30},{60,36},{66,42},{7... | collective-permute-start | bytes 786440 | tf_op jit(solution)/shard_map/ppermute | solution.py:434
  72.9 2.0 %collective-permute-start.10 = (f32[32,16,128]{2,1,0:T(8,128)S(1)}, f32[32,16,128]{2,1,0:T(8,128)S(1)}, u32[]{:S(2)}, u32[]{:S(2)}) collective-permute-start(f32[32,16,128]{2,1,0:T(8,128)S(1)} %get-tuple-element.72), channel_id=1, source_target_pairs={{0,24},{6,30},{12,36},{18,42},{24,0},{30,6},{36,12},{42,18},{48,72... | collective-permute-start | bytes 786440 | tf_op jit(solution)/shard_map/ppermute | solution.py:434
  75.0 4.0 %collective-permute-start.11 = (f32[32,16,128]{2,1,0:T(8,128)S(1)}, f32[32,16,128]{2,1,0:T(8,128)S(1)}, u32[]{:S(2)}, u32[]{:S(2)}) collective-permute-start(f32[32,16,128]{2,1,0:T(8,128)S(1)} %get-tuple-element.72), channel_id=1, source_target_pairs={{24,48},{30,54},{36,60},{42,66},{48,24},{54,30},{60,36},{66,42},{7... | collective-permute-start | bytes 786440 | tf_op jit(solution)/shard_map/ppermute | solution.py:434
  79.0 0.0 collective-permute-done.12.back_e
  79.0 0.0 collective-permute-done.13.back_o
  79.1 0.7 shard_map.118
  79.7 6.4 %collective-permute-start.14 = (f32[32,16,128]{2,1,0:T(8,128)S(1)}, f32[32,16,128]{2,1,0:T(8,128)S(1)}, u32[]{:S(2)}, u32[]{:S(2)}) collective-permute-start(f32[32,16,128]{2,1,0:T(8,128)S(1)} %get-tuple-element.77), channel_id=1, source_target_pairs={{0,6},{6,0},{12,18},{18,12},{24,30},{30,24},{36,42},{42,36},{48,54... | collective-permute-start | bytes 786440 | tf_op jit(solution)/shard_map/ppermute | solution.py:434
  86.2 1.9 %collective-permute-start.15 = (f32[32,16,128]{2,1,0:T(8,128)S(1)}, f32[32,16,128]{2,1,0:T(8,128)S(1)}, u32[]{:S(2)}, u32[]{:S(2)}) collective-permute-start(f32[32,16,128]{2,1,0:T(8,128)S(1)} %get-tuple-element.80), channel_id=1, source_target_pairs={{6,12},{12,6},{30,36},{36,30},{54,60},{60,54},{78,84},{84,78},{102... | collective-permute-start | bytes 786440 | tf_op jit(solution)/shard_map/ppermute | solution.py:434
  88.1 0.0 collective-permute-done.10.same_e
  88.1 0.0 collective-permute-done.11.same_o
  88.1 0.0 collective-permute-done.14.sum_a
  88.1 0.6 shard_map.119
  88.8 17.0 %collective-permute-done.15 = f32[32,16,128]{2,1,0:T(8,128)S(1)} collective-permute-done((f32[32,16,128]{2,1,0:T(8,128)S(1)}, f32[32,16,128]{2,1,0:T(8,128)S(1)}, u32[]{:S(2)}, u32[]{:S(2)}) %collective-permute-start.15) | collective-permute-done | bytes 262176 | tf_op jit(solution)/shard_map/ppermute | solution.py:434
  105.8 0.8 add_bitcast_fusion
Async XLA Ops:
  0.0 29.3 %collective-permute-start.1 = (f32[32,16,128]{2,1,0:T(8,128)}, f32[32,16,128]{2,1,0:T(8,128)S(1)}, u32[]{:S(2)}, u32[]{:S(2)}) collective-permute-start(f32[32,16,128]{2,1,0:T(8,128)} %bitcast.29), channel_id=1, source_target_pairs={{6,12},{12,6},{30,36},{36,30},{54,60},{60,54},{78,84},{84,78},{102... | collective-permute-start | bytes 786440 | tf_op jit(solution)/shard_map/ppermute | solution.py:434
  15.3 15.9 %collective-permute-start = (f32[34,16,128]{2,1,0:T(8,128)S(1)}, f32[34,16,128]{2,1,0:T(8,128)S(1)}, u32[]{:S(2)}, u32[]{:S(2)}) collective-permute-start(f32[34,16,128]{2,1,0:T(8,128)S(1)} %get-tuple-element.44.own.tile), channel_id=1, source_target_pairs={{0,6},{6,0},{12,18},{18,12},{24,30},{30,24},{36,42},{42,36},{48,54... | collective-permute-start | bytes 835592 | tf_op jit(solution)/shard_map/ppermute | solution.py:434
  17.3 14.0 %collective-permute-start.2 = (f32[34,16,128]{2,1,0:T(8,128)S(1)}, f32[34,16,128]{2,1,0:T(8,128)S(1)}, u32[]{:S(2)}, u32[]{:S(2)}) collective-permute-start(f32[34,16,128]{2,1,0:T(8,128)S(1)} %get-tuple-element.44.own.tile), channel_id=1, source_target_pairs={{0,24},{6,30},{12,36},{18,42},{24,0},{30,6},{36,12},{42,18},{48,72... | collective-permute-start | bytes 835592 | tf_op jit(solution)/shard_map/ppermute | solution.py:434
  20.5 11.4 %collective-permute-start.3 = (f32[34,16,128]{2,1,0:T(8,128)S(1)}, f32[34,16,128]{2,1,0:T(8,128)S(1)}, u32[]{:S(2)}, u32[]{:S(2)}) collective-permute-start(f32[34,16,128]{2,1,0:T(8,128)S(1)} %get-tuple-element.44.own.tile), channel_id=1, source_target_pairs={{24,48},{30,54},{36,60},{42,66},{48,24},{54,30},{60,36},{66,42},{7... | collective-permute-start | bytes 835592 | tf_op jit(solution)/shard_map/ppermute | solution.py:434
  25.6 20.8 %collective-permute-start.6 = (f32[64,8,256]{2,1,0:T(8,128)S(1)}, f32[64,8,256]{2,1,0:T(8,128)S(1)}, u32[]{:S(2)}, u32[]{:S(2)}) collective-permute-start(f32[64,8,256]{2,1,0:T(8,128)S(1)} %get-tuple-element.53), channel_id=1, source_target_pairs={{0,1},{1,2},{2,3},{3,4},{4,5},{6,7},{7,8},{8,9},{9,10},{10,11},{12... | collective-permute-start | bytes 1572872 | tf_op jit(solution)/shard_map/ppermute | solution.py:434
  29.4 17.1 %collective-permute-start.7 = (f32[64,8,256]{2,1,0:T(8,128)S(1)}, f32[64,8,256]{2,1,0:T(8,128)S(1)}, u32[]{:S(2)}, u32[]{:S(2)}) collective-permute-start(f32[64,8,256]{2,1,0:T(8,128)S(1)} %get-tuple-element.54), channel_id=1, source_target_pairs={{1,0},{2,1},{3,2},{4,3},{5,4},{7,6},{8,7},{9,8},{10,9},{11,10},{13... | collective-permute-start | bytes 1572872 | tf_op jit(solution)/shard_map/ppermute | solution.py:434
  31.9 7.7 %copy-start.4 = (bf16[3,128,256]{2,1,0:T(8,128)(2,1)S(1)}, bf16[3,128,256]{2,1,0:T(8,128)(2,1)}, u32[]{:S(2)}) copy-start(bf16[3,128,256]{2,1,0:T(8,128)(2,1)} %constant.4.clone.xz) | copy-start | bytes 589828
  31.9 7.7 %copy-start.5 = (bf16[256,256]{1,0:T(8,128)(2,1)S(1)}, bf16[256,256]{1,0:T(8,128)(2,1)}, u32[]{:S(2)}) copy-start(bf16[256,256]{1,0:T(8,128)(2,1)} %constant.5.clone.y) | copy-start | bytes 393220
  32.5 13.9 %collective-permute-start.4 = (f32[32,16,128]{2,1,0:T(8,128)S(1)}, f32[32,16,128]{2,1,0:T(8,128)S(1)}, u32[]{:S(2)}, u32[]{:S(2)}) collective-permute-start(f32[32,16,128]{2,1,0:T(8,128)S(1)} %get-tuple-element.45), channel_id=1, source_target_pairs={{0,24},{6,30},{12,36},{18,42},{24,0},{30,6},{36,12},{42,18},{48,72... | collective-permute-start | bytes 786440 | tf_op jit(solution)/shard_map/ppermute | solution.py:434
  34.5 12.0 %collective-permute-start.5 = (f32[32,16,128]{2,1,0:T(8,128)S(1)}, f32[32,16,128]{2,1,0:T(8,128)S(1)}, u32[]{:S(2)}, u32[]{:S(2)}) collective-permute-start(f32[32,16,128]{2,1,0:T(8,128)S(1)} %get-tuple-element.46), channel_id=1, source_target_pairs={{24,48},{30,54},{36,60},{42,66},{48,24},{54,30},{60,36},{66,42},{7... | collective-permute-start | bytes 786440 | tf_op jit(solution)/shard_map/ppermute | solution.py:434
  39.6 3.5 %copy-start = (f32[1,2,1024]{2,1,0:T(2,128)S(1)}, f32[1,2,1024]{2,1,0:T(2,128)}, u32[]{:S(2)}) copy-start(f32[1,2,1024]{2,1,0:T(2,128)} %param.19) | copy-start | bytes 24580
  42.5 0.7 copy-start.1
  43.1 0.7 copy-start.2
  43.2 0.7 copy-start.3
  48.5 13.5 %collective-permute-start.8 = (f32[64,8,256]{2,1,0:T(8,128)S(1)}, f32[64,8,256]{2,1,0:T(8,128)S(1)}, u32[]{:S(2)}, u32[]{:S(2)}) collective-permute-start(f32[64,8,256]{2,1,0:T(8,128)S(1)} %get-tuple-element.69), channel_id=1, source_target_pairs={{0,1},{1,2},{2,3},{3,4},{4,5},{6,7},{7,8},{8,9},{9,10},{10,11},{12... | collective-permute-start | bytes 1572872 | tf_op jit(solution)/shard_map/ppermute | solution.py:434
  52.2 13.8 %collective-permute-start.9 = (f32[64,8,256]{2,1,0:T(8,128)S(1)}, f32[64,8,256]{2,1,0:T(8,128)S(1)}, u32[]{:S(2)}, u32[]{:S(2)}) collective-permute-start(f32[64,8,256]{2,1,0:T(8,128)S(1)} %get-tuple-element.70), channel_id=1, source_target_pairs={{1,0},{2,1},{3,2},{4,3},{5,4},{7,6},{8,7},{9,8},{10,9},{11,10},{13... | collective-permute-start | bytes 1572872 | tf_op jit(solution)/shard_map/ppermute | solution.py:434
  67.8 11.3 %collective-permute-start.12 = (f32[32,16,128]{2,1,0:T(8,128)S(1)}, f32[32,16,128]{2,1,0:T(8,128)S(1)}, u32[]{:S(2)}, u32[]{:S(2)}) collective-permute-start(f32[32,16,128]{2,1,0:T(8,128)S(1)} %get-tuple-element.76), channel_id=1, source_target_pairs={{0,24},{6,30},{12,36},{18,42},{24,0},{30,6},{36,12},{42,18},{48,72... | collective-permute-start | bytes 786440 | tf_op jit(solution)/shard_map/ppermute | solution.py:434
  69.7 9.3 %collective-permute-start.13 = (f32[32,16,128]{2,1,0:T(8,128)S(1)}, f32[32,16,128]{2,1,0:T(8,128)S(1)}, u32[]{:S(2)}, u32[]{:S(2)}) collective-permute-start(f32[32,16,128]{2,1,0:T(8,128)S(1)} %get-tuple-element.76), channel_id=1, source_target_pairs={{24,48},{30,54},{36,60},{42,66},{48,24},{54,30},{60,36},{66,42},{7... | collective-permute-start | bytes 786440 | tf_op jit(solution)/shard_map/ppermute | solution.py:434
  72.9 15.2 %collective-permute-start.10 = (f32[32,16,128]{2,1,0:T(8,128)S(1)}, f32[32,16,128]{2,1,0:T(8,128)S(1)}, u32[]{:S(2)}, u32[]{:S(2)}) collective-permute-start(f32[32,16,128]{2,1,0:T(8,128)S(1)} %get-tuple-element.72), channel_id=1, source_target_pairs={{0,24},{6,30},{12,36},{18,42},{24,0},{30,6},{36,12},{42,18},{48,72... | collective-permute-start | bytes 786440 | tf_op jit(solution)/shard_map/ppermute | solution.py:434
  75.0 13.1 %collective-permute-start.11 = (f32[32,16,128]{2,1,0:T(8,128)S(1)}, f32[32,16,128]{2,1,0:T(8,128)S(1)}, u32[]{:S(2)}, u32[]{:S(2)}) collective-permute-start(f32[32,16,128]{2,1,0:T(8,128)S(1)} %get-tuple-element.72), channel_id=1, source_target_pairs={{24,48},{30,54},{36,60},{42,66},{48,24},{54,30},{60,36},{66,42},{7... | collective-permute-start | bytes 786440 | tf_op jit(solution)/shard_map/ppermute | solution.py:434
  79.7 8.4 %collective-permute-start.14 = (f32[32,16,128]{2,1,0:T(8,128)S(1)}, f32[32,16,128]{2,1,0:T(8,128)S(1)}, u32[]{:S(2)}, u32[]{:S(2)}) collective-permute-start(f32[32,16,128]{2,1,0:T(8,128)S(1)} %get-tuple-element.77), channel_id=1, source_target_pairs={{0,6},{6,0},{12,18},{18,12},{24,30},{30,24},{36,42},{42,36},{48,54... | collective-permute-start | bytes 786440 | tf_op jit(solution)/shard_map/ppermute | solution.py:434
  86.2 19.6 %collective-permute-start.15 = (f32[32,16,128]{2,1,0:T(8,128)S(1)}, f32[32,16,128]{2,1,0:T(8,128)S(1)}, u32[]{:S(2)}, u32[]{:S(2)}) collective-permute-start(f32[32,16,128]{2,1,0:T(8,128)S(1)} %get-tuple-element.80), channel_id=1, source_target_pairs={{6,12},{12,6},{30,36},{36,30},{54,60},{60,54},{78,84},{84,78},{102... | collective-permute-start | bytes 786440 | tf_op jit(solution)/shard_map/ppermute | solution.py:434
